TPU v7x, 32 devices: a whole 2x2x4 slice. The times are simulated.
32 devices in a mesh: dp: 32 (over z, y, x, core).
Axes of the slice: x: 2, y: 2, z: 4, core: 2. Of those that a mesh axis runs over, the one named last changes fastest.
Arguments:
- tokens: bfloat16 [8192, 1024], P('dp'), may hold values from -6 to 6
- w_query: bfloat16 [1024, 1024], P('dp'), may hold values from -0.1875 to 0.1875
- key_weight: bfloat16 [1024, 512], P('dp'), may hold values from -0.1875 to 0.1875
- w_value: bfloat16 [1024, 512], P('dp'), may hold values from -0.1875 to 0.1875
- w_out: bfloat16 [1024, 1024], P('dp'), may hold values from -3 to 3
- w_gate: bfloat16 [1024, 4608], P('dp'), may hold values from -0.1875 to 0.1875
- w_up: bfloat16 [1024, 4608], P('dp'), may hold values from -0.1875 to 0.1875
- w_down: bfloat16 [4608, 1024], P('dp'), may hold values from -0.09375 to 0.09375
- norm_gains: bfloat16 [2176], P('dp'), may hold values from 0.099609375 to 1.8984375
- seq_lengths: int32 [4, 4], replicated, may hold values from 1 to 1024, 2048 in all within a row
- slot_order: int32 [4, 16], replicated, may hold values from 0 to 15, each once within a row
- out_grad: bfloat16 [8192, 1024], P('dp'), may hold values from -6 to 6
Outputs:
- result: bfloat16 [8192, 1024], P('dp')
- grad_tokens: float32 [8192, 1024], P('dp')
- grad_w_query: float32 [1024, 1024], P('dp')
- grad_w_key: float32 [1024, 512], P('dp')
- grad_w_value: float32 [1024, 512], P('dp')
- grad_w_out: float32 [1024, 1024], P('dp')
- grad_w_gate: float32 [1024, 4608], P('dp')
- grad_w_up: float32 [1024, 4608], P('dp')
- grad_w_down: float32 [4608, 1024], P('dp')
- grad_norm_gains: float32 [2176], P('dp')
Inputs may be any that keep to these rules, and one draw needn't show every extreme that they name: Each row of seq_lengths sums to 2048, and its largest entry is 1024. Each row of slot_order is a permutation of the group's 16 slots.
All inputs are finite; a program needn't handle non-finite values.
Results may differ from a plain program's by a relative error of at most 0.014.
Values may be sent and summed in bfloat16 or wider, within the bound.
A program may use at most 192 MiB of HBM per device.

v0:
```python
import math

import jax
import jax.numpy as jnp
from jax import lax
from jax.sharding import PartitionSpec as P

D = 1024
QUERY_HEADS = 16
KEY_VALUE_HEADS = 8
HEAD_SIZE = 64
SLOT = 128
GROUP_BITS = 3
DQ = 1024
KEY_VALUE_DIMS = 512
GROUP = 8


EPSILON = 1e-05
ROPE_THETA = 1000000.0
MASKED = -1e30
TRANSPOSED = (((0,), (0,)), ((), ()))
AGAINST = (((1,), (1,)), ((), ()))


def for_sending(value):

    def short(part):
        return part.astype(jnp.bfloat16) if part.dtype == jnp.float32 else part

    return jax.tree.map(short, value)


def swapped(block, axis, stride):
    count = lax.axis_size(axis)
    route = []
    for low in range(count):
        high = low | 1 << stride
        if high != low and high < count:
            route += [(low, high), (high, low)]
    return lax.ppermute(block, axis, route)


def norm_rows(value_rows, gain_vec):
    return (
        value_rows
        * lax.rsqrt(jnp.mean(value_rows * value_rows, axis=-1, keepdims=True) + EPSILON)
        * gain_vec
    )


def rotate(value_rows, angles):
    half_width = value_rows.shape[-1] // 2
    cosine = jnp.cos(angles)[:, None, :]
    sine_part = jnp.sin(angles)[:, None, :]
    front_half = value_rows[..., :half_width]
    back_half = value_rows[..., half_width:]
    return jnp.concatenate(
        [front_half * cosine - back_half * sine_part, back_half * cosine + front_half * sine_part],
        axis=-1,
    )


def rotary_angles(position, head_width):
    frequency = jnp.exp(
        jnp.arange(head_width // 2, dtype=jnp.float32) * (-2.0 * math.log(ROPE_THETA) / head_width)
    )
    return position.astype(jnp.float32)[:, None] * frequency[None, :]


def token_info(order_row, length_row, slot_ids, slot_len):
    offsets = jnp.arange(slot_len, dtype=jnp.int32)
    group_positions = (order_row[slot_ids][:, None] * slot_len + offsets[None, :]).reshape(-1)
    seq_ends = jnp.cumsum(length_row, dtype=jnp.int32)
    starts = seq_ends - length_row
    inside = (group_positions[:, None] >= starts[None, :]) & (
        group_positions[:, None] < seq_ends[None, :]
    )
    labels = jnp.arange(length_row.shape[0], dtype=jnp.int32)
    sequence_ids = jnp.sum(jnp.where(inside, labels[None, :], 0), axis=-1, dtype=jnp.int32)
    position = group_positions - jnp.sum(
        jnp.where(inside, starts[None, :], 0), axis=-1, dtype=jnp.int32
    )
    return (group_positions, sequence_ids, position)


def head_piece(raw_heads, gain_vec, angles):
    return rotate(norm_rows(raw_heads, gain_vec), angles)


def left_product(left_side, right_side):
    return lax.dot_general(left_side, right_side, TRANSPOSED, preferred_element_type=jnp.float32)


def right_product(left_side, right_side):
    return lax.dot_general(left_side, right_side, AGAINST, preferred_element_type=jnp.float32)


def gather_weights(shards):
    return jax.tree.map(
        lambda part, own: part.astype(own.dtype),
        lax.all_gather(for_sending(shards), "dp", axis=0, tiled=True),
        shards,
    )


def join_sides(block_data, partner, device, bit_index):
    lower_side = device >> bit_index & 1 == 0
    return jnp.where(
        lower_side,
        jnp.concatenate([block_data, partner], axis=0),
        jnp.concatenate([partner, block_data], axis=0),
    )


def group_gather(block_data, device):
    for bit_index in range(GROUP_BITS):
        partner = swapped(block_data, "dp", bit_index)
        block_data = join_sides(block_data, partner, device, bit_index)
    return block_data


def deal_collect(block_data, device):
    for bit_index in range(GROUP_BITS):
        partner = swapped(block_data, "dp", bit_index)
        block_data = join_sides(block_data, partner, device, bit_index)
    return block_data


def return_collect(block_data, device):
    for bit_index in range(GROUP_BITS):
        partner = swapped(block_data.astype(jnp.bfloat16), "dp", bit_index).astype(block_data.dtype)
        block_data = join_sides(block_data, partner, device, bit_index)
    return block_data


def pick_slots(group_rows, slot_index, count_rows):
    width = group_rows.shape[-1]
    slot_rows = group_rows.reshape(-1, SLOT, width)
    return jnp.take(slot_rows, slot_index, axis=0).reshape(count_rows, width)


def group_reduce(block_data, device):
    for bit_index in reversed(range(GROUP_BITS)):
        half_rows = block_data.shape[0] // 2
        lower_side = device >> bit_index & 1 == 0
        keep_half = jnp.where(lower_side, block_data[:half_rows], block_data[half_rows:])
        send_half = jnp.where(lower_side, block_data[half_rows:], block_data[:half_rows])
        block_data = keep_half + swapped(send_half.astype(jnp.bfloat16), "dp", bit_index).astype(
            send_half.dtype
        )
    return block_data


def split_keys(grouped_keys, grouped_values, pos_keys, seq_keys):
    group_rows = grouped_keys.shape[0]
    block_length = min(512, group_rows)
    count_of_blocks = group_rows // block_length
    return (
        grouped_keys.reshape(count_of_blocks, block_length, KEY_VALUE_HEADS, HEAD_SIZE),
        grouped_values.reshape(count_of_blocks, block_length, KEY_VALUE_HEADS, HEAD_SIZE),
        pos_keys.reshape(count_of_blocks, block_length),
        seq_keys.reshape(count_of_blocks, block_length),
    )


def block_scores(heads_query, block_item, pos_own, seq_own):
    key_block, value_block, pos_block, seq_block = block_item
    scores = jnp.einsum(
        "qgrd,kgd->qgrk", heads_query, key_block, preferred_element_type=jnp.float32
    ) * (1.0 / math.sqrt(HEAD_SIZE))
    allowed = (seq_own[:, None] == seq_block[None, :]) & (pos_block[None, :] <= pos_own[:, None])
    return (scores, allowed[:, None, None, :])


def softmax_stats(heads_query, key_blocks, pos_own, seq_own):
    stat_shape = heads_query.shape[:3]

    def scan_step(carry_in, block_item):
        row_top, row_total = carry_in
        scores, allowed = block_scores(heads_query, block_item, pos_own, seq_own)
        scores = jnp.where(allowed, scores, MASKED)
        new_top = jnp.maximum(row_top, jnp.max(scores, axis=-1))
        fresh = jnp.sum(jnp.where(allowed, jnp.exp(scores - new_top[..., None]), 0.0), axis=-1)
        return ((new_top, row_total * jnp.exp(row_top - new_top) + fresh), None)

    start_state = (jnp.full(stat_shape, MASKED, jnp.float32), jnp.zeros(stat_shape, jnp.float32))
    (row_top, row_total), unused = lax.scan(scan_step, start_state, key_blocks)
    return row_top + jnp.log(row_total)


def attend(heads_query, key_blocks, pos_own, seq_own, log_total):

    def scan_step(accum_out, block_item):
        scores, allowed = block_scores(heads_query, block_item, pos_own, seq_own)
        prob_low = jnp.where(allowed, jnp.exp(scores - log_total[..., None]), 0.0).astype(
            jnp.bfloat16
        )
        return (
            accum_out
            + jnp.einsum(
                "qgrk,kgd->qgrd", prob_low, block_item[1], preferred_element_type=jnp.float32
            ),
            None,
        )

    accum_out, unused = lax.scan(scan_step, jnp.zeros(heads_query.shape, jnp.float32), key_blocks)
    return accum_out


def attend_back(heads_query, key_blocks, pos_own, seq_own, log_total, grad_mixed, row_delta):
    score_scale = 1.0 / math.sqrt(HEAD_SIZE)

    def scan_step(accum_query, block_item):
        key_block, value_block = (block_item[0], block_item[1])
        block_length = key_block.shape[0]
        scores, allowed = block_scores(heads_query, block_item, pos_own, seq_own)
        prob_rows = jnp.where(allowed, jnp.exp(scores - log_total[..., None]), 0.0)
        grad_probs = jnp.einsum(
            "qgrd,kgd->qgrk", grad_mixed, value_block, preferred_element_type=jnp.float32
        )
        grad_scores = (prob_rows * (grad_probs - row_delta[..., None])).astype(jnp.bfloat16)
        grad_value = jnp.einsum(
            "qgrk,qgrd->kgd",
            prob_rows.astype(jnp.bfloat16),
            grad_mixed,
            preferred_element_type=jnp.float32,
        )
        grad_key = (
            jnp.einsum(
                "qgrk,qgrd->kgd", grad_scores, heads_query, preferred_element_type=jnp.float32
            )
            * score_scale
        )
        accum_query = (
            accum_query
            + jnp.einsum(
                "qgrk,kgd->qgrd", grad_scores, key_block, preferred_element_type=jnp.float32
            )
            * score_scale
        )
        return (
            accum_query,
            jnp.concatenate(
                [grad_key.reshape(block_length, -1), grad_value.reshape(block_length, -1)], axis=1
            ),
        )

    accum_query, key_value_grads = lax.scan(
        scan_step, jnp.zeros(heads_query.shape, jnp.float32), key_blocks
    )
    return (accum_query, key_value_grads.reshape(-1, key_value_grads.shape[-1]))


def forward_pass(tokens, full_weights, context):
    w_query, key_weight, w_value, w_out, w_gate, w_up, w_down, norm_gains = full_weights
    angles, pos_own, seq_own, pos_keys, seq_keys, device = context
    gain_all = norm_gains.astype(jnp.float32)
    count_rows = tokens.shape[0]
    token_f32 = tokens.astype(jnp.float32)
    normalized_rows = norm_rows(token_f32, gain_all[:D]).astype(jnp.bfloat16)
    query_raw = jnp.dot(normalized_rows, w_query, preferred_element_type=jnp.float32).reshape(
        count_rows, QUERY_HEADS, HEAD_SIZE
    )
    unrotated_key = jnp.dot(
        normalized_rows, key_weight, preferred_element_type=jnp.float32
    ).reshape(count_rows, KEY_VALUE_HEADS, HEAD_SIZE)
    value_low = jnp.dot(normalized_rows, w_value, preferred_element_type=jnp.float32).astype(
        jnp.bfloat16
    )
    reduced_query = head_piece(query_raw, gain_all[2 * D : 2 * D + HEAD_SIZE], angles).astype(
        jnp.bfloat16
    )
    key_low = head_piece(unrotated_key, gain_all[2 * D + HEAD_SIZE :], angles).astype(jnp.bfloat16)
    paired_parts = group_gather(
        jnp.concatenate([key_low.reshape(count_rows, KEY_VALUE_DIMS), value_low], axis=1), device
    )
    grouped_keys = paired_parts[:, :KEY_VALUE_DIMS].reshape(-1, KEY_VALUE_HEADS, HEAD_SIZE)
    grouped_values = paired_parts[:, KEY_VALUE_DIMS:].reshape(-1, KEY_VALUE_HEADS, HEAD_SIZE)
    key_blocks = split_keys(grouped_keys, grouped_values, pos_keys, seq_keys)
    heads_query = reduced_query.reshape(
        count_rows, KEY_VALUE_HEADS, QUERY_HEADS // KEY_VALUE_HEADS, HEAD_SIZE
    )
    log_total = softmax_stats(heads_query, key_blocks, pos_own, seq_own)
    mixed_f32 = attend(heads_query, key_blocks, pos_own, seq_own, log_total)
    mixed_low = mixed_f32.reshape(count_rows, DQ).astype(jnp.bfloat16)
    residual_mid = token_f32 + jnp.dot(mixed_low, w_out, preferred_element_type=jnp.float32)
    normed_ffn = norm_rows(residual_mid, gain_all[D : 2 * D]).astype(jnp.bfloat16)
    gate_pre = jnp.dot(normed_ffn, w_gate, preferred_element_type=jnp.float32)
    up_pre = jnp.dot(normed_ffn, w_up, preferred_element_type=jnp.float32)
    act_low = (jax.nn.silu(gate_pre) * up_pre).astype(jnp.bfloat16)
    result = residual_mid + jnp.dot(act_low, w_down, preferred_element_type=jnp.float32)
    return (
        token_f32,
        normalized_rows,
        query_raw,
        unrotated_key,
        heads_query,
        key_blocks,
        log_total,
        mixed_f32,
        mixed_low,
        residual_mid,
        normed_ffn,
        gate_pre,
        up_pre,
        act_low,
        result,
    )


def body(
    tokens,
    w_query,
    key_weight,
    w_value,
    w_out,
    w_gate,
    w_up,
    w_down,
    norm_gains,
    seq_lengths,
    slot_order,
    out_grad,
):
    shards = (w_query, key_weight, w_value, w_out, w_gate, w_up, w_down, norm_gains)
    device = lax.axis_index("dp")
    count_rows = tokens.shape[0]
    per_device = count_rows // SLOT
    group_id = device // GROUP
    member = device % GROUP
    order_row = lax.dynamic_index_in_dim(slot_order, group_id, 0, keepdims=False)
    length_row = lax.dynamic_index_in_dim(seq_lengths, group_id, 0, keepdims=False)
    slot_count = order_row.shape[0]
    own_slots = member * per_device + jnp.arange(per_device, dtype=jnp.int32)
    pos_own, seq_own, position_own = token_info(order_row, length_row, own_slots, SLOT)
    key_info = token_info(order_row, length_row, jnp.arange(slot_count, dtype=jnp.int32), SLOT)
    angles = rotary_angles(position_own, HEAD_SIZE)
    context = (angles, pos_own, seq_own, key_info[0], key_info[1], device)
    group_inputs = deal_collect(tokens, device)
    dealt_tokens = pick_slots(group_inputs, order_row[own_slots], count_rows)
    full_weights = gather_weights(shards)
    first_pass = forward_pass(dealt_tokens, full_weights, context)
    result = first_pass[-1]
    tokens_again, shards_again, result = lax.optimization_barrier((dealt_tokens, shards, result))
    weights_now = gather_weights(shards_again)
    saved_state = forward_pass(tokens_again, weights_now, context)
    (
        token_f32,
        normalized_rows,
        query_raw,
        unrotated_key,
        heads_query,
        key_blocks,
        log_total,
        mixed_f32,
        mixed_low,
        residual_mid,
        normed_ffn,
        gate_pre,
        up_pre,
        act_low,
        unused_result,
    ) = saved_state
    w_query, key_weight, w_value, w_out, w_gate, w_up, w_down, norm_gains = weights_now
    gain_all = norm_gains.astype(jnp.float32)
    gain_attn = gain_all[:D]
    gain_ffn = gain_all[D : 2 * D]
    gain_query = gain_all[2 * D : 2 * D + HEAD_SIZE]
    gain_key = gain_all[2 * D + HEAD_SIZE :]
    grad_w_down = left_product(act_low, out_grad)
    grad_act = right_product(out_grad, w_down)
    silu_pull = jax.vjp(lambda gate_in, up_in: jax.nn.silu(gate_in) * up_in, gate_pre, up_pre)[1]
    grad_gate, grad_up = silu_pull(grad_act)
    grad_gate = grad_gate.astype(jnp.bfloat16)
    grad_up = grad_up.astype(jnp.bfloat16)
    grad_w_gate = left_product(normed_ffn, grad_gate)
    grad_w_up = left_product(normed_ffn, grad_up)
    grad_normed_ffn = right_product(grad_gate, w_gate) + right_product(grad_up, w_up)
    ffn_pull = jax.vjp(norm_rows, residual_mid, gain_ffn)[1]
    grad_mid_part, grad_gain_ffn = ffn_pull(grad_normed_ffn)
    grad_mid = out_grad.astype(jnp.float32) + grad_mid_part
    grad_mid_low = grad_mid.astype(jnp.bfloat16)
    grad_w_out = left_product(mixed_low, grad_mid_low)
    grad_mixed = right_product(grad_mid_low, w_out).astype(jnp.bfloat16).reshape(heads_query.shape)
    row_delta = jnp.sum(grad_mixed.astype(jnp.float32) * mixed_f32, axis=-1)
    grad_query_rot, key_value_grads = attend_back(
        heads_query, key_blocks, pos_own, seq_own, log_total, grad_mixed, row_delta
    )
    local_gradients = group_reduce(key_value_grads, device)
    rotated_key_gradient = local_gradients[:, :KEY_VALUE_DIMS].reshape(
        count_rows, KEY_VALUE_HEADS, HEAD_SIZE
    )
    grad_values = local_gradients[:, KEY_VALUE_DIMS:].astype(jnp.bfloat16)
    query_pull = jax.vjp(
        lambda raw_heads, gain_vec: head_piece(raw_heads, gain_vec, angles), query_raw, gain_query
    )[1]
    grad_query_raw, grad_gain_query = query_pull(
        grad_query_rot.reshape(count_rows, QUERY_HEADS, HEAD_SIZE)
    )
    key_pull = jax.vjp(
        lambda raw_heads, gain_vec: head_piece(raw_heads, gain_vec, angles), unrotated_key, gain_key
    )[1]
    grad_key_raw, grad_gain_key = key_pull(rotated_key_gradient)
    grad_query_raw = grad_query_raw.reshape(count_rows, DQ).astype(jnp.bfloat16)
    grad_key_raw = grad_key_raw.reshape(count_rows, KEY_VALUE_DIMS).astype(jnp.bfloat16)
    grad_w_query = left_product(normalized_rows, grad_query_raw)
    grad_w_key = left_product(normalized_rows, grad_key_raw)
    grad_w_value = left_product(normalized_rows, grad_values)
    grad_normed = (
        right_product(grad_query_raw, w_query)
        + right_product(grad_key_raw, key_weight)
        + right_product(grad_values, w_value)
    )
    attn_pull = jax.vjp(norm_rows, token_f32, gain_attn)[1]
    grad_token_part, grad_gain_attn = attn_pull(grad_normed)
    dealt_grad_tokens = grad_mid + grad_token_part
    grad_norm_gains = jnp.concatenate(
        [grad_gain_attn, grad_gain_ffn, grad_gain_query, grad_gain_key], axis=0
    )
    owned = (
        lax.psum_scatter(grad_w_query, "dp", scatter_dimension=0, tiled=True),
        lax.psum_scatter(grad_w_key, "dp", scatter_dimension=0, tiled=True),
        lax.psum_scatter(grad_w_value, "dp", scatter_dimension=0, tiled=True),
        lax.psum_scatter(grad_w_out, "dp", scatter_dimension=0, tiled=True),
        lax.psum_scatter(grad_w_gate, "dp", scatter_dimension=0, tiled=True),
        lax.psum_scatter(grad_w_up, "dp", scatter_dimension=0, tiled=True),
        lax.psum_scatter(grad_w_down, "dp", scatter_dimension=0, tiled=True),
        lax.psum_scatter(grad_norm_gains, "dp", scatter_dimension=0, tiled=True),
    )
    result_rounded = result.astype(jnp.bfloat16).astype(jnp.float32)
    group_outputs = return_collect(
        jnp.concatenate([result_rounded, dealt_grad_tokens], axis=1), device
    )
    slot_labels = jnp.arange(slot_count, dtype=jnp.int32)
    source_slots = jnp.sum(
        jnp.where(order_row[None, :] == own_slots[:, None], slot_labels[None, :], 0),
        axis=-1,
        dtype=jnp.int32,
    )
    back_rows = pick_slots(group_outputs, source_slots, count_rows)
    result_out = back_rows[:, :D].astype(jnp.bfloat16)
    grad_tokens = back_rows[:, D:]
    return (
        result_out,
        grad_tokens,
        owned[0],
        owned[1],
        owned[2],
        owned[3],
        owned[4],
        owned[5],
        owned[6],
        owned[7],
    )


def solution(mesh):
    return jax.shard_map(
        body,
        mesh=mesh,
        in_specs=(
            P("dp", None),
            P("dp", None),
            P("dp", None),
            P("dp", None),
            P("dp", None),
            P("dp", None),
            P("dp", None),
            P("dp", None),
            P("dp"),
            P(),
            P(),
            P("dp", None),
        ),
        out_specs=(
            P("dp", None),
            P("dp", None),
            P("dp", None),
            P("dp", None),
            P("dp", None),
            P("dp", None),
            P("dp", None),
            P("dp", None),
            P("dp", None),
            P("dp"),
        ),
        check_vma=False,
    )
```

profile of v0, /device:TPU:0, one launch (start us, length us, event | category | flops | bytes accessed | tf_op | source)
XLA Modules:
  0.0 2372.8 jit_solution(1234167851982325617)
XLA Ops:
  20.4 57.2 %all-reduce.4 = bf16[2176]{0:T(1024)(128)(2,1)S(1)} all-reduce(bf16[2176]{0:T(1024)(128)(2,1)S(1)} %dynamic-update-slice), channel_id=1, replica_groups=mesh['dp'=32] {'dp'}, use_global_device_ids=true, to_apply=%add.4 | all-reduce | flops 2176 | bytes 8704
  85.3 43.8 %collective-permute-done.2 = bf16[1024,1024]{1,0:T(8,128)(2,1)} collective-permute-done((bf16[1024,1024]{1,0:T(8,128)(2,1)S(1)}, bf16[1024,1024]{1,0:T(8,128)(2,1)}, u32[]{:S(2)}, u32[]{:S(2)}) %collective-permute-start.2) | collective-permute-done | bytes 2097184 | tf_op jit(solution)/shard_map/ppermute | solution.py:41
  144.8 24.6 %collective-permute-done.4 = bf16[512,1024]{1,0:T(8,128)(2,1)} collective-permute-done((bf16[512,1024]{1,0:T(8,128)(2,1)S(1)}, bf16[512,1024]{1,0:T(8,128)(2,1)}, u32[]{:S(2)}, u32[]{:S(2)}) %collective-permute-start.4) | collective-permute-done | bytes 1048608 | tf_op jit(solution)/shard_map/ppermute | solution.py:41
  190.0 32.0 %collective-permute-done.5 = bf16[1024,1024]{1,0:T(8,128)(2,1)} collective-permute-done((bf16[1024,1024]{1,0:T(8,128)(2,1)}, bf16[1024,1024]{1,0:T(8,128)(2,1)}, u32[]{:S(2)}, u32[]{:S(2)}) %collective-permute-start.5) | collective-permute-done | bytes 2097184 | tf_op jit(solution)/shard_map/ppermute | solution.py:41
  251.9 42.8 %while.61 = (s32[]{:T(128)}, f32[256,8,2]{0,2,1:T(2,128)S(1)}, f32[256,8,2]{0,2,1:T(2,128)S(1)}, s32[256]{0:T(256)S(1)}, s32[4,512]{1,0:T(4,128)S(1)}, /*index=5...) while((s32[]{:T(128)}, f32[256,8,2]{0,2,1:T(2,128)S(1)}, ...), condition=%wide.region_11.12_spmd.clone, body=%wide.region_8.11_spmd.clone.sunk | while | flops 285626624 | bytes 18448004 | solution.py:188
  334.9 75.1 %all-gather.25.cloned.1.call-done = bf16[1024,4608]{1,0:T(8,128)(2,1)} async-done(((bf16[32,4608]{1,0:T(8,128)(2,1)}), bf16[1024,4608]{1,0:T(8,128)(2,1)}) %all-gather.25.cloned.1.call-update) | async-done | bytes 9437200 | tf_op jit(solution)/shard_map/all_gather | solution.py:102
  410.0 83.6 %all-gather.27.cloned.1.call-done = bf16[4608,1024]{1,0:T(8,128)(2,1)} async-done(((bf16[144,1024]{1,0:T(8,128)(2,1)}), bf16[4608,1024]{1,0:T(8,128)(2,1)}) %all-gather.27.cloned.1.call-update) | async-done | bytes 9437200 | tf_op jit(solution)/shard_map/all_gather | solution.py:102
  511.2 39.3 %all-reduce.5 = bf16[2176]{0:T(1024)(128)(2,1)S(1)} all-reduce(bf16[2176]{0:T(1024)(128)(2,1)S(1)} %dynamic-update-slice.1), channel_id=1, replica_groups=mesh['dp'=32] {'dp'}, use_global_device_ids=true, to_apply=%add.5 | all-reduce | flops 2176 | bytes 8704
  563.0 52.6 %all-gather.33.cloned.1.call-done = bf16[1024,512]{1,0:T(8,128)(2,1)} async-done(((bf16[32,512]{1,0:T(8,128)(2,1)}), bf16[1024,512]{1,0:T(8,128)(2,1)}) %all-gather.33.cloned.1.call-update) | async-done | bytes 1048592 | tf_op jit(solution)/shard_map/all_gather | solution.py:102
  621.1 26.4 %collective-permute-done.7 = bf16[512,1024]{1,0:T(8,128)(2,1)S(1)} collective-permute-done((bf16[512,1024]{1,0:T(8,128)(2,1)S(1)}, bf16[512,1024]{1,0:T(8,128)(2,1)S(1)}, u32[]{:S(2)}, u32[]{:S(2)}) %collective-permute-start.7) | collective-permute-done | bytes 1048608 | tf_op jit(solution)/shard_map/ppermute | solution.py:41
  650.2 26.3 %all-gather.35.cloned.1.call-done = bf16[1024,1024]{1,0:T(8,128)(2,1)} async-done(((bf16[32,1024]{1,0:T(8,128)(2,1)}), bf16[1024,1024]{1,0:T(8,128)(2,1)}) %all-gather.35.cloned.1.call-update) | async-done | bytes 2097168 | tf_op jit(solution)/shard_map/all_gather | solution.py:102
  724.8 42.4 %while.63 = (s32[]{:T(128)}, f32[256,8,2]{0,2,1:T(2,128)S(1)}, f32[256,8,2]{0,2,1:T(2,128)S(1)}, s32[256]{0:T(256)S(1)}, s32[4,512]{1,0:T(4,128)S(1)}, /*index=5...) while((s32[]{:T(128)}, f32[256,8,2]{0,2,1:T(2,128)S(1)}, ...), condition=%wide.region_21.22_spmd.clone, body=%wide.region_18.21_spmd.clone.sunk | while | flops 285626624 | bytes 18448004 | solution.py:188
  787.4 30.9 %all-gather.39.cloned.1.call-done = bf16[1024,4608]{1,0:T(8,128)(2,1)} async-done(((bf16[32,4608]{1,0:T(8,128)(2,1)}), bf16[1024,4608]{1,0:T(8,128)(2,1)}) %all-gather.39.cloned.1.call-update) | async-done | bytes 9437200 | tf_op jit(solution)/shard_map/all_gather | solution.py:102
  826.3 75.6 %all-gather.41.cloned.1.call-done = bf16[1024,4608]{1,0:T(8,128)(2,1)} async-done(((bf16[32,4608]{1,0:T(8,128)(2,1)}), bf16[1024,4608]{1,0:T(8,128)(2,1)}) %all-gather.41.cloned.1.call-update) | async-done | bytes 9437200 | tf_op jit(solution)/shard_map/all_gather | solution.py:102
  910.0 75.4 %all-gather.29.cloned.1.call-done = bf16[4608,1024]{1,0:T(8,128)(2,1)} async-done(((bf16[144,1024]{1,0:T(8,128)(2,1)}), bf16[4608,1024]{1,0:T(8,128)(2,1)}) %all-gather.29.cloned.1.call-update) | async-done | bytes 9437200 | tf_op jit(solution)/shard_map/all_gather | solution.py:102
  1009.7 85.5 %while.65 = (s32[]{:T(128)}, f32[256,8,2,64]{0,3,2,1:T(8,128)}, f32[4,512,1024]{2,1,0:T(8,128)}, bf16[4,512,8,64]{1,3,2,0:T(8,128)(2,1)}, s32[256]{0:T(256)S(1)}...) while((s32[]{:T(128)}, f32[256,8,2,64]{0,3,2,1:T(8,128)}, ...), condition=%wide.region_28.29_spmd.clone, body=%wide.region_27.28_spmd.clone.sunk | while | flops 1365115136 | bytes 88016168 | solution.py:249
  1105.0 41.9 %collective-permute-done.9 = bf16[1024,1024]{1,0:T(8,128)(2,1)S(1)} collective-permute-done((bf16[1024,1024]{1,0:T(8,128)(2,1)S(1)}, bf16[1024,1024]{1,0:T(8,128)(2,1)S(1)}, u32[]{:S(2)}, u32[]{:S(2)}) %collective-permute-start.9) | collective-permute-done | bytes 2097184 | tf_op jit(solution)/shard_map/ppermute | solution.py:41
  1233.6 56.0 %collective-permute-done.13 = bf16[512,2048]{1,0:T(8,128)(2,1)S(1)} collective-permute-done((bf16[512,2048]{1,0:T(8,128)(2,1)S(1)}, bf16[512,2048]{1,0:T(8,128)(2,1)S(1)}, u32[]{:S(2)}, u32[]{:S(2)}) %collective-permute-start.13) | collective-permute-done | bytes 2097184 | tf_op jit(solution)/shard_map/ppermute | solution.py:41
  1297.4 131.8 %all-reduce.6 = f32[2176]{0:T(1024)S(1)} all-reduce(f32[2176]{0:T(1024)S(1)} %concatenate.148), channel_id=9, replica_groups=mesh['dp'=32] {'dp'}, use_global_device_ids=true, to_apply=%region_43.44.clone | all-reduce | flops 2176 | bytes 17408
  1451.9 139.4 %reduce-scatter.8.cloned.1.call-done = f32[32,1024]{1,0:T(8,128)} async-done(((f32[1024,1024]{1,0:T(8,128)}), f32[32,1024]{1,0:T(8,128)}) %reduce-scatter.8.cloned.1.call-update) | async-done | bytes 131088 | tf_op jit(solution)/shard_map/reduce_scatter | solution.py:422
  1591.4 139.5 %reduce-scatter.14.cloned.1.call-done = f32[32,1024]{1,0:T(8,128)} async-done(((f32[1024,1024]{1,0:T(8,128)}), f32[32,1024]{1,0:T(8,128)}) %reduce-scatter.14.cloned.1.call-update) | async-done | bytes 131088 | tf_op jit(solution)/shard_map/reduce_scatter | solution.py:425
  1730.9 209.7 %reduce-scatter.16.cloned.1.call-done = f32[32,4608]{1,0:T(8,128)} async-done(((f32[1024,4608]{1,0:T(8,128)}), f32[32,4608]{1,0:T(8,128)}) %reduce-scatter.16.cloned.1.call-update) | async-done | bytes 589840 | tf_op jit(solution)/shard_map/reduce_scatter | solution.py:426
  1940.6 212.6 %reduce-scatter.18.cloned.1.call-done = f32[32,4608]{1,0:T(8,128)} async-done(((f32[1024,4608]{1,0:T(8,128)}), f32[32,4608]{1,0:T(8,128)}) %reduce-scatter.18.cloned.1.call-update) | async-done | bytes 589840 | tf_op jit(solution)/shard_map/reduce_scatter | solution.py:427
  2153.2 212.6 %reduce-scatter.20.cloned.1.call-done = f32[144,1024]{1,0:T(8,128)} async-done(((f32[4608,1024]{1,0:T(8,128)}), f32[144,1024]{1,0:T(8,128)}) %reduce-scatter.20.cloned.1.call-update) | async-done | bytes 589840 | tf_op jit(solution)/shard_map/reduce_scatter | solution.py:428
  (535 shorter events, 601.7 us)
Async XLA Ops:
  7.2 76.6 %all-gather.15.cloned.1.call-start = ((), (), s32[]{:S(2)}) async-start(), calls=%async_computation.7 | async-start | bytes 1081344 | tf_op jit(solution)/shard_map/all_gather | solution.py:102
  7.9 130.1 %all-gather.17.cloned.1.call-start = ((), (), s32[]{:S(2)}) async-start(), calls=%async_computation.8 | async-start | bytes 1081344 | tf_op jit(solution)/shard_map/all_gather | solution.py:102
  8.7 176.1 %all-gather.19.cloned.1.call-start = ((), (), s32[]{:S(2)}) async-start(), calls=%async_computation.9 | async-start | bytes 2162688 | tf_op jit(solution)/shard_map/all_gather | solution.py:102
  9.4 301.7 %all-gather.21.cloned.1.call-start = ((), (), s32[]{:S(2)}) async-start(), calls=%async_computation.10 | async-start | bytes 2162688 | tf_op jit(solution)/shard_map/all_gather | solution.py:102
  10.0 316.7 %all-gather.23.cloned.1.call-start = ((), (), s32[]{:S(2)}) async-start(), calls=%async_computation.11 | async-start | bytes 9732096 | tf_op jit(solution)/shard_map/all_gather | solution.py:102
  10.6 399.5 %all-gather.25.cloned.1.call-start = ((), (), s32[]{:S(2)}) async-start(), calls=%async_computation.12 | async-start | bytes 9732096 | tf_op jit(solution)/shard_map/all_gather | solution.py:102
  11.2 482.4 %all-gather.27.cloned.1.call-start = ((), (), s32[]{:S(2)}) async-start(), calls=%async_computation.13 | async-start | bytes 9732096 | tf_op jit(solution)/shard_map/all_gather | solution.py:102
  15.1 62.6 %collective-permute-start.1 = (bf16[512,1024]{1,0:T(8,128)(2,1)S(1)}, bf16[512,1024]{1,0:T(8,128)(2,1)}, u32[]{:S(2)}, u32[]{:S(2)}) collective-permute-start(bf16[512,1024]{1,0:T(8,128)(2,1)S(1)} %maximum_select_fusion.9), channel_id=1, source_target_pairs={{0,2},{2,0},{1,3},{3,1},{4,6},{6,4},{5,7},{7,5},{8,10},{10,8},{9,1... | collective-permute-start | bytes 3145736 | tf_op jit(solution)/shard_map/ppermute | solution.py:41
  144.0 416.0 %all-gather.31.cloned.1.call-start = ((), (), s32[]{:S(2)}) async-start(), calls=%async_computation.15 | async-start | bytes 1081344 | tf_op jit(solution)/shard_map/all_gather | solution.py:102
  507.5 108.0 %all-gather.33.cloned.1.call-start = ((), (), s32[]{:S(2)}) async-start(), calls=%async_computation.16 | async-start | bytes 1081344 | tf_op jit(solution)/shard_map/all_gather | solution.py:102
  508.2 168.2 %all-gather.35.cloned.1.call-start = ((), (), s32[]{:S(2)}) async-start(), calls=%async_computation.17 | async-start | bytes 2162688 | tf_op jit(solution)/shard_map/all_gather | solution.py:102
  508.8 274.8 %all-gather.37.cloned.1.call-start = ((), (), s32[]{:S(2)}) async-start(), calls=%async_computation.18 | async-start | bytes 2162688 | tf_op jit(solution)/shard_map/all_gather | solution.py:102
  509.6 308.8 %all-gather.39.cloned.1.call-start = ((), (), s32[]{:S(2)}) async-start(), calls=%async_computation.19 | async-start | bytes 9732096 | tf_op jit(solution)/shard_map/all_gather | solution.py:102
  510.1 391.8 %all-gather.41.cloned.1.call-start = ((), (), s32[]{:S(2)}) async-start(), calls=%async_computation.20 | async-start | bytes 9732096 | tf_op jit(solution)/shard_map/all_gather | solution.py:102
  510.9 474.5 %all-gather.29.cloned.1.call-start = ((), (), s32[]{:S(2)}) async-start(), calls=%async_computation.14 | async-start | bytes 9732096 | tf_op jit(solution)/shard_map/all_gather | solution.py:102
  650.1 800.9 %reduce-scatter.12.cloned.1.call-start = ((), (), s32[]{:S(2)}) async-start(), calls=%async_computation.23 | async-start | bytes 2162688 | tf_op jit(solution)/shard_map/reduce_scatter | solution.py:424
  1177.7 274.2 %reduce-scatter.10.cloned.1.call-start = ((), (), s32[]{:S(2)}) async-start(), calls=%async_computation.22 | async-start | bytes 2162688 | tf_op jit(solution)/shard_map/reduce_scatter | solution.py:423
  1180.6 410.8 %reduce-scatter.8.cloned.1.call-start = ((), (), s32[]{:S(2)}) async-start(), calls=%async_computation.21 | async-start | bytes 4325376 | tf_op jit(solution)/shard_map/reduce_scatter | solution.py:422
  1184.5 546.4 %reduce-scatter.14.cloned.1.call-start = ((), (), s32[]{:S(2)}) async-start(), calls=%async_computation.24 | async-start | bytes 4325376 | tf_op jit(solution)/shard_map/reduce_scatter | solution.py:425
  1187.5 753.1 %reduce-scatter.16.cloned.1.call-start = ((), (), s32[]{:S(2)}) async-start(), calls=%async_computation.25 | async-start | bytes 19464192 | tf_op jit(solution)/shard_map/reduce_scatter | solution.py:426
  1197.1 956.1 %reduce-scatter.18.cloned.1.call-start = ((), (), s32[]{:S(2)}) async-start(), calls=%async_computation.26 | async-start | bytes 19464192 | tf_op jit(solution)/shard_map/reduce_scatter | solution.py:427
  1206.8 1158.9 %reduce-scatter.20.cloned.1.call-start = ((), (), s32[]{:S(2)}) async-start(), calls=%async_computation.27 | async-start | bytes 19464192 | tf_op jit(solution)/shard_map/reduce_scatter | solution.py:428
  1232.0 57.6 %collective-permute-start.13 = (bf16[512,2048]{1,0:T(8,128)(2,1)S(1)}, bf16[512,2048]{1,0:T(8,128)(2,1)S(1)}, u32[]{:S(2)}, u32[]{:S(2)}) collective-permute-start(bf16[512,2048]{1,0:T(8,128)(2,1)S(1)} %get-tuple-element.807), channel_id=1, source_target_pairs={{0,2},{2,0},{1,3},{3,1},{4,6},{6,4},{5,7},{7,5},{8,10},{10,8},{9,1... | collective-permute-start | bytes 6291464 | tf_op jit(solution)/shard_map/ppermute | solution.py:41
  1295.9 133.8 %collective-permute-start.14 = (bf16[1024,2048]{1,0:T(8,128)(2,1)}, bf16[1024,2048]{1,0:T(8,128)(2,1)}, u32[]{:S(2)}, u32[]{:S(2)}) collective-permute-start(bf16[1024,2048]{1,0:T(8,128)(2,1)} %get-tuple-element.805), channel_id=1, source_target_pairs={{0,4},{4,0},{1,5},{5,1},{2,6},{6,2},{3,7},{7,3},{8,12},{12,8},{9,1... | collective-permute-start | bytes 12582920 | tf_op jit(solution)/shard_map/ppermute | solution.py:41
  (87 other events, 3834.5 us)
Sparse Core Ops, SparseCore 0:
  10.9 56.9 all-gather.14
  70.8 53.8 all-gather.16
  127.5 57.1 all-gather.18
  187.4 55.3 all-gather.20
  245.6 81.0 all-gather.22
  329.4 80.5 all-gather.24
  412.9 80.6 all-gather.26
  507.6 52.3 all-gather.30
  562.8 52.6 all-gather.32
  618.2 58.1 all-gather.34
  679.3 55.3 all-gather.36
  737.4 80.8 all-gather.38
  821.2 80.6 all-gather.40
  904.7 80.6 all-gather.28
  1177.9 136.9 reduce-scatter.11
  1317.6 134.2 reduce-scatter.9
  1454.6 136.7 reduce-scatter.7
  1594.1 136.7 reduce-scatter.13
  1737.9 202.6 reduce-scatter.15
  1947.4 205.6 reduce-scatter.17
  2160.2 205.5 reduce-scatter.19
where the time goes:
time: 2380 us; the launch traced here: 2370 us
  waiting for transfers between devices  1650 us (69%)
  matrix products  247 us (10%)
  blocking collectives  228 us (10%)
  local copies, waits for them, and re-layouts  107 us (4%)
  other arithmetic  104 us (4%)
    all_gather x14, waiting for transfers between devices, gather_weights(): lax.all_gather(for_sending(shards), 'dp', axis=0, tiled=True)  452 us
    ppermute x15, waiting for transfers between devices, swapped(): return lax.ppermute(block, axis, route)  276 us
    unnamed x3, blocking collectives  228 us
    reduce_scatter x1, waiting for transfers between devices, body(): lax.psum_scatter(grad_w_up, 'dp', scatter_dimension=0, tiled=True)  213 us
    reduce_scatter x1, waiting for transfers between devices, body(): lax.psum_scatter(grad_w_down, 'dp', scatter_dimension=0, tiled=True)  213 us
    reduce_scatter x1, waiting for transfers between devices, body(): lax.psum_scatter(grad_w_gate, 'dp', scatter_dimension=0, tiled=True)  210 us
    reduce_scatter x1, waiting for transfers between devices, body(): lax.psum_scatter(grad_w_out, 'dp', scatter_dimension=0, tiled=True)  140 us
    reduce_scatter x1, waiting for transfers between devices, body(): lax.psum_scatter(grad_w_query, 'dp', scatter_dimension=0, tiled=True)  139 us
  transfers between devices with their start and end apart: 36, of which 29 were waited for; matrix products, arithmetic and copies ran while one was open for 14% of the time, Pallas kernels for 0%

commit v1 on v0

v1 whole, which is shorter than its diff:
```python
import functools
import math

import jax
import jax.numpy as jnp
from jax import lax
from jax.experimental import pallas as pl
from jax.experimental.pallas import tpu as pltpu
from jax.sharding import PartitionSpec as P

D = 1024
FF = 4608
QUERY_HEADS = 16
KEY_VALUE_HEADS = 8
HEAD = 64
SLOT = 128
GROUP = 8
ROWS = 2048
BLOCK = 256
QKV = 256
EPSILON = 1e-05
ROPE_THETA = 1000000.0
SCALE = 1.0 / math.sqrt(HEAD)
LOG2E = math.log2(math.e)
F32 = jnp.float32
BF16 = jnp.bfloat16
MESH = pl.DeviceIdType.MESH
DMA = pltpu.SemaphoreType.DMA
VM = pl.BlockSpec(memory_space=pltpu.VMEM)
ANY = pl.BlockSpec(memory_space=pl.ANY)
SM = pl.BlockSpec(memory_space=pltpu.SMEM)
SDS = jax.ShapeDtypeStruct


def nn(a, b):
    return lax.dot_general(a, b, (((1,), (0,)), ((), ())), preferred_element_type=F32)


def nt(a, b):
    return lax.dot_general(a, b, (((1,), (1,)), ((), ())), preferred_element_type=F32)


def tn(a, b):
    return lax.dot_general(a, b, (((0,), (0,)), ((), ())), preferred_element_type=F32)


def rcopy(src, dst, send, recv, dev):
    return pltpu.make_async_remote_copy(
        src_ref=src, dst_ref=dst, send_sem=send, recv_sem=recv, device_id=(dev,), device_id_type=MESH
    )


def barrier(peers):
    sem = pltpu.get_barrier_semaphore()
    for q in peers:
        pl.semaphore_signal(sem, inc=1, device_id=(q,), device_id_type=MESH)
    pl.semaphore_wait(sem, len(peers))


def places(n):
    me = lax.axis_index("dp")
    p = lax.rem(me, GROUP)
    g = me // GROUP
    groups = n // GROUP
    zq = [lax.rem(g + s, groups) * GROUP + p for s in range(1, groups)]
    zg = [lax.rem(g + s, groups) for s in range(1, groups)]
    return me, p, g, groups, zq, zg


def start_all(copies):
    for c in copies:
        c.start()
    return copies


def wait_all(copies):
    for c in copies:
        c.wait()


def gather_plane(me, p, src, out, ss, rs):
    half = src.shape[0] // 2
    h = [pl.ds(0, half), pl.ds(half, half)]
    sib, xn, yn = me ^ 1, me ^ 2, me ^ 4

    def cp(a, blk, i, dev):
        return rcopy(a, out.at[blk] if isinstance(blk, jax.Array) else blk, ss.at[i], rs.at[i], dev)

    x0 = cp(src.at[h[0]], out.at[p, h[0]], 0, xn)
    y1 = cp(src.at[h[1]], out.at[p, h[1]], 1, yn)
    x1 = cp(src.at[h[1]], out.at[p, h[1]], 2, xn)
    y0 = cp(src.at[h[0]], out.at[p, h[0]], 3, yn)
    own = cp(src, out.at[p], 4, sib)
    first = start_all([x0, y1, x1, y0, own])

    def middle():
        x0.wait_recv()
        r0 = cp(out.at[p ^ 2, h[0]], out.at[p ^ 2, h[0]], 5, yn)
        f0 = cp(out.at[p ^ 2, h[0]], out.at[p ^ 2, h[0]], 6, sib)
        start_all([r0, f0])
        y1.wait_recv()
        r1 = cp(out.at[p ^ 4, h[1]], out.at[p ^ 4, h[1]], 7, xn)
        f1 = cp(out.at[p ^ 4, h[1]], out.at[p ^ 4, h[1]], 8, sib)
        start_all([r1, f1])
        x1.wait_recv()
        f2 = cp(out.at[p ^ 2, h[1]], out.at[p ^ 2, h[1]], 9, sib)
        f2.start()
        y0.wait_recv()
        f3 = cp(out.at[p ^ 4, h[0]], out.at[p ^ 4, h[0]], 10, sib)
        f3.start()
        r0.wait_recv()
        f4 = cp(out.at[p ^ 6, h[0]], out.at[p ^ 6, h[0]], 11, sib)
        f4.start()
        r1.wait_recv()
        f5 = cp(out.at[p ^ 6, h[1]], out.at[p ^ 6, h[1]], 12, sib)
        f5.start()
        own.wait_recv()
        for c in first + [r0, r1]:
            c.wait_send()
        for c in (f0, f1, f2, f3, f4, f5):
            c.wait()

    return middle


ORDER = (6, 2, 4, 0)


def reduce_plane(me, part, sibbuf, sendbuf, rbuf, s1, r1, s2, r2):
    p = lax.rem(me, GROUP)
    first = start_all(
        [
            rcopy(part(p ^ (m ^ 1)), sibbuf.at[i], s1.at[i], r1.at[i], me ^ 1)
            for i, m in enumerate(ORDER)
        ]
    )

    def middle():
        second = []
        own = None
        for i, m in enumerate(ORDER):
            first[i].wait_recv()
            val = part(p ^ m)[...].astype(F32) + sibbuf[i].astype(F32)
            if m:
                sendbuf[i] = val.astype(BF16)
                c = rcopy(sendbuf.at[i], rbuf.at[i], s2.at[i], r2.at[i], me ^ m)
                c.start()
                second.append(c)
            else:
                own = val
        for i, c in enumerate(second):
            c.wait_recv()
            own = own + rbuf[i].astype(F32)
        for c in first + second:
            c.wait_send()
        return own

    return middle


def gather_kernel(n, x, dy, a1, a2, wo, wd, gt, xo, dyo, a1o, a2o, woo, wdo, gto, ls, xs, xr, ds_, dr, ps, pr, zs, zr):
    me, p, g, groups, zq, zg = places(n)
    barrier([me ^ m for m in range(1, GROUP)] + zq)
    nz = groups - 1
    local = [
        pltpu.make_async_copy(a1.at[p], a1o.at[g, p], ls.at[0]),
        pltpu.make_async_copy(gt, gto.at[g, p], ls.at[1]),
        pltpu.make_async_copy(wo, woo.at[g, p], ls.at[2]),
        pltpu.make_async_copy(a2.at[p], a2o.at[g, p], ls.at[3]),
        pltpu.make_async_copy(wd, wdo.at[g], ls.at[4]),
        pltpu.make_async_copy(x, xo.at[p], ls.at[5]),
        pltpu.make_async_copy(dy, dyo.at[p], ls.at[6]),
    ]
    start_all(local)
    pc = {}
    for k, (src, dst) in enumerate(((a1, a1o), (gt, gto))):
        for m in range(1, GROUP):
            block = src.at[p ^ m] if k == 0 else src
            pc[k, m] = rcopy(block, dst.at[g, p], ps.at[k, m - 1], pr.at[k, m - 1], me ^ m)
            pc[k, m].start()
    xmid = gather_plane(me, p, x, xo, xs, xr)
    for k, (src, dst) in ((2, (wo, woo)), (3, (a2, a2o))):
        for m in range(1, GROUP):
            block = src.at[p ^ m] if k == 3 else src
            pc[k, m] = rcopy(block, dst.at[g, p], ps.at[k, m - 1], pr.at[k, m - 1], me ^ m)
            pc[k, m].start()
    zc = start_all([rcopy(wd, wdo.at[g], zs.at[4, s], zr.at[4, s], zq[s]) for s in range(nz)])
    for k, dst in enumerate((a1o, gto)):
        for m in range(1, GROUP):
            pc[k, m].wait_recv()
        local[k].wait()
        zc += start_all([rcopy(dst.at[g], dst.at[g], zs.at[k, s], zr.at[k, s], zq[s]) for s in range(nz)])
    for k, dst in ((2, woo), (3, a2o)):
        for m in range(1, GROUP):
            pc[k, m].wait_recv()
        local[k].wait()
        zc += start_all([rcopy(dst.at[g], dst.at[g], zs.at[k, s], zr.at[k, s], zq[s]) for s in range(nz)])
    dmid = gather_plane(me, p, dy, dyo, ds_, dr)
    xmid()
    dmid()
    for c in pc.values():
        c.wait_send()
    for c in local[4:]:
        c.wait()
    wait_all(zc)


def gather_all(n, x, dy, a1, a2, wo, wd, gt):
    groups = n // GROUP
    r = wo.shape[0]
    ffc = wd.shape[0]
    return pl.pallas_call(
        functools.partial(gather_kernel, n),
        out_shape=(
            SDS((GROUP, BLOCK, D), BF16),
            SDS((GROUP, BLOCK, D), BF16),
            SDS((groups, GROUP, r, a1.shape[-1]), BF16),
            SDS((groups, GROUP, r, a2.shape[-1]), BF16),
            SDS((groups, GROUP, r, D), BF16),
            SDS((groups, ffc, D), BF16),
            SDS((groups, GROUP, 8, 128), F32),
        ),
        in_specs=[ANY] * 7,
        out_specs=(ANY,) * 7,
        scratch_shapes=[
            DMA((7,)),
            DMA((13,)),
            DMA((13,)),
            DMA((13,)),
            DMA((13,)),
            DMA((4, 7)),
            DMA((4, 7)),
            DMA((5, groups - 1)),
            DMA((5, groups - 1)),
        ],
        compiler_params=pltpu.CompilerParams(collective_id=1, has_side_effects=True),
        name="gather_all",
    )(x, dy, a1, a2, wo, wd, gt)


def swap_halves(v):
    lane = lax.broadcasted_iota(jnp.int32, v.shape, 1)
    low = lax.rem(lane, HEAD) < HEAD // 2
    width = v.shape[1]
    return jnp.where(low, pltpu.roll(v, width - HEAD // 2, 1), pltpu.roll(v, HEAD // 2, 1))


def head_mean(v):
    lane = lax.broadcasted_iota(jnp.int32, v.shape, 1)
    low = lane < HEAD
    a = jnp.sum(jnp.where(low, v, 0.0), axis=-1, keepdims=True)
    b = jnp.sum(jnp.where(low, 0.0, v), axis=-1, keepdims=True)
    return jnp.where(low, a, b) * (1.0 / HEAD)


def seq_start(row, len_ref, g):
    e1 = len_ref[g, 0]
    e2 = e1 + len_ref[g, 1]
    e3 = e2 + len_ref[g, 2]
    zero = row * 0
    s = jnp.where(row >= e1, zero + e1, zero)
    s = jnp.where(row >= e2, zero + e2, s)
    return jnp.where(row >= e3, zero + e3, s)


def tables(cs_ref):
    t = cs_ref[...].T
    c, s = t[:, : HEAD // 2], t[:, HEAD // 2 :]
    return jnp.concatenate([c, c, c, c], axis=1), jnp.concatenate([-s, s, -s, s], axis=1)


def attn_fwd_kernel(len_ref, x_ref, w_ref, ga_ref, gqk_ref, cs_ref, h_ref, raw_ref, q_ref, kv_ref, mix_ref, mixf_ref, lse_ref, k_s, v_s, acc):
    i = pl.program_id(0)
    g = lax.axis_index("dp") // GROUP
    xb = x_ref[0].astype(F32)
    r = lax.rsqrt(jnp.mean(xb * xb, axis=-1, keepdims=True) + EPSILON)
    h = (xb * r * ga_ref[...]).astype(BF16)
    h_ref[0] = h
    raw = nn(h, w_ref[...])
    raw_ref[0] = raw
    ct, st = tables(cs_ref)
    qraw, kvraw = raw[:, :128], raw[:, 128:]
    qn = qraw * lax.rsqrt(head_mean(qraw * qraw) + EPSILON) * gqk_ref[0:1, :]
    q = (qn * ct + swap_halves(qn) * st).astype(BF16)
    kn = kvraw * lax.rsqrt(head_mean(kvraw * kvraw) + EPSILON) * gqk_ref[1:2, :]
    k = (kn * ct + swap_halves(kn) * st).astype(BF16)
    lane = lax.broadcasted_iota(jnp.int32, (BLOCK, 128), 1)
    kv = jnp.where(lane < HEAD, k.astype(F32), kvraw).astype(BF16)
    q_ref[0] = q
    kv_ref[0] = kv
    k_s[pl.ds(i * BLOCK, BLOCK), :] = kv[:, :HEAD]
    v_s[pl.ds(i * BLOCK, BLOCK), :] = jnp.where(lane < HEAD, pltpu.roll(kvraw, HEAD, 1), 1.0).astype(BF16)
    q2 = jnp.concatenate([q[:, :HEAD], q[:, HEAD:]], axis=0)
    acc[...] = jnp.zeros_like(acc)
    row = lax.broadcasted_iota(jnp.int32, (2 * BLOCK, 1), 0)
    qrow = i * BLOCK + jnp.where(row >= BLOCK, row - BLOCK, row)
    qstart = seq_start(qrow, len_ref, g)
    first = seq_start(i * BLOCK, len_ref, g) // BLOCK
    col = lax.broadcasted_iota(jnp.int32, (2 * BLOCK, BLOCK), 1)

    def step(j, carry):
        kb = k_s[pl.ds(pl.multiple_of(j * BLOCK, BLOCK), BLOCK), :]
        vb = v_s[pl.ds(pl.multiple_of(j * BLOCK, BLOCK), BLOCK), :]
        s = nt(q2, kb)
        kc = col + j * BLOCK
        ok = (kc >= qstart) & (kc <= qrow)
        e = jnp.where(ok, jnp.exp2(s * (SCALE * LOG2E)), 0.0).astype(BF16)
        acc[...] += nn(e, vb)
        return carry

    lax.fori_loop(first, i + 1, step, 0)
    total = acc[:, HEAD:]
    m = acc[:, :HEAD] / total
    both = jnp.concatenate([m[:BLOCK], m[BLOCK:]], axis=1)
    mixf_ref[0] = both
    mix_ref[0] = both.astype(BF16)
    lse_ref[0] = jnp.log2(total.T)[:8, :]


def attn_fwd(lengths, x_all, wqkv, ga, gqk, cs):
    blk = lambda c: pl.BlockSpec((1, BLOCK, c), lambda i: (i, 0, 0))
    whole = lambda s: pl.BlockSpec(s, lambda i: (0,) * len(s), pipeline_mode=pl.Buffered(1))
    nb = ROWS // BLOCK
    return pl.pallas_call(
        attn_fwd_kernel,
        grid=(nb,),
        in_specs=[
            SM,
            blk(D),
            whole((D, QKV)),
            whole((1, D)),
            whole((2, 128)),
            pl.BlockSpec((HEAD, BLOCK), lambda i: (0, i)),
        ],
        out_specs=(blk(D), blk(QKV), blk(128), blk(128), blk(128), blk(128), pl.BlockSpec((1, 8, 2 * BLOCK), lambda i: (i, 0, 0))),
        out_shape=(
            SDS((nb, BLOCK, D), BF16),
            SDS((nb, BLOCK, QKV), F32),
            SDS((nb, BLOCK, 128), BF16),
            SDS((nb, BLOCK, 128), BF16),
            SDS((nb, BLOCK, 128), BF16),
            SDS((nb, BLOCK, 128), F32),
            SDS((nb, 8, 2 * BLOCK), F32),
        ),
        scratch_shapes=[
            pltpu.VMEM((ROWS, HEAD), BF16),
            pltpu.VMEM((ROWS, 128), BF16),
            pltpu.VMEM((2 * BLOCK, 128), F32),
        ],
        compiler_params=pltpu.CompilerParams(dimension_semantics=("arbitrary",), vmem_limit_bytes=48 << 20),
        cost_estimate=pl.CostEstimate(flops=4 * 10**9, bytes_accessed=16 << 20, transcendentals=4 * 10**6),
        name="attn_fwd",
    )(lengths, x_all, wqkv, ga, gqk, cs)


def mid_kernel(n, mix, x, wo, gf, res, mown, h2, h2all, mbuf, ps, pr, hs, hr, ls):
    me, p, g, groups, zq, zg = places(n)
    barrier([me ^ m for m in range(1, GROUP)])
    pc = start_all(
        [rcopy(mix.at[p ^ m], mbuf.at[p], ps.at[m - 1], pr.at[m - 1], me ^ m) for m in range(1, GROUP)]
    )
    mbuf[p] = mix[p]
    for c in pc:
        c.wait_recv()
    m = jnp.concatenate([mbuf[b] for b in range(GROUP)], axis=1)
    mown[...] = m
    z = x[...].astype(F32) + nn(m, wo[...])
    res[...] = z
    r = lax.rsqrt(jnp.mean(z * z, axis=-1, keepdims=True) + EPSILON)
    h2[...] = (z * r * gf[...]).astype(BF16)
    done = gather_plane(me, p, h2, h2all, hs, hr)
    cl = pltpu.make_async_copy(h2, h2all.at[p], ls)
    cl.start()
    done()
    cl.wait()
    for c in pc:
        c.wait_send()


def mid(n, mix, x, wo, gf):
    return pl.pallas_call(
        functools.partial(mid_kernel, n),
        out_shape=(SDS((BLOCK, D), F32), SDS((BLOCK, D), BF16), SDS((BLOCK, D), BF16), SDS((GROUP, BLOCK, D), BF16)),
        in_specs=[VM] * 4,
        out_specs=(VM, VM, VM, ANY),
        scratch_shapes=[
            pltpu.VMEM((GROUP, BLOCK, 128), BF16),
            DMA((7,)),
            DMA((7,)),
            DMA((13,)),
            DMA((13,)),
            DMA,
        ],
        compiler_params=pltpu.CompilerParams(collective_id=2, has_side_effects=True, vmem_limit_bytes=48 << 20),
        name="mid",
    )(mix, x, wo, gf)


def ffn_kernel(inv_ref, h_ref, da_ref, db_ref, wgu_ref, wd_ref, po_ref, dh_ref, dwgu_ref, dwd_ref, agu, ad):
    i = pl.program_id(0)
    fl = wd_ref.shape[0]

    @pl.when(i == 0)
    def _():
        agu[...] = jnp.zeros_like(agu)
        ad[...] = jnp.zeros_like(ad)

    h = h_ref[0]
    dy = jnp.concatenate([da_ref[0], db_ref[0]], axis=0)
    gp = nn(h, wgu_ref[:, :fl])
    up = nn(h, wgu_ref[:, fl:])
    sig = 1.0 / (1.0 + jnp.exp(-gp))
    sg = gp * sig
    act = (sg * up).astype(BF16)
    po_ref[0] = nn(act, wd_ref[...]).astype(BF16)
    da = nt(dy, wd_ref[...])
    dg = (da * up * (sig * (1.0 + gp * (1.0 - sig)))).astype(BF16)
    du = (da * sg).astype(BF16)
    dh_ref[0] = (nt(dg, wgu_ref[:, :fl]) + nt(du, wgu_ref[:, fl:])).astype(BF16)
    ad[...] += tn(act, dy)
    agu[:, :fl] += tn(h, dg)
    agu[:, fl:] += tn(h, du)

    @pl.when(i == pl.num_programs(0) - 1)
    def _():
        dwgu_ref[...] = agu[...].astype(BF16)
        dwd_ref[...] = ad[...].astype(BF16)


def ffn(inv, h2all, dyall, wgu, wd):
    nb = ROWS // BLOCK
    fl = wd.shape[0]
    blk = pl.BlockSpec((1, BLOCK, D), lambda i, inv: (i, 0, 0))
    one = pl.Buffered(1)
    slots = dyall.reshape(ROWS // SLOT, SLOT, D)
    return pl.pallas_call(
        ffn_kernel,
        grid_spec=pltpu.PrefetchScalarGridSpec(
            num_scalar_prefetch=1,
            grid=(nb,),
            in_specs=[
                blk,
                pl.BlockSpec((1, SLOT, D), lambda i, inv: (inv[2 * i], 0, 0)),
                pl.BlockSpec((1, SLOT, D), lambda i, inv: (inv[2 * i + 1], 0, 0)),
                pl.BlockSpec((D, 2 * fl), lambda i, inv: (0, 0), pipeline_mode=one),
                pl.BlockSpec((fl, D), lambda i, inv: (0, 0), pipeline_mode=one),
            ],
            out_specs=(
                blk,
                blk,
                pl.BlockSpec((D, 2 * fl), lambda i, inv: (0, 0), pipeline_mode=one),
                pl.BlockSpec((fl, D), lambda i, inv: (0, 0), pipeline_mode=one),
            ),
            scratch_shapes=[pltpu.VMEM((D, 2 * fl), F32), pltpu.VMEM((fl, D), F32)],
        ),
        out_shape=(
            SDS((nb, BLOCK, D), BF16),
            SDS((nb, BLOCK, D), BF16),
            SDS((D, 2 * fl), BF16),
            SDS((fl, D), BF16),
        ),
        compiler_params=pltpu.CompilerParams(dimension_semantics=("arbitrary",), vmem_limit_bytes=56 << 20),
        cost_estimate=pl.CostEstimate(flops=24 * 10**9, bytes_accessed=24 << 20, transcendentals=10**6),
        name="ffn",
    )(inv, h2all, slots, slots, wgu, wd)


def norm_back(dyv, xv, gain):
    r = lax.rsqrt(jnp.mean(xv * xv, axis=-1, keepdims=True) + EPSILON)
    xr = xv * r
    gy = dyv * gain
    dx = r * (gy - xr * jnp.mean(gy * xr, axis=-1, keepdims=True))
    return dx, jnp.sum(dyv * xr, axis=0, keepdims=True)


def back_mid_kernel(n, dh, po, dyo, res, mown, wo, gf, result, gmid, dgf, dwo, dmh, sib1, send1, rb1, sib2, send2, rb2, dmix, sem, ps, pr):
    me, p, g, groups, zq, zg = places(n)
    barrier([me ^ m for m in range(1, GROUP)])
    part = lambda ref: (lambda b: ref.at[b])
    mid1 = reduce_plane(me, part(dh), sib1, send1, rb1, sem.at[0], sem.at[1], sem.at[2], sem.at[3])
    dh2 = mid1()
    mid2 = reduce_plane(me, part(po), sib2, send2, rb2, sem.at[4], sem.at[5], sem.at[6], sem.at[7])
    dx, dgain = norm_back(dh2, res[...], gf[...])
    gm = dyo[...].astype(F32) + dx
    gmid[...] = gm
    dgf[...] = dgain
    gl = gm.astype(BF16)
    dm = nt(gl, wo[...]).astype(BF16)
    for b in range(GROUP):
        dmix[b] = dm[:, 128 * b : 128 * (b + 1)]
    pc = start_all(
        [rcopy(dmix.at[p ^ m], dmh.at[p], ps.at[m - 1], pr.at[m - 1], me ^ m) for m in range(1, GROUP)]
    )
    dmh[p] = dmix[p]
    dwo[...] = tn(mown[...], gl).astype(BF16)
    result[...] = (mid2() + res[...]).astype(BF16)
    wait_all(pc)


def back_mid(n, dh, po, dyo, res, mown, wo, gf):
    rb = lambda k: pltpu.VMEM((k, BLOCK, D), BF16)
    return pl.pallas_call(
        functools.partial(back_mid_kernel, n),
        out_shape=(
            SDS((BLOCK, D), BF16),
            SDS((BLOCK, D), F32),
            SDS((1, D), F32),
            SDS((D, D), BF16),
            SDS((GROUP, BLOCK, 128), BF16),
        ),
        in_specs=[VM] * 7,
        out_specs=(VM,) * 5,
        scratch_shapes=[
            rb(4),
            rb(3),
            rb(3),
            rb(4),
            rb(3),
            rb(3),
            pltpu.VMEM((GROUP, BLOCK, 128), BF16),
            DMA((8, 4)),
            DMA((7,)),
            DMA((7,)),
        ],
        compiler_params=pltpu.CompilerParams(collective_id=3, has_side_effects=True, vmem_limit_bytes=58 << 20),
        name="back_mid",
    )(dh, po, dyo, res, mown, wo, gf)


def attn_bwd_kernel(len_ref, dm_ref, q_ref, kvall_ref, lse_ref, mixf_ref, h_ref, raw_ref, w_ref, gqk_ref, cs_ref, dh_ref, dw_ref, dg_ref, k_s, v_s, dkv, dqt, dws):
    step_id = pl.program_id(0)
    nb = pl.num_programs(0)
    i = nb - 1 - step_id
    g = lax.axis_index("dp") // GROUP

    @pl.when(step_id == 0)
    def _():
        dkv[...] = jnp.zeros_like(dkv)
        dws[...] = jnp.zeros_like(dws)
        dg_ref[...] = jnp.zeros_like(dg_ref)
        for b in range(ROWS // BLOCK):
            kvb = kvall_ref[b]
            k_s[pl.ds(b * BLOCK, BLOCK), :] = kvb[:, :HEAD]
            v_s[pl.ds(b * BLOCK, BLOCK), :] = kvb[:, HEAD:]

    q, do, mf = q_ref[0], dm_ref[0], mixf_ref[0]
    q2 = jnp.concatenate([q[:, :HEAD], q[:, HEAD:]], axis=0)
    do2 = jnp.concatenate([do[:, :HEAD], do[:, HEAD:]], axis=0)
    prod = (do.astype(F32) * mf).T
    delta = jnp.concatenate(
        [jnp.sum(prod[:HEAD], axis=0, keepdims=True), jnp.sum(prod[HEAD:], axis=0, keepdims=True)], axis=1
    )
    lse = lse_ref[0, 0:1, :]
    colq = lax.broadcasted_iota(jnp.int32, (1, 2 * BLOCK), 1)
    qrow = i * BLOCK + jnp.where(colq >= BLOCK, colq - BLOCK, colq)
    qstart = seq_start(qrow, len_ref, g)
    first = seq_start(i * BLOCK, len_ref, g) // BLOCK
    rowk = lax.broadcasted_iota(jnp.int32, (BLOCK, 2 * BLOCK), 0)
    dqt[...] = jnp.zeros_like(dqt)

    def step(j, carry):
        at = pl.ds(pl.multiple_of(j * BLOCK, BLOCK), BLOCK)
        kb, vb = k_s[at, :], v_s[at, :]
        s = nt(kb, q2)
        kc = rowk + j * BLOCK
        ok = (kc >= qstart) & (kc <= qrow)
        pr = jnp.where(ok, jnp.exp2(s * (SCALE * LOG2E) - lse), 0.0)
        dp = nt(vb, do2)
        dsc = (pr * (dp - delta)).astype(BF16)
        dkv[at, :HEAD] += nn(dsc, q2)
        dkv[at, HEAD:] += nn(pr.astype(BF16), do2)
        dqt[...] += tn(dsc, kb)
        return carry

    lax.fori_loop(first, i + 1, step, 0)
    ct, st = tables(cs_ref)
    raw = raw_ref[0]
    dq = jnp.concatenate([dqt[:BLOCK], dqt[BLOCK:]], axis=1) * SCALE
    dkvb = dkv[pl.ds(pl.multiple_of(i * BLOCK, BLOCK), BLOCK), :]
    lane = lax.broadcasted_iota(jnp.int32, (BLOCK, 128), 1)

    def pull(d, v, gain):
        dn = d * ct - swap_halves(d) * st
        r = lax.rsqrt(head_mean(v * v) + EPSILON)
        vr = v * r
        gy = dn * gain
        return r * (gy - vr * head_mean(gy * vr)), jnp.sum(dn * vr, axis=0, keepdims=True)

    dqr, dgq = pull(dq, raw[:, :128], gqk_ref[0:1, :])
    dkr, dgk = pull(dkvb * SCALE, raw[:, 128:], gqk_ref[1:2, :])
    dg_ref[0:1, :] += dgq
    dg_ref[1:2, :] += dgk
    dqkv = jnp.concatenate([dqr, jnp.where(lane < HEAD, dkr, dkvb)], axis=1).astype(BF16)
    dh_ref[0] = nt(dqkv, w_ref[...]).astype(BF16)
    dws[...] += tn(h_ref[0], dqkv)

    @pl.when(step_id == nb - 1)
    def _():
        dw_ref[...] = dws[...].astype(BF16)


def attn_bwd(lengths, dmh, q, kv, lse, mixf, h, raw, wqkv, gqk, cs):
    nb = ROWS // BLOCK
    blk = lambda c: pl.BlockSpec((1, BLOCK, c), lambda i: (nb - 1 - i, 0, 0))
    whole = lambda s: pl.BlockSpec(s, lambda i: (0,) * len(s), pipeline_mode=pl.Buffered(1))
    return pl.pallas_call(
        attn_bwd_kernel,
        grid=(nb,),
        in_specs=[
            SM,
            blk(128),
            blk(128),
            whole((nb, BLOCK, 128)),
            pl.BlockSpec((1, 8, 2 * BLOCK), lambda i: (nb - 1 - i, 0, 0)),
            blk(128),
            blk(D),
            blk(QKV),
            whole((D, QKV)),
            whole((2, 128)),
            pl.BlockSpec((HEAD, BLOCK), lambda i: (0, nb - 1 - i)),
        ],
        out_specs=(blk(D), whole((D, QKV)), whole((8, 128))),
        out_shape=(SDS((nb, BLOCK, D), BF16), SDS((D, QKV), BF16), SDS((8, 128), F32)),
        scratch_shapes=[
            pltpu.VMEM((ROWS, HEAD), BF16),
            pltpu.VMEM((ROWS, HEAD), BF16),
            pltpu.VMEM((ROWS, 128), F32),
            pltpu.VMEM((2 * BLOCK, HEAD), F32),
            pltpu.VMEM((D, QKV), F32),
        ],
        compiler_params=pltpu.CompilerParams(dimension_semantics=("arbitrary",), vmem_limit_bytes=48 << 20),
        cost_estimate=pl.CostEstimate(flops=8 * 10**9, bytes_accessed=16 << 20, transcendentals=4 * 10**6),
        name="attn_bwd",
    )(lengths, dmh, q, kv, lse, mixf, h, raw, wqkv, gqk, cs)


def final_kernel(n, dh, x, gmid, ga, dgf, dgqk, dw1, dw2, dwd, dwo, gtok, o1, o2, od, oo, og, sib1, send1, rb1, z1, z2, zd, zo, t1, t2, wsib, wsend, wrb, wsum, gpart, gin, gsum, gz, sem, wsem, zs, zr, ps, pr, gs, gr):
    me, p, g, groups, zq, zg = places(n)
    nz = groups - 1
    barrier([me ^ m for m in range(1, GROUP)] + zq)
    mid1 = reduce_plane(me, lambda b: dh.at[b], sib1, send1, rb1, sem.at[0], sem.at[1], sem.at[2], sem.at[3])
    zc = {}
    for k, (src, dst) in enumerate(((dw1, z1), (dw2, z2), (dwd, zd))):
        for s in range(nz):
            zc[k, s] = rcopy(src.at[zg[s]], dst.at[s], zs.at[k, s], zr.at[k, s], zq[s])
            zc[k, s].start()
    first = start_all(
        [rcopy(dwo.at[:, p ^ (m ^ 1)], wsib.at[i], wsem.at[0, i], wsem.at[1, i], me ^ 1) for i, m in enumerate(ORDER)]
    )
    dh1 = mid1()
    dx, dga = norm_back(dh1, x[...].astype(F32), ga[...])
    gtok[...] = gmid[...] + dx
    gpart[...] = jnp.zeros_like(gpart)
    for b in range(8):
        gpart[b : b + 1, :] = dga[:, 128 * b : 128 * (b + 1)]
        gpart[8 + b : 9 + b, :] = dgf[:, 128 * b : 128 * (b + 1)]
    lane = lax.broadcasted_iota(jnp.int32, (1, 128), 1)
    dgq = dgqk[0:1, :]
    dgq = dgq + pltpu.roll(jnp.broadcast_to(dgq, (8, 128)), HEAD, 1)[0:1, :]
    dgk = pltpu.roll(jnp.broadcast_to(dgqk[1:2, :], (8, 128)), HEAD, 1)[0:1, :]
    gpart[16:17, :] = jnp.where(lane < HEAD, dgq, dgk)
    gc = start_all([rcopy(gpart, gin.at[m - 1], gs.at[m - 1], gr.at[m - 1], me ^ m) for m in range(1, GROUP)])
    second = []
    own = None
    for i, m in enumerate(ORDER):
        first[i].wait_recv()
        val = dwo[:, p ^ m].astype(F32) + wsib[i].astype(F32)
        if m:
            wsend[i] = val.astype(BF16)
            c = rcopy(wsend.at[i], wrb.at[i], wsem.at[2, i], wsem.at[3, i], me ^ m)
            c.start()
            second.append(c)
        else:
            own = val
    tot = gpart[...]
    for m in range(1, GROUP):
        gc[m - 1].wait_recv()
        tot = tot + gin[m - 1]
    gsum[...] = tot
    gzc = start_all([rcopy(gsum, gz.at[s], gs.at[7 + s], gr.at[7 + s], zq[s]) for s in range(nz)])
    for i, c in enumerate(second):
        c.wait_recv()
        own = own + wrb[i].astype(F32)
    wsum[...] = own.astype(BF16)
    for s in range(nz):
        zc[3, s] = rcopy(wsum.at[zg[s]], zo.at[s], zs.at[3, s], zr.at[3, s], zq[s])
        zc[3, s].start()
    pc = []
    for k, (src, dst, tmp, out) in enumerate(((dw1, z1, t1, o1), (dw2, z2, t2, o2))):
        acc = src[g].astype(F32)
        for s in range(nz):
            zc[k, s].wait_recv()
            acc = acc + dst[s].astype(F32)
        tmp[...] = acc.astype(BF16)
        for m in range(1, GROUP):
            c = rcopy(tmp.at[p ^ m], out.at[p], ps.at[k, m - 1], pr.at[k, m - 1], me ^ m)
            c.start()
            pc.append(c)
        out[p] = tmp[p]
    for k, (mine, dst, out) in ((2, (dwd[g], zd, od)), (3, (wsum[g], zo, oo))):
        acc = mine.astype(F32)
        for s in range(nz):
            zc[k, s].wait_recv()
            acc = acc + dst[s].astype(F32)
        out[...] = acc
    tot = gsum[...]
    for s in range(nz):
        gzc[s].wait_recv()
        tot = tot + gz[s]
    og[...] = tot
    wait_all(pc)
    for c in gc + gzc + first + second + list(zc.values()):
        c.wait_send()


def final(n, dh, x, gmid, ga, dgf, dgqk, dw1, dw2, dwd, dwo):
    groups = n // GROUP
    nz = groups - 1
    r, c1, c2, ffc = dw1.shape[2], dw1.shape[3], dw2.shape[3], dwd.shape[1]
    rb = lambda k: pltpu.VMEM((k, BLOCK, D), BF16)
    return pl.pallas_call(
        functools.partial(final_kernel, n),
        out_shape=(
            SDS((BLOCK, D), F32),
            SDS((GROUP, r, c1), BF16),
            SDS((GROUP, r, c2), BF16),
            SDS((ffc, D), F32),
            SDS((r, D), F32),
            SDS((24, 128), F32),
        ),
        in_specs=[VM] * 10,
        out_specs=(VM,) * 6,
        scratch_shapes=[
            rb(4),
            rb(3),
            rb(3),
            pltpu.VMEM((nz, GROUP, r, c1), BF16),
            pltpu.VMEM((nz, GROUP, r, c2), BF16),
            pltpu.VMEM((nz, ffc, D), BF16),
            pltpu.VMEM((nz, r, D), BF16),
            pltpu.VMEM((GROUP, r, c1), BF16),
            pltpu.VMEM((GROUP, r, c2), BF16),
            pltpu.VMEM((4, groups, r, D), BF16),
            pltpu.VMEM((3, groups, r, D), BF16),
            pltpu.VMEM((3, groups, r, D), BF16),
            pltpu.VMEM((groups, r, D), BF16),
            pltpu.VMEM((24, 128), F32),
            pltpu.VMEM((7, 24, 128), F32),
            pltpu.VMEM((24, 128), F32),
            pltpu.VMEM((nz, 24, 128), F32),
            DMA((4, 4)),
            DMA((4, 4)),
            DMA((4, nz)),
            DMA((4, nz)),
            DMA((2, 7)),
            DMA((2, 7)),
            DMA((7 + nz,)),
            DMA((7 + nz,)),
        ],
        compiler_params=pltpu.CompilerParams(collective_id=4, has_side_effects=True, vmem_limit_bytes=58 << 20),
        name="final",
    )(dh, x, gmid, ga, dgf, dgqk, dw1, dw2, dwd, dwo)


def body(n, tokens, w_query, key_weight, w_value, w_out, w_gate, w_up, w_down, norm_gains, seq_lengths, slot_order, out_grad):
    groups = n // GROUP
    r = w_query.shape[0]
    ffc = w_down.shape[0]
    device = lax.axis_index("dp")
    g, p = device // GROUP, device % GROUP
    lengths = seq_lengths
    a1 = jnp.concatenate(
        [
            w_query.reshape(r, GROUP, 128),
            key_weight.reshape(r, GROUP, HEAD),
            w_value.reshape(r, GROUP, HEAD),
        ],
        axis=2,
    ).transpose(1, 0, 2)
    wgu = jnp.stack([w_gate, w_up], axis=1).reshape(r, 2, groups, GROUP, ffc)
    a2 = wgu.transpose(3, 0, 1, 2, 4).reshape(GROUP, r, 2 * groups * ffc)
    share = norm_gains.shape[0]
    gt = jnp.pad(norm_gains.astype(F32)[None, :], ((0, 7), (0, 128 - share)))
    x_all, dy_all, w1, w2, wo, wd, gains = gather_all(n, tokens, out_grad, a1, a2, w_out, w_down, gt)
    gains = gains[:, :, 0, :share].reshape(1, -1)
    ga, gf = gains[:, :D], gains[:, D : 2 * D]
    gq = gains[:, 2 * D : 2 * D + HEAD]
    gk = gains[:, 2 * D + HEAD :]
    gqk = jnp.concatenate([jnp.concatenate([gq, gq], axis=1), jnp.concatenate([gk, gk], axis=1)], axis=0)
    wqkv = w1.reshape(D, QKV)
    wgu = w2.reshape(D, -1)
    wo = wo.reshape(D, D)
    wd = wd.reshape(-1, D)
    row = jnp.arange(ROWS, dtype=jnp.int32)
    length_row = lax.dynamic_index_in_dim(seq_lengths, g, 0, keepdims=False)
    order_row = lax.dynamic_index_in_dim(slot_order, g, 0, keepdims=False)
    ends = jnp.cumsum(length_row)
    start = jnp.max(jnp.where(row[:, None] >= ends[None, :], ends[None, :], 0), axis=1)
    frequency = jnp.exp(jnp.arange(HEAD // 2, dtype=F32) * (-2.0 * math.log(ROPE_THETA) / HEAD))
    angles = frequency[:, None] * (row - start).astype(F32)[None, :]
    cs = jnp.concatenate([jnp.cos(angles), jnp.sin(angles)], axis=0)
    slots = jnp.arange(ROWS // SLOT, dtype=jnp.int32)
    inv = jnp.sum(jnp.where(order_row[None, :] == slots[:, None], slots[None, :], 0), axis=1)

    h, raw, q, kv, mix, mixf, lse = attn_fwd(lengths, x_all, wqkv, ga, gqk, cs)
    res, mown, _, h2_all = mid(n, mix, tokens, wo, gf)
    po, dh2, dwgu, dwd = ffn(inv, h2_all, dy_all, wgu, wd)
    dslots = dy_all.reshape(ROWS // SLOT, SLOT, D)
    dy_own = jnp.concatenate(
        [lax.dynamic_index_in_dim(dslots, inv[2 * p + k], 0, keepdims=False) for k in range(2)], axis=0
    )
    result, gmid, dgf, dwo, dmh = back_mid(n, dh2, po, dy_own, res, mown, wo, gf)
    dh1, dwqkv, dgqk = attn_bwd(lengths, dmh, q, kv, lse, mixf, h, raw, wqkv, gqk, cs)
    gtok, o1, o2, od, oo, og = final(
        n,
        dh1,
        tokens,
        gmid,
        ga,
        dgf,
        dgqk,
        dwqkv.reshape(groups, GROUP, r, QKV),
        dwgu.reshape(groups, GROUP, r, -1),
        dwd.reshape(groups, ffc, D),
        dwo.reshape(groups, GROUP, r, D),
    )
    o1 = o1.transpose(1, 0, 2).astype(F32)
    gwq = o1[:, :, :128].reshape(r, -1)
    gwk = o1[:, :, 128 : 128 + HEAD].reshape(r, -1)
    gwv = o1[:, :, 128 + HEAD :].reshape(r, -1)
    o2 = o2.reshape(GROUP, r, 2, groups, ffc).transpose(2, 1, 3, 0, 4).reshape(2, r, -1).astype(F32)
    gains_out = lax.dynamic_slice(og.reshape(-1), (device * share,), (share,))
    return result, gtok, gwq, gwk, gwv, oo, o2[0], o2[1], od, gains_out


def solution(mesh):
    n = mesh.shape["dp"]
    row = P("dp", None)
    return jax.shard_map(
        functools.partial(body, n),
        mesh=mesh,
        in_specs=(row,) * 8 + (P("dp"), P(), P(), row),
        out_specs=(row,) * 9 + (P("dp"),),
        check_vma=False,
    )
```

time: 2380 us -> 480 us (0.20)
  waiting for transfers between devices: 1650 us -> 0 us
  Pallas kernels: 0 us -> 437 us
  matrix products: 247 us -> 0 us
  blocking collectives: 228 us -> 0 us
  other arithmetic: 104 us -> 4.97 us
  local copies, waits for them, and re-layouts: 107 us -> 33.8 us
    reduce_scatter x7 -> x0, waiting for transfers between devices: 915 us -> none  [the longest x1 213 us: body(): lax.psum_scatter(grad_w_up, 'dp', scatter_dimension=0, tiled=True)]
    all_gather x14 -> x0, waiting for transfers between devices: 452 us -> none  [gather_weights(): lax.all_gather(for_sending(shards), 'dp', axis=0, tiled=True)]
    pallas_call x0 -> x7, Pallas kernels: none -> 437 us  [the longest x1 132 us: gather_all(): pl.pallas_call(functools.partial(gather_kernel, n), out_shape=(SDS((GROUP...]
    ppermute x15 -> x0, waiting for transfers between devices: 276 us -> none  [swapped(): return lax.ppermute(block, axis, route)]
    dot_general x62 -> x0, matrix products: 247 us -> none  [the longest x12 54.8 us: block_scores(): jnp.einsum('qgrd,kgd->qgrk', heads_query, key_block, preferred_element_ty...]
    unnamed x3 -> x0, blocking collectives: 228 us -> none
    reduce_sum x16 -> x1, other arithmetic: 38.2 us -> 0.63 us  [body(): jnp.sum(jnp.where(order_row[None, :] == slots[:, None], slots[None, :], 0...]
    select_n x16 -> x0, other arithmetic: 34.8 us -> none  [the longest x10 30 us: join_sides(): jnp.where(lower_side, jnp.concatenate([block_data, partner], axis=0), jnp...]
  transfers between devices with their start and end apart: 36 -> 0, of which waited for: 29 -> 0; matrix products, arithmetic and copies ran while one was open for 14% -> 0% of each run, Pallas kernels for 0% -> 0%
where the time goes in v1:
time: 480 us; the launch traced here: 481 us
  Pallas kernels  437 us (91%)
  local copies, waits for them, and re-layouts  33.8 us (7%)
  other arithmetic  4.97 us (1%)
  between operations  4.96 us (1%)
    pallas_call x1, Pallas kernels, gather_all(): pl.pallas_call(functools.partial(gather_kernel, n), out_shape=(SDS((GROUP...  132 us
    pallas_call x1, Pallas kernels, final(): pl.pallas_call(functools.partial(final_kernel, n), out_shape=(SDS((BLOCK,...  119 us
    pallas_call x1, Pallas kernels, back_mid(): pl.pallas_call(functools.partial(back_mid_kernel, n), out_shape=(SDS((BLO...  67.4 us
    pallas_call x1, Pallas kernels, ffn(): pl.pallas_call(ffn_kernel, grid_spec=pltpu.PrefetchScalarGridSpec(num_sca...  39.9 us
    pallas_call x1, Pallas kernels, mid(): pl.pallas_call(functools.partial(mid_kernel, n), out_shape=(SDS((BLOCK, D...  31.8 us
    pallas_call x1, Pallas kernels, attn_bwd(): pl.pallas_call(attn_bwd_kernel, grid=(nb,), in_specs=[SM, blk(128), blk(1...  28.2 us
    pallas_call x1, Pallas kernels, attn_fwd(): pl.pallas_call(attn_fwd_kernel, grid=(nb,), in_specs=[SM, blk(D), whole((...  18.9 us
    unnamed x66, local copies, waits for them, and re-layouts  12.4 us

profile of v1, /device:TPU:0, one launch (start us, length us, event | category | flops | bytes accessed | tf_op | source)
XLA Modules:
  0.0 481.0 jit_solution(2901809241455648952)
XLA Ops:
  1.7 1.0 multiply_cosine_fusion
  2.8 1.8 stack.9
  4.8 0.9 stack.10
  6.7 1.8 reshape.125.a2
  10.2 132.0 %gather_all.1 = (bf16[8,256,1024]{2,1,0:T(8,128)(2,1)}, bf16[8,256,1024]{2,1,0:T(8,128)(2,1)}, bf16[4,8,32,256]{3,2,1,0:T(8,128)(2,1)}, bf16[4,8,32,1152]{3,2,1,...) custom-call(bf16[256,1024]{1,0:T(8,128)(2,1)} %x.7, ...), custom_call_target="tpu_custom_call" | custom-call | tf_op jit(solution)/shard_map/gather_all/pallas_call | solution.py:212
  142.2 0.9 slice_reduce_fusion
  143.4 1.0 copy-done.10
  144.5 18.9 %attn_fwd.1 = (bf16[8,256,1024]{2,1,0:T(8,128)(2,1)}, f32[8,256,256]{2,1,0:T(8,128)S(1)}, bf16[8,256,128]{2,1,0:T(8,128)(2,1)S(1)}, bf16[8,256,128]{2,1,0:T(8,12...) custom-call(s32[4,4]{1,0:T(4,128)S(1)} %copy-done.13, ...), custom_call_target="tpu_custom_call" | custom-call | flops 4000000000 | bytes 16777216 | tf_op jit(solution)/shard_map/attn_fwd/pallas_call | solution.py:324
  163.3 1.3 copy-done.14
  164.7 1.0 copy-done.15
  167.2 31.8 %mid.1 = (f32[256,1024]{1,0:T(8,128)S(1)}, bf16[256,1024]{1,0:T(8,128)(2,1)S(1)}, bf16[256,1024]{1,0:T(8,128)(2,1)}, bf16[8,256,1024]{2,1,0:T(8,128)(2,1)}) custom-call(bf16[8,256,128]{2,1,0:T(8,128)(2,1)S(1)} %get-tuple-element.48.mix, bf16[256,1024]{1,0:T(8,128)(2,1)S(1)} %copy-done.3, bf16[1024,1024]{1,0:T(8,128)(2,1)S(1)} %bitcast.44, ...), custom_call_target="tpu_custom_call" | custom-call | tf_op jit(solution)/shard_map/mid/pallas_call | solution.py:381
  199.0 1.0 copy-done.4
  202.1 39.9 %ffn.1 = (bf16[8,256,1024]{2,1,0:T(8,128)(2,1)}, bf16[8,256,1024]{2,1,0:T(8,128)(2,1)}, bf16[1024,1152]{1,0:T(8,128)(2,1)}, bf16[576,1024]{1,0:T(8,128)(2,1)}) custom-call(s32[16]{0:T(128)} %select_reduce_fusion.1.inv_ref, bf16[8,256,1024]{2,1,0:T(8,128)(2,1)} %get-tuple-element.50.h_ref, bf16[16,128,1024]{2,1,0:T(8,128)(2,1)} %bitcast.52, ...), custom_call_target="tpu_custom_call" | custom-call | flops 24000000000 | bytes 25165824 | tf_op jit(solution)/shard_map/ffn/pallas_call | solution.py:436
  246.5 1.1 dynamic-slice_bitcast_fusion.1
  247.6 0.8 pad_maximum_fusion.1.dyo
  248.4 67.4 %back_mid.1 = (bf16[256,1024]{1,0:T(8,128)(2,1)}, f32[256,1024]{1,0:T(8,128)}, f32[1,1024]{1,0:T(1,128)}, bf16[1024,1024]{1,0:T(8,128)(2,1)}, bf16[8,256,128]{2,1,0:T(8,128)(2,1)}) custom-call(bf16[8,256,1024]{2,1,0:T(8,128)(2,1)} %get-tuple-element.54.dh, bf16[8,256,1024]{2,1,0:T(8,128)(2,1)} %get-tuple-element.55.po, ...), custom_call_target="tpu_custom_call" | custom-call | tf_op jit(solution)/shard_map/back_mid/pallas_call | solution.py:502
  315.9 1.0 copy-done.12
  316.9 28.2 %attn_bwd.1 = (bf16[8,256,1024]{2,1,0:T(8,128)(2,1)}, bf16[1024,256]{1,0:T(8,128)(2,1)S(1)}, f32[8,128]{1,0:T(8,128)S(1)}) custom-call(s32[4,4]{1,0:T(4,128)S(1)} %copy-done.13, bf16[8,256,128]{2,1,0:T(8,128)(2,1)S(1)} %copy-done.12, bf16[8,256,128]{2,1,0:T(8,128)(2,1)S(1)} %copy-done.18, bf16[8,256,128]{2,1,0:T(8,128)(2,1)S(1)} %copy-done.20, ...), custom_call_target="tpu_custom_call" | custom-call | flops 8000000000 | bytes 16777216 | tf_op jit(solution)/shard_map/attn_bwd/pallas_call | solution.py:606
  346.5 119.2 %final.1 = (f32[256,1024]{1,0:T(8,128)}, bf16[8,32,256]{2,1,0:T(8,128)(2,1)}, bf16[8,32,1152]{2,1,0:T(8,128)(2,1)}, f32[144,1024]{1,0:T(8,128)}, f32[32,1024]{1,0:T(8,128)}, /*index=5*/f32[24,128]{1,0:T(8,128)}) custom-call(bf16[8,256,1024]{2,1,0:T(8,128)(2,1)} %get-tuple-element.66.dh, bf16[256,1024]{1,0:T(8,128)(2,1)} %x.7, ...), custom_call_target="tpu_custom_call" | custom-call | tf_op jit(solution)/shard_map/final/pallas_call | solution.py:721
  465.7 4.2 reshape.141
  470.8 1.3 squeeze.27
  472.8 1.3 squeeze.28
  476.5 1.3 dynamic_slice.30
  478.6 1.0 copy.55
  (93 shorter events, 16.1 us)
Async XLA Ops:
  0.6 8.2 %copy-start = (bf16[32,1024]{1,0:T(8,128)(2,1)S(1)}, bf16[32,1024]{1,0:T(8,128)(2,1)}, u32[]{:S(2)}) copy-start(bf16[32,1024]{1,0:T(8,128)(2,1)} %param.13) | copy-start | bytes 196612
  0.7 4.2 copy-start.24
  5.7 2.9 copy-start.27
  5.7 3.0 copy-start.28
  5.9 3.7 copy-start.30
  6.7 136.7 %copy-start.13 = (s32[4,4]{1,0:T(4,128)S(1)}, s32[4,4]{1,0:T(4,128)}, u32[]{:S(2)}) copy-start(s32[4,4]{1,0:T(4,128)} %len_ref.3) | copy-start | bytes 196
  143.4 19.9 %copy-start.8 = (f32[1,1024]{1,0:T(1,128)}, f32[1,1024]{1,0:T(1,128)S(1)}, u32[]{:S(2)}) copy-start(f32[1,1024]{1,0:T(1,128)S(1)} %get-tuple-element.87.ga_ref.ga) | copy-start | bytes 12292
  143.4 23.8 %copy-start.7 = (f32[1,1024]{1,0:T(1,128)}, f32[1,1024]{1,0:T(1,128)S(1)}, u32[]{:S(2)}) copy-start(f32[1,1024]{1,0:T(1,128)S(1)} %get-tuple-element.86.gf) | copy-start | bytes 12292
  143.4 1.0 copy-start.10
  144.5 22.8 %copy-start.2 = (bf16[4,8,32,1024]{3,2,1,0:T(8,128)(2,1)S(1)}, bf16[4,8,32,1024]{3,2,1,0:T(8,128)(2,1)}, u32[]{:S(2)}) copy-start(bf16[4,8,32,1024]{3,2,1,0:T(8,128)(2,1)} %get-tuple-element.49) | copy-start | bytes 6291460
  144.5 22.8 %copy-start.3 = (bf16[256,1024]{1,0:T(8,128)(2,1)S(1)}, bf16[256,1024]{1,0:T(8,128)(2,1)}, u32[]{:S(2)}) copy-start(bf16[256,1024]{1,0:T(8,128)(2,1)} %x.7) | copy-start | bytes 1572868
  163.3 1.3 copy-start.14
  202.1 39.9 %copy-start.29 = (s32[16]{0:T(128)S(1)}, s32[16]{0:T(128)}, u32[]{:S(2)}) copy-start(s32[16]{0:T(128)} %select_reduce_fusion.1.inv_ref) | copy-start | bytes 196
  248.4 67.4 %copy-start.11 = (bf16[4,8,32,256]{3,2,1,0:T(8,128)(2,1)S(1)}, bf16[4,8,32,256]{3,2,1,0:T(8,128)(2,1)}, u32[]{:S(2)}) copy-start(bf16[4,8,32,256]{3,2,1,0:T(8,128)(2,1)} %get-tuple-element.46) | copy-start | bytes 1572868
  248.4 67.4 %copy-start.16 = (f32[8,256,128]{2,1,0:T(8,128)S(1)}, f32[8,256,128]{2,1,0:T(8,128)}, u32[]{:S(2)}) copy-start(f32[8,256,128]{2,1,0:T(8,128)} %copy-done.15) | copy-start | bytes 3145732
  248.4 67.4 %copy-start.18 = (bf16[8,256,128]{2,1,0:T(8,128)(2,1)S(1)}, bf16[8,256,128]{2,1,0:T(8,128)(2,1)}, u32[]{:S(2)}) copy-start(bf16[8,256,128]{2,1,0:T(8,128)(2,1)} %copy-done.17) | copy-start | bytes 1572868
  248.4 67.4 %copy-start.20 = (bf16[8,256,128]{2,1,0:T(8,128)(2,1)S(1)}, bf16[8,256,128]{2,1,0:T(8,128)(2,1)}, u32[]{:S(2)}) copy-start(bf16[8,256,128]{2,1,0:T(8,128)(2,1)} %copy-done.19) | copy-start | bytes 1572868
  315.9 1.0 copy-start.12
  470.8 3.3 copy-start.25
  472.7 5.0 %copy-start.23 = (bf16[256,1024]{1,0:T(8,128)(2,1)S(1)}, bf16[256,1024]{1,0:T(8,128)(2,1)}, u32[]{:S(2)}) copy-start(bf16[256,1024]{1,0:T(8,128)(2,1)} %get-tuple-element.104) | copy-start | bytes 1572868
  472.7 5.8 %copy-start.21 = (f32[256,1024]{1,0:T(8,128)S(1)}, f32[256,1024]{1,0:T(8,128)}, u32[]{:S(2)}) copy-start(f32[256,1024]{1,0:T(8,128)} %get-tuple-element.105) | copy-start | bytes 3145732
  474.1 5.5 %copy-start.26 = (f32[32,1024]{1,0:T(8,128)S(1)}, f32[32,1024]{1,0:T(8,128)}, u32[]{:S(2)}) copy-start(f32[32,1024]{1,0:T(8,128)} %get-tuple-element.109) | copy-start | bytes 393220
  474.2 6.0 %copy-start.22 = (f32[144,1024]{1,0:T(8,128)S(1)}, f32[144,1024]{1,0:T(8,128)}, u32[]{:S(2)}) copy-start(f32[144,1024]{1,0:T(8,128)} %get-tuple-element.112) | copy-start | bytes 1769476
  475.8 5.2 %copy-start.1 = (bf16[32,1024]{1,0:T(8,128)(2,1)S(1)}, bf16[32,1024]{1,0:T(8,128)(2,1)}, u32[]{:S(2)}) copy-start(bf16[32,1024]{1,0:T(8,128)(2,1)} %param.13) | copy-start | bytes 196612
  (7 other events, 5.7 us)

commit v2 on v1

v2 whole, which is shorter than its diff:
```python
import functools
import math

import jax
import jax.numpy as jnp
from jax import lax
from jax.experimental import pallas as pl
from jax.experimental.pallas import tpu as pltpu
from jax.sharding import PartitionSpec as P

D = 1024
FF = 4608
QUERY_HEADS = 16
KEY_VALUE_HEADS = 8
HEAD = 64
SLOT = 128
GROUP = 8
ROWS = 2048
BLOCK = 256
QKV = 256
WINDOW = 4
EPSILON = 1e-05
ROPE_THETA = 1000000.0
SCALE = 1.0 / math.sqrt(HEAD)
LOG2E = math.log2(math.e)
F32 = jnp.float32
BF16 = jnp.bfloat16
MESH = pl.DeviceIdType.MESH
DMA = pltpu.SemaphoreType.DMA
VM = pl.BlockSpec(memory_space=pltpu.VMEM)
ANY = pl.BlockSpec(memory_space=pl.ANY)
SM = pl.BlockSpec(memory_space=pltpu.SMEM)
SDS = jax.ShapeDtypeStruct


def nn(a, b):
    return lax.dot_general(a, b, (((1,), (0,)), ((), ())), preferred_element_type=F32)


def nt(a, b):
    return lax.dot_general(a, b, (((1,), (1,)), ((), ())), preferred_element_type=F32)


def tn(a, b):
    return lax.dot_general(a, b, (((0,), (0,)), ((), ())), preferred_element_type=F32)


def rcopy(src, dst, send, recv, dev):
    return pltpu.make_async_remote_copy(
        src_ref=src, dst_ref=dst, send_sem=send, recv_sem=recv, device_id=(dev,), device_id_type=MESH
    )


def barrier(peers):
    sem = pltpu.get_barrier_semaphore()
    for q in peers:
        pl.semaphore_signal(sem, inc=1, device_id=(q,), device_id_type=MESH)
    pl.semaphore_wait(sem, len(peers))


def places(n):
    me = lax.axis_index("dp")
    p = lax.rem(me, GROUP)
    g = me // GROUP
    groups = n // GROUP
    zq = [lax.rem(g + s, groups) * GROUP + p for s in range(1, groups)]
    zg = [lax.rem(g + s, groups) for s in range(1, groups)]
    return me, p, g, groups, zq, zg


def start_all(copies):
    for c in copies:
        c.start()
    return copies


def wait_all(copies):
    for c in copies:
        c.wait()


class PlaneGather:
    COPIES = 14

    def __init__(self, me, p, src, dst, ss, rs, ls=None):
        sib, xn, yn = me ^ 1, me ^ 2, me ^ 4

        def cp(a, b, i, dev):
            return rcopy(a, b, ss.at[i], rs.at[i], dev)

        def own(i, dev):
            return [cp(src(h), dst(p, h), i + h, dev) for h in range(2)]

        def on(m, h, i, dev):
            return cp(dst(p ^ m, h), dst(p ^ m, h), i, dev)

        self.x, self.y, self.o = own(0, xn), own(2, yn), own(4, sib)
        self.r = [on(2, 0, 6, yn), on(4, 1, 7, xn)]
        self.fx = [on(2, h, 8 + h, sib) for h in range(2)]
        self.fy = [on(4, h, 10 + h, sib) for h in range(2)]
        self.fd = [on(6, h, 12 + h, sib) for h in range(2)]
        self.local = [] if ls is None else [
            pltpu.make_async_copy(src(h), dst(p, h), ls.at[h]) for h in range(2)
        ]

    def start(self):
        start_all([self.x[0], self.y[1], self.x[1], self.y[0]] + self.o + self.local)

    def relay1(self):
        self.x[0].wait_recv()
        start_all([self.r[0], self.fx[0]])
        self.y[1].wait_recv()
        start_all([self.r[1], self.fy[1]])

    def relay2(self):
        self.x[1].wait_recv()
        self.fx[1].start()
        self.y[0].wait_recv()
        self.fy[0].start()

    def relay3(self):
        for h in range(2):
            self.r[h].wait_recv()
            self.fd[h].start()

    def finish(self):
        wait_all(self.o + self.fx + self.fy + self.fd + self.local)
        for c in self.x + self.y + self.r:
            c.wait_send()


class Ring:
    def __init__(self, n, p, g, src, dst, ss, rs, ls=None):
        groups = n // GROUP
        to = lambda s: lax.rem(g + s, groups) * GROUP + p
        at = lambda s: lax.rem(g + s, groups)

        def cp(a, b, i, dev):
            return rcopy(a, b, ss.at[i], rs.at[i], dev)

        self.relays = []
        if groups == 4:
            self.up = [cp(src(h), dst(g, h), h, to(1)) for h in range(2)]
            self.down = [cp(src(h), dst(g, h), 2 + h, to(3)) for h in range(2)]
            self.first = [self.up[0], self.down[1], self.up[1], self.down[0]]
            below, above = at(3), at(1)
            self.relays = [cp(dst(below, 0), dst(below, 0), 4, to(1)), cp(dst(above, 1), dst(above, 1), 5, to(3))]
        else:
            self.first = [cp(src(None), dst(g, None), s - 1, to(s)) for s in range(1, groups)]
        self.local = [] if ls is None else [pltpu.make_async_copy(src(None), dst(g, None), ls)]

    def start(self):
        start_all(self.first + self.local)

    def relay(self):
        if self.relays:
            self.up[0].wait_recv()
            self.relays[0].start()
            self.down[1].wait_recv()
            self.relays[1].start()

    def finish(self):
        if self.relays:
            self.up[1].wait_recv()
            self.down[0].wait_recv()
            for c in self.first:
                c.wait_send()
        else:
            wait_all(self.first)
        wait_all(self.relays + self.local)


def ring_count(n):
    return max(6, n // GROUP - 1)


def halves(length):
    cut = length // 2
    part = (pl.ds(0, cut), pl.ds(cut, length - cut))
    return lambda h: slice(None) if h is None else part[h]


class RingReduce:
    def __init__(self, n, p, g, part, low, high, send, fin, ss, rs):
        groups = n // GROUP
        to = lambda s: lax.rem(g + s, groups) * GROUP + p
        at = lambda s: lax.rem(g + s, groups)
        hs = halves(part.shape[1])
        self.part, self.fin, self.send, self.g, self.hs = part, fin, send, g, hs

        def cp(a, b, i, dev):
            return rcopy(a, b, ss.at[i], rs.at[i], dev)

        self.ring = groups == 4
        if self.ring:
            self.above, self.below = at(1), at(3)
            self.low, self.high = low, high
            far = at(2)
            self.a = cp(part.at[far, hs(0)], low, 0, to(1))
            self.b = cp(part.at[far, hs(1)], high, 1, to(3))
            self.c = cp(part.at[self.above, hs(1)], fin.at[0, hs(1)], 2, to(1))
            self.d = cp(part.at[self.below, hs(0)], fin.at[1, hs(0)], 3, to(3))
            self.e = cp(send.at[hs(0)], fin.at[0, hs(0)], 4, to(1))
            self.f = cp(send.at[hs(1)], fin.at[1, hs(1)], 5, to(3))
            self.all = [self.a, self.b, self.c, self.d, self.e, self.f]
        else:
            self.all = [cp(part.at[at(s)], fin.at[s - 1], s - 1, to(s)) for s in range(1, groups)]
        self.count = groups - 1

    def start(self):
        start_all(self.all[:4] if self.ring else self.all)

    def relay(self):
        if self.ring:
            for got, buf, h, b, out in (
                (self.a, self.low, 0, self.above, self.e),
                (self.b, self.high, 1, self.below, self.f),
            ):
                got.wait_recv()
                at = self.hs(h)
                self.send[at] = (self.part[b, at].astype(F32) + buf[...].astype(F32)).astype(BF16)
                out.start()

    def finish(self):
        for c in self.all[2:] if self.ring else self.all:
            c.wait_recv()
        val = self.part[self.g].astype(F32)
        for s in range(2 if self.ring else self.count):
            val = val + self.fin[s].astype(F32)
        for c in self.all:
            c.wait_send()
        return val


def ring_scratch(n, shape):
    cut = shape[0] // 2
    groups = n // GROUP
    count = 2 if groups == 4 else groups - 1
    tail = tuple(shape[1:])
    vm = lambda s: pltpu.VMEM(s, BF16)
    return [
        vm((max(cut, 1),) + tail),
        vm((shape[0] - cut,) + tail),
        vm(tuple(shape)),
        vm((count,) + tuple(shape)),
        DMA((ring_count(n),)),
        DMA((ring_count(n),)),
    ]


ORDER = (6, 2, 4, 0)


class PlaneReduce:
    def __init__(self, me, part, sib, send, relay, fx, fy, ss, rs):
        p = lax.rem(me, GROUP)
        xn, yn = me ^ 2, me ^ 4
        hs = halves(sib.shape[1])
        self.hs, self.p, self.part = hs, p, part
        self.sib, self.send, self.relay, self.fx, self.fy = sib, send, relay, fx, fy

        def cp(a, b, i, dev):
            return rcopy(a, b, ss.at[i], rs.at[i], dev)

        self.first = [cp(part(p ^ (m ^ 1)), sib.at[i], i, me ^ 1) for i, m in enumerate(ORDER)]
        self.diag = [cp(send.at[0, hs(0)], relay.at[0], 4, xn), cp(send.at[0, hs(1)], relay.at[1], 5, yn)]
        self.toy = [cp(send.at[2, hs(h)], fy.at[hs(h)], 6 + h, yn) for h in range(2)]
        self.tox = [cp(send.at[1, hs(h)], fx.at[hs(h)], 8 + h, xn) for h in range(2)]

    def start(self):
        start_all(self.first)

    def chip(self, i):
        self.first[i].wait_recv()
        return self.part(self.p ^ ORDER[i])[...].astype(F32) + self.sib[i].astype(F32)

    def phase1(self):
        self.send[0] = self.chip(0).astype(BF16)
        start_all(self.diag)
        self.send[1] = self.chip(1).astype(BF16)
        self.tox[0].start()
        self.send[2] = self.chip(2).astype(BF16)
        self.toy[1].start()

    def phase2(self):
        self.diag[0].wait_recv()
        at = self.hs(0)
        self.send[2, at] = (self.send[2, at].astype(F32) + self.relay[0].astype(F32)).astype(BF16)
        self.toy[0].start()
        self.diag[1].wait_recv()
        at = self.hs(1)
        self.send[1, at] = (self.send[1, at].astype(F32) + self.relay[1].astype(F32)).astype(BF16)
        self.tox[1].start()

    def phase3(self):
        own = self.chip(3)
        for c in self.toy + self.tox:
            c.wait_recv()
        own = own + self.fx[...].astype(F32) + self.fy[...].astype(F32)
        for c in self.first + self.diag + self.toy + self.tox:
            c.wait_send()
        return own


def plane_scratch(shape):
    tail = tuple(shape[1:])
    vm = lambda *s: pltpu.VMEM(s + tail, BF16)
    return [
        vm(4, shape[0]),
        vm(3, shape[0]),
        vm(2, shape[0] // 2),
        vm(shape[0]),
        vm(shape[0]),
        DMA((10,)),
        DMA((10,)),
    ]


def gather_kernel(n, x, a1, a2, wo, wd, gt, xo, a1o, a2o, woo, wdo, gto, ls, xs, xr, ps, pr, zs, zr):
    me, p, g, groups, zq, zg = places(n)
    barrier([me ^ m for m in range(1, GROUP)] + zq)
    local = [
        pltpu.make_async_copy(a1.at[p], a1o.at[g, p], ls.at[0]),
        pltpu.make_async_copy(gt, gto.at[g, p], ls.at[1]),
        pltpu.make_async_copy(a2.at[p], a2o.at[p], ls.at[2]),
    ]
    start_all(local)
    pc = {}

    def exchange(k, src, dst):
        for m in range(1, GROUP):
            pc[k, m] = rcopy(src(p ^ m), dst, ps.at[k, m - 1], pr.at[k, m - 1], me ^ m)
            pc[k, m].start()

    exchange(0, lambda b: a1.at[b], a1o.at[g, p])
    exchange(1, lambda b: gt, gto.at[g, p])
    hx = halves(BLOCK)
    xg = PlaneGather(me, p, lambda h: x.at[hx(h)], lambda b, h: xo.at[b, hx(h)], xs, xr, ls.at[pl.ds(5, 2)])
    xg.start()

    def ring(k, src, dst, local=None):
        hk = halves(dst.shape[1])
        return Ring(n, p, g, lambda h: src.at[hk(h)], lambda b, h: dst.at[b, hk(h)], zs.at[k], zr.at[k], local)

    rings = [
        ring(0, a1o.at[g], a1o),
        ring(1, gto.at[g], gto),
        ring(2, wd, wdo, ls.at[3]),
        ring(3, wo, woo, ls.at[4]),
    ]
    rings[2].start()
    rings[3].start()
    exchange(2, lambda b: a2.at[b], a2o.at[p])
    for k in range(2):
        for m in range(1, GROUP):
            pc[k, m].wait_recv()
        local[k].wait()
        rings[k].start()
    xg.relay1()
    for k in (3, 0, 1, 2):
        rings[k].relay()
    xg.relay2()
    xg.relay3()
    for m in range(1, GROUP):
        pc[2, m].wait_recv()
    local[2].wait()
    for c in pc.values():
        c.wait_send()
    for k in range(4):
        rings[k].finish()
    xg.finish()


def gather_all(n, x, a1, a2, wo, wd, gt):
    groups = n // GROUP
    r = a1.shape[1]
    return pl.pallas_call(
        functools.partial(gather_kernel, n),
        out_shape=(
            SDS((GROUP, BLOCK, D), BF16),
            SDS((groups, GROUP, r, a1.shape[-1]), BF16),
            SDS((GROUP, r, a2.shape[-1]), BF16),
            SDS((groups,) + wo.shape, BF16),
            SDS((groups,) + wd.shape, BF16),
            SDS((groups, GROUP, 8, 128), F32),
        ),
        in_specs=[ANY] * 6,
        out_specs=(ANY,) * 6,
        scratch_shapes=[
            DMA((7,)),
            DMA((14,)),
            DMA((14,)),
            DMA((3, 7)),
            DMA((3, 7)),
            DMA((4, ring_count(n))),
            DMA((4, ring_count(n))),
        ],
        compiler_params=pltpu.CompilerParams(collective_id=1, has_side_effects=True),
        name="gather_all",
    )(x, a1, a2, wo, wd, gt)


def swap_halves(v):
    lane = lax.broadcasted_iota(jnp.int32, v.shape, 1)
    low = lax.rem(lane, HEAD) < HEAD // 2
    width = v.shape[1]
    return jnp.where(low, pltpu.roll(v, width - HEAD // 2, 1), pltpu.roll(v, HEAD // 2, 1))


def head_mean(v):
    lane = lax.broadcasted_iota(jnp.int32, v.shape, 1)
    low = lane < HEAD
    a = jnp.sum(jnp.where(low, v, 0.0), axis=-1, keepdims=True)
    b = jnp.sum(jnp.where(low, 0.0, v), axis=-1, keepdims=True)
    return jnp.where(low, a, b) * (1.0 / HEAD)


def seq_start(row, len_ref, g):
    e1 = len_ref[g, 0]
    e2 = e1 + len_ref[g, 1]
    e3 = e2 + len_ref[g, 2]
    zero = row * 0
    s = jnp.where(row >= e1, zero + e1, zero)
    s = jnp.where(row >= e2, zero + e2, s)
    return jnp.where(row >= e3, zero + e3, s)


def tables(cs_ref):
    t = cs_ref[...].T
    c, s = t[:, : HEAD // 2], t[:, HEAD // 2 :]
    return jnp.concatenate([c, c, c, c], axis=1), jnp.concatenate([-s, s, -s, s], axis=1)


def attn_fwd_kernel(n, len_ref, x_ref, w_ref, ga_ref, gqk_ref, cs_ref, dy, w2, wo, h_ref, raw_ref, q_ref, kv_ref, mix_ref, mixf_ref, lse_ref, dyo, w2o, woo, k_s, v_s, acc, ls, ds_, dr, os_, orr, zs, zr):
    i = pl.program_id(0)
    me, p, g, groups, zq, zg = places(n)
    hd, hw, ho = halves(BLOCK), halves(w2.shape[0]), halves(wo.shape[0])
    dg = PlaneGather(me, p, lambda h: dy.at[hd(h)], lambda b, h: dyo.at[b, hd(h)], ds_, dr, ls.at[pl.ds(0, 2)])
    og = PlaneGather(me, p, lambda h: wo.at[ho(h)], lambda b, h: woo.at[ho(h), b], os_, orr, ls.at[pl.ds(2, 2)])
    zg_ = Ring(n, p, g, lambda h: w2.at[hw(h)], lambda b, h: w2o.at[b, hw(h)], zs, zr, ls.at[4])

    @pl.when(i == 0)
    def _():
        barrier([me ^ m for m in (1, 2, 4)] + zq)
        dg.start()
        zg_.start()
        og.start()

    @pl.when(i == 3)
    def _():
        dg.relay1()

    @pl.when(i == 5)
    def _():
        zg_.relay()
        dg.relay2()

    @pl.when(i == 6)
    def _():
        og.relay1()
        dg.relay3()

    @pl.when(i == 7)
    def _():
        og.relay2()

    xb = x_ref[0].astype(F32)
    r = lax.rsqrt(jnp.mean(xb * xb, axis=-1, keepdims=True) + EPSILON)
    h = (xb * r * ga_ref[...]).astype(BF16)
    h_ref[0] = h
    raw = nn(h, w_ref[...])
    raw_ref[0] = raw
    ct, st = tables(cs_ref)
    qraw, kvraw = raw[:, :128], raw[:, 128:]
    qn = qraw * lax.rsqrt(head_mean(qraw * qraw) + EPSILON) * gqk_ref[0:1, :]
    q = (qn * ct + swap_halves(qn) * st).astype(BF16)
    kn = kvraw * lax.rsqrt(head_mean(kvraw * kvraw) + EPSILON) * gqk_ref[1:2, :]
    k = (kn * ct + swap_halves(kn) * st).astype(BF16)
    lane = lax.broadcasted_iota(jnp.int32, (BLOCK, 128), 1)
    kv = jnp.where(lane < HEAD, k.astype(F32), kvraw).astype(BF16)
    q_ref[0] = q
    kv_ref[0] = kv
    k_s[pl.ds(i * BLOCK, BLOCK), :] = kv[:, :HEAD]
    v_s[pl.ds(i * BLOCK, BLOCK), :] = jnp.where(lane < HEAD, pltpu.roll(kvraw, HEAD, 1), 1.0).astype(BF16)
    q2 = jnp.concatenate([q[:, :HEAD], q[:, HEAD:]], axis=0)
    acc[...] = jnp.zeros_like(acc)
    row = lax.broadcasted_iota(jnp.int32, (2 * BLOCK, 1), 0)
    qrow = i * BLOCK + jnp.where(row >= BLOCK, row - BLOCK, row)
    qstart = seq_start(qrow, len_ref, g)
    first = jnp.maximum(i - WINDOW, 0)
    col = lax.broadcasted_iota(jnp.int32, (2 * BLOCK, BLOCK), 1)

    def step(j, carry):
        kb = k_s[pl.ds(pl.multiple_of(j * BLOCK, BLOCK), BLOCK), :]
        vb = v_s[pl.ds(pl.multiple_of(j * BLOCK, BLOCK), BLOCK), :]
        s = nt(q2, kb)
        kc = col + j * BLOCK
        ok = (kc >= qstart) & (kc <= qrow)
        e = jnp.where(ok, jnp.exp2(s * (SCALE * LOG2E)), 0.0).astype(BF16)
        acc[...] += nn(e, vb)
        return carry

    lax.fori_loop(first, i + 1, step, 0)
    total = acc[:, HEAD:]
    m = acc[:, :HEAD] / total
    both = jnp.concatenate([m[:BLOCK], m[BLOCK:]], axis=1)
    mixf_ref[0] = both
    mix_ref[0] = both.astype(BF16)
    lse_ref[0] = jnp.log2(total.T)[:8, :]

    @pl.when(i == 7)
    def _():
        og.relay3()
        dg.finish()
        zg_.finish()
        og.finish()


def attn_fwd(n, lengths, x_all, wqkv, ga, gqk, cs, dy, w2, wo):
    groups = n // GROUP
    blk = lambda c: pl.BlockSpec((1, BLOCK, c), lambda i: (i, 0, 0))
    whole = lambda s: pl.BlockSpec(s, lambda i: (0,) * len(s), pipeline_mode=pl.Buffered(1))
    nb = ROWS // BLOCK
    return pl.pallas_call(
        functools.partial(attn_fwd_kernel, n),
        grid=(nb,),
        in_specs=[
            SM,
            blk(D),
            whole((D, QKV)),
            whole((1, D)),
            whole((2, 128)),
            pl.BlockSpec((HEAD, BLOCK), lambda i: (0, i)),
            ANY,
            ANY,
            ANY,
        ],
        out_specs=(blk(D), blk(QKV), blk(128), blk(128), blk(128), blk(128), pl.BlockSpec((1, 8, 2 * BLOCK), lambda i: (i, 0, 0)), ANY, ANY, ANY),
        out_shape=(
            SDS((nb, BLOCK, D), BF16),
            SDS((nb, BLOCK, QKV), F32),
            SDS((nb, BLOCK, 128), BF16),
            SDS((nb, BLOCK, 128), BF16),
            SDS((nb, BLOCK, 128), BF16),
            SDS((nb, BLOCK, 128), F32),
            SDS((nb, 8, 2 * BLOCK), F32),
            SDS((GROUP, BLOCK, D), BF16),
            SDS((groups,) + w2.shape, BF16),
            SDS((groups, GROUP) + wo.shape[1:], BF16),
        ),
        scratch_shapes=[
            pltpu.VMEM((ROWS, HEAD), BF16),
            pltpu.VMEM((ROWS, 128), BF16),
            pltpu.VMEM((2 * BLOCK, 128), F32),
            DMA((5,)),
            DMA((14,)),
            DMA((14,)),
            DMA((14,)),
            DMA((14,)),
            DMA((ring_count(n),)),
            DMA((ring_count(n),)),
        ],
        compiler_params=pltpu.CompilerParams(
            collective_id=5, has_side_effects=True, dimension_semantics=("arbitrary",), vmem_limit_bytes=48 << 20
        ),
        cost_estimate=pl.CostEstimate(flops=4 * 10**9, bytes_accessed=16 << 20, transcendentals=4 * 10**6),
        name="attn_fwd",
    )(lengths, x_all, wqkv, ga, gqk, cs, dy, w2, wo)


def mid_kernel(n, mix, x, wo, gf, res, mown, h2, h2all, mbuf, ps, pr, hs, hr, ls):
    me, p, g, groups, zq, zg = places(n)
    barrier([me ^ m for m in range(1, GROUP)])
    pc = start_all(
        [rcopy(mix.at[p ^ m], mbuf.at[p], ps.at[m - 1], pr.at[m - 1], me ^ m) for m in range(1, GROUP)]
    )
    mbuf[p] = mix[p]
    for c in pc:
        c.wait_recv()
    m = jnp.concatenate([mbuf[b] for b in range(GROUP)], axis=1)
    mown[...] = m
    z = x[...].astype(F32) + nn(m, wo[...])
    res[...] = z
    r = lax.rsqrt(jnp.mean(z * z, axis=-1, keepdims=True) + EPSILON)
    h2[...] = (z * r * gf[...]).astype(BF16)
    hb = halves(BLOCK)
    hg = PlaneGather(me, p, lambda h: h2.at[hb(h)], lambda b, h: h2all.at[b, hb(h)], hs, hr, ls)
    hg.start()
    hg.relay1()
    hg.relay2()
    hg.relay3()
    hg.finish()
    for c in pc:
        c.wait_send()


def mid(n, mix, x, wo, gf):
    return pl.pallas_call(
        functools.partial(mid_kernel, n),
        out_shape=(SDS((BLOCK, D), F32), SDS((BLOCK, D), BF16), SDS((BLOCK, D), BF16), SDS((GROUP, BLOCK, D), BF16)),
        in_specs=[VM] * 4,
        out_specs=(VM, VM, VM, ANY),
        scratch_shapes=[
            pltpu.VMEM((GROUP, BLOCK, 128), BF16),
            DMA((7,)),
            DMA((7,)),
            DMA((14,)),
            DMA((14,)),
            DMA((2,)),
        ],
        compiler_params=pltpu.CompilerParams(collective_id=2, has_side_effects=True, vmem_limit_bytes=48 << 20),
        name="mid",
    )(mix, x, wo, gf)


def ffn_kernel(inv_ref, h_ref, da_ref, db_ref, wgu_ref, wd_ref, po_ref, dh_ref, dwgu_ref, dwd_ref, agu, ad):
    i = pl.program_id(0)
    fl = wd_ref.shape[0]

    @pl.when(i == 0)
    def _():
        agu[...] = jnp.zeros_like(agu)
        ad[...] = jnp.zeros_like(ad)

    h = h_ref[0]
    dy = jnp.concatenate([da_ref[0], db_ref[0]], axis=0)
    gp = nn(h, wgu_ref[:, :fl])
    up = nn(h, wgu_ref[:, fl:])
    sig = 1.0 / (1.0 + jnp.exp(-gp))
    sg = gp * sig
    act = (sg * up).astype(BF16)
    po_ref[0] = nn(act, wd_ref[...]).astype(BF16)
    da = nt(dy, wd_ref[...])
    dg = (da * up * (sig * (1.0 + gp * (1.0 - sig)))).astype(BF16)
    du = (da * sg).astype(BF16)
    dh_ref[0] = (nt(dg, wgu_ref[:, :fl]) + nt(du, wgu_ref[:, fl:])).astype(BF16)
    ad[...] += tn(act, dy)
    agu[:, :fl] += tn(h, dg)
    agu[:, fl:] += tn(h, du)

    @pl.when(i == pl.num_programs(0) - 1)
    def _():
        dwgu_ref[...] = agu[...].astype(BF16)
        dwd_ref[...] = ad[...].astype(BF16)


def ffn(inv, h2all, dyall, wgu, wd):
    nb = ROWS // BLOCK
    fl = wd.shape[0]
    blk = pl.BlockSpec((1, BLOCK, D), lambda i, inv: (i, 0, 0))
    one = pl.Buffered(1)
    slots = dyall.reshape(ROWS // SLOT, SLOT, D)
    return pl.pallas_call(
        ffn_kernel,
        grid_spec=pltpu.PrefetchScalarGridSpec(
            num_scalar_prefetch=1,
            grid=(nb,),
            in_specs=[
                blk,
                pl.BlockSpec((1, SLOT, D), lambda i, inv: (inv[2 * i], 0, 0)),
                pl.BlockSpec((1, SLOT, D), lambda i, inv: (inv[2 * i + 1], 0, 0)),
                pl.BlockSpec((D, 2 * fl), lambda i, inv: (0, 0), pipeline_mode=one),
                pl.BlockSpec((fl, D), lambda i, inv: (0, 0), pipeline_mode=one),
            ],
            out_specs=(
                blk,
                blk,
                pl.BlockSpec((D, 2 * fl), lambda i, inv: (0, 0), pipeline_mode=one),
                pl.BlockSpec((fl, D), lambda i, inv: (0, 0), pipeline_mode=one),
            ),
            scratch_shapes=[pltpu.VMEM((D, 2 * fl), F32), pltpu.VMEM((fl, D), F32)],
        ),
        out_shape=(
            SDS((nb, BLOCK, D), BF16),
            SDS((nb, BLOCK, D), BF16),
            SDS((D, 2 * fl), BF16),
            SDS((fl, D), BF16),
        ),
        compiler_params=pltpu.CompilerParams(dimension_semantics=("arbitrary",), vmem_limit_bytes=56 << 20),
        cost_estimate=pl.CostEstimate(flops=24 * 10**9, bytes_accessed=24 << 20, transcendentals=10**6),
        name="ffn",
    )(inv, h2all, slots, slots, wgu, wd)


def norm_back(dyv, xv, gain):
    r = lax.rsqrt(jnp.mean(xv * xv, axis=-1, keepdims=True) + EPSILON)
    xr = xv * r
    gy = dyv * gain
    dx = r * (gy - xr * jnp.mean(gy * xr, axis=-1, keepdims=True))
    return dx, jnp.sum(dyv * xr, axis=0, keepdims=True)


def back_mid_kernel(n, dh, dyo, res, mown, wo, gf, gmid, dgf, dwo, dmh, sib, send, rel, fx, fy, ss, rs, dmix, ps, pr):
    me, p, g, groups, zq, zg = places(n)
    barrier([me ^ m for m in range(1, GROUP)])
    red = PlaneReduce(me, lambda b: dh.at[b], sib, send, rel, fx, fy, ss, rs)
    red.start()
    red.phase1()
    red.phase2()
    dx, dgain = norm_back(red.phase3(), res[...], gf[...])
    gm = dyo[...].astype(F32) + dx
    gmid[...] = gm
    dgf[...] = dgain
    gl = gm.astype(BF16)
    dm = nt(gl, wo[...]).astype(BF16)
    for b in range(GROUP):
        dmix[b] = dm[:, 128 * b : 128 * (b + 1)]
    pc = start_all(
        [rcopy(dmix.at[p ^ m], dmh.at[p], ps.at[m - 1], pr.at[m - 1], me ^ m) for m in range(1, GROUP)]
    )
    dmh[p] = dmix[p]
    dwo[...] = tn(mown[...], gl).astype(BF16)
    wait_all(pc)


def back_mid(n, dh, dyo, res, mown, wo, gf):
    return pl.pallas_call(
        functools.partial(back_mid_kernel, n),
        out_shape=(
            SDS((BLOCK, D), F32),
            SDS((1, D), F32),
            SDS((D, D), BF16),
            SDS((GROUP, BLOCK, 128), BF16),
        ),
        in_specs=[VM] * 6,
        out_specs=(VM,) * 4,
        scratch_shapes=plane_scratch((BLOCK, D))
        + [
            pltpu.VMEM((GROUP, BLOCK, 128), BF16),
            DMA((7,)),
            DMA((7,)),
        ],
        compiler_params=pltpu.CompilerParams(collective_id=3, has_side_effects=True, vmem_limit_bytes=58 << 20),
        name="back_mid",
    )(dh, dyo, res, mown, wo, gf)


def attn_bwd_kernel(n, len_ref, dm_ref, q_ref, kvall_ref, lse_ref, mixf_ref, h_ref, raw_ref, w_ref, gqk_ref, cs_ref, po, res, dwo, dw2, dwd, dh_ref, dw_ref, dg_ref, result, two, t2, od, k_s, v_s, dkv, dqt, dws, *rest):
    step_id = pl.program_id(0)
    nb = ROWS // BLOCK
    i = nb - 1 - step_id
    me, p, g, groups, zq, zg = places(n)
    ored = PlaneReduce(me, lambda b: po.at[b], *rest[:7])
    wred = PlaneReduce(me, lambda b: dwo.at[:, b], *rest[7:14])
    ring2 = RingReduce(n, p, g, dw2, *rest[14:20])
    ringd = RingReduce(n, p, g, dwd, *rest[20:26])

    @pl.when(step_id == 0)
    def _():
        barrier([me ^ m for m in (1, 2, 4)] + zq)
        ored.start()
        ring2.start()
        wred.start()
        ringd.start()

    @pl.when(step_id == 1)
    def _():
        ored.phase1()
        wred.phase1()

    @pl.when(step_id == 3)
    def _():
        ring2.relay()
        ored.phase2()

    @pl.when(step_id == 4)
    def _():
        ringd.relay()
        wred.phase2()


    @pl.when(step_id == 0)
    def _():
        dkv[...] = jnp.zeros_like(dkv)
        dws[...] = jnp.zeros_like(dws)
        dg_ref[...] = jnp.zeros_like(dg_ref)
        for b in range(ROWS // BLOCK):
            kvb = kvall_ref[b]
            k_s[pl.ds(b * BLOCK, BLOCK), :] = kvb[:, :HEAD]
            v_s[pl.ds(b * BLOCK, BLOCK), :] = kvb[:, HEAD:]

    q, do, mf = q_ref[0], dm_ref[0], mixf_ref[0]
    q2 = jnp.concatenate([q[:, :HEAD], q[:, HEAD:]], axis=0)
    do2 = jnp.concatenate([do[:, :HEAD], do[:, HEAD:]], axis=0)
    prod = (do.astype(F32) * mf).T
    delta = jnp.concatenate(
        [jnp.sum(prod[:HEAD], axis=0, keepdims=True), jnp.sum(prod[HEAD:], axis=0, keepdims=True)], axis=1
    )
    lse = lse_ref[0, 0:1, :]
    colq = lax.broadcasted_iota(jnp.int32, (1, 2 * BLOCK), 1)
    qrow = i * BLOCK + jnp.where(colq >= BLOCK, colq - BLOCK, colq)
    qstart = seq_start(qrow, len_ref, g)
    first = jnp.maximum(i - WINDOW, 0)
    rowk = lax.broadcasted_iota(jnp.int32, (BLOCK, 2 * BLOCK), 0)
    dqt[...] = jnp.zeros_like(dqt)

    def step(j, carry):
        at = pl.ds(pl.multiple_of(j * BLOCK, BLOCK), BLOCK)
        kb, vb = k_s[at, :], v_s[at, :]
        s = nt(kb, q2)
        kc = rowk + j * BLOCK
        ok = (kc >= qstart) & (kc <= qrow)
        pr = jnp.where(ok, jnp.exp2(s * (SCALE * LOG2E) - lse), 0.0)
        dp = nt(vb, do2)
        dsc = (pr * (dp - delta)).astype(BF16)
        dkv[at, :HEAD] += nn(dsc, q2)
        dkv[at, HEAD:] += nn(pr.astype(BF16), do2)
        dqt[...] += tn(dsc, kb)
        return carry

    lax.fori_loop(first, i + 1, step, 0)
    ct, st = tables(cs_ref)
    raw = raw_ref[0]
    dq = jnp.concatenate([dqt[:BLOCK], dqt[BLOCK:]], axis=1) * SCALE
    dkvb = dkv[pl.ds(pl.multiple_of(i * BLOCK, BLOCK), BLOCK), :]
    lane = lax.broadcasted_iota(jnp.int32, (BLOCK, 128), 1)

    def pull(d, v, gain):
        dn = d * ct - swap_halves(d) * st
        r = lax.rsqrt(head_mean(v * v) + EPSILON)
        vr = v * r
        gy = dn * gain
        return r * (gy - vr * head_mean(gy * vr)), jnp.sum(dn * vr, axis=0, keepdims=True)

    dqr, dgq = pull(dq, raw[:, :128], gqk_ref[0:1, :])
    dkr, dgk = pull(dkvb * SCALE, raw[:, 128:], gqk_ref[1:2, :])
    dg_ref[0:1, :] += dgq
    dg_ref[1:2, :] += dgk
    dqkv = jnp.concatenate([dqr, jnp.where(lane < HEAD, dkr, dkvb)], axis=1).astype(BF16)
    dh_ref[0] = nt(dqkv, w_ref[...]).astype(BF16)
    dws[...] += tn(h_ref[0], dqkv)

    @pl.when(step_id == nb - 1)
    def _():
        dw_ref[...] = dws[...].astype(BF16)
        result[...] = (ored.phase3() + res[...]).astype(BF16)
        two[...] = wred.phase3().astype(BF16)
        t2[...] = ring2.finish().astype(BF16)
        od[...] = ringd.finish()


def attn_bwd(n, lengths, dmh, q, kv, lse, mixf, h, raw, wqkv, gqk, cs, po, res, dwo, dw2, dwd):
    nb = ROWS // BLOCK
    groups = n // GROUP
    blk = lambda c: pl.BlockSpec((1, BLOCK, c), lambda i: (nb - 1 - i, 0, 0))
    whole = lambda s: pl.BlockSpec(s, lambda i: (0,) * len(s), pipeline_mode=pl.Buffered(1))
    return pl.pallas_call(
        functools.partial(attn_bwd_kernel, n),
        grid=(nb,),
        in_specs=[
            SM,
            blk(128),
            blk(128),
            whole((nb, BLOCK, 128)),
            pl.BlockSpec((1, 8, 2 * BLOCK), lambda i: (nb - 1 - i, 0, 0)),
            blk(128),
            blk(D),
            blk(QKV),
            whole((D, QKV)),
            whole((2, 128)),
            pl.BlockSpec((HEAD, BLOCK), lambda i: (0, nb - 1 - i)),
            whole(po.shape),
            whole(res.shape),
            whole(dwo.shape),
            whole(dw2.shape),
            whole(dwd.shape),
        ],
        out_specs=(
            blk(D),
            whole((D, QKV)),
            whole((8, 128)),
            whole((BLOCK, D)),
            whole((groups,) + dwo.shape[2:]),
            whole(dw2.shape[1:]),
            whole(dwd.shape[1:]),
        ),
        out_shape=(
            SDS((nb, BLOCK, D), BF16),
            SDS((D, QKV), BF16),
            SDS((8, 128), F32),
            SDS((BLOCK, D), BF16),
            SDS((groups,) + dwo.shape[2:], BF16),
            SDS(dw2.shape[1:], BF16),
            SDS(dwd.shape[1:], F32),
        ),
        scratch_shapes=[
            pltpu.VMEM((ROWS, HEAD), BF16),
            pltpu.VMEM((ROWS, HEAD), BF16),
            pltpu.VMEM((ROWS, 128), F32),
            pltpu.VMEM((2 * BLOCK, HEAD), F32),
            pltpu.VMEM((D, QKV), F32),
        ]
        + plane_scratch((BLOCK, D))
        + plane_scratch((groups,) + dwo.shape[2:])
        + ring_scratch(n, dw2.shape[1:])
        + ring_scratch(n, dwd.shape[1:]),
        compiler_params=pltpu.CompilerParams(
            collective_id=6, has_side_effects=True, dimension_semantics=("arbitrary",), vmem_limit_bytes=60 << 20
        ),
        cost_estimate=pl.CostEstimate(flops=8 * 10**9, bytes_accessed=16 << 20, transcendentals=4 * 10**6),
        name="attn_bwd",
    )(lengths, dmh, q, kv, lse, mixf, h, raw, wqkv, gqk, cs, po, res, dwo, dw2, dwd)


def final_kernel(n, dh, x, gmid, ga, dgf, dgqk, dw1, two, t2, gtok, o1, o2, oo, og, t1, gpart, gin, gsum, gz, ps, pr, gs, gr, *rest):
    me, p, g, groups, zq, zg = places(n)
    nz = groups - 1
    barrier([me ^ m for m in range(1, GROUP)] + zq)
    red = PlaneReduce(me, lambda b: dh.at[b], *rest[:7])
    ring1 = RingReduce(n, p, g, dw1, *rest[7:13])
    ringo = RingReduce(n, p, g, two, *rest[13:19])
    red.start()
    ring1.start()
    ringo.start()
    pc = []

    def exchange(k, src, out):
        for m in range(1, GROUP):
            c = rcopy(src.at[p ^ m], out.at[p], ps.at[k, m - 1], pr.at[k, m - 1], me ^ m)
            c.start()
            pc.append(c)
        out[p] = src[p]

    red.phase1()
    exchange(1, t2, o2)
    ring1.relay()
    ringo.relay()
    red.phase2()
    t1[...] = ring1.finish().astype(BF16)
    exchange(0, t1, o1)
    dx, dga = norm_back(red.phase3(), x[...].astype(F32), ga[...])
    gtok[...] = gmid[...] + dx
    gpart[...] = jnp.zeros_like(gpart)
    for b in range(8):
        gpart[b : b + 1, :] = dga[:, 128 * b : 128 * (b + 1)]
        gpart[8 + b : 9 + b, :] = dgf[:, 128 * b : 128 * (b + 1)]
    lane = lax.broadcasted_iota(jnp.int32, (1, 128), 1)
    dgq = dgqk[0:1, :]
    dgq = dgq + pltpu.roll(jnp.broadcast_to(dgq, (8, 128)), HEAD, 1)[0:1, :]
    dgk = pltpu.roll(jnp.broadcast_to(dgqk[1:2, :], (8, 128)), HEAD, 1)[0:1, :]
    gpart[16:17, :] = jnp.where(lane < HEAD, dgq, dgk)
    gc = start_all([rcopy(gpart, gin.at[m - 1], gs.at[m - 1], gr.at[m - 1], me ^ m) for m in range(1, GROUP)])
    oo[...] = ringo.finish()
    tot = gpart[...]
    for m in range(1, GROUP):
        gc[m - 1].wait_recv()
        tot = tot + gin[m - 1]
    gsum[...] = tot
    gzc = start_all([rcopy(gsum, gz.at[s], gs.at[7 + s], gr.at[7 + s], zq[s]) for s in range(nz)])
    for s in range(nz):
        gzc[s].wait_recv()
        tot = tot + gz[s]
    og[...] = tot
    wait_all(pc)
    for c in gc + gzc:
        c.wait_send()


def final(n, dh, x, gmid, ga, dgf, dgqk, dw1, two, t2):
    groups = n // GROUP
    nz = groups - 1
    return pl.pallas_call(
        functools.partial(final_kernel, n),
        out_shape=(
            SDS((BLOCK, D), F32),
            SDS(dw1.shape[1:], BF16),
            SDS(t2.shape, BF16),
            SDS(two.shape[1:], F32),
            SDS((24, 128), F32),
        ),
        in_specs=[VM] * 9,
        out_specs=(VM,) * 5,
        scratch_shapes=[
            pltpu.VMEM(dw1.shape[1:], BF16),
            pltpu.VMEM((24, 128), F32),
            pltpu.VMEM((7, 24, 128), F32),
            pltpu.VMEM((24, 128), F32),
            pltpu.VMEM((nz, 24, 128), F32),
            DMA((2, 7)),
            DMA((2, 7)),
            DMA((7 + nz,)),
            DMA((7 + nz,)),
        ]
        + plane_scratch((BLOCK, D))
        + ring_scratch(n, dw1.shape[1:])
        + ring_scratch(n, two.shape[1:]),
        compiler_params=pltpu.CompilerParams(collective_id=4, has_side_effects=True, vmem_limit_bytes=58 << 20),
        name="final",
    )(dh, x, gmid, ga, dgf, dgqk, dw1, two, t2)


def body(n, tokens, w_query, key_weight, w_value, w_out, w_gate, w_up, w_down, norm_gains, seq_lengths, slot_order, out_grad):
    groups = n // GROUP
    r = w_query.shape[0]
    ffc = w_down.shape[0]
    device = lax.axis_index("dp")
    g, p = device // GROUP, device % GROUP
    lengths = seq_lengths
    a1 = jnp.concatenate(
        [
            w_query.reshape(r, GROUP, 128),
            key_weight.reshape(r, GROUP, HEAD),
            w_value.reshape(r, GROUP, HEAD),
        ],
        axis=2,
    ).transpose(1, 0, 2)
    wgu = jnp.stack([w_gate, w_up], axis=1).reshape(r, 2, groups, GROUP, ffc)
    a2 = wgu.transpose(3, 0, 1, 2, 4).reshape(GROUP, r, 2 * groups * ffc)
    share = norm_gains.shape[0]
    gt = jnp.pad(norm_gains.astype(F32)[None, :], ((0, 7), (0, 128 - share)))
    wok = r // 16 if r % 16 == 0 else 1
    wdk = ffc // 16 if ffc % 16 == 0 else 1
    x_all, w1, w2, wo, wd, gains = gather_all(
        n, tokens, a1, a2, w_out.reshape(wok, r // wok, D), w_down.reshape(wdk, ffc // wdk, D), gt
    )
    gains = gains[:, :, 0, :share].reshape(1, -1)
    ga, gf = gains[:, :D], gains[:, D : 2 * D]
    gq = gains[:, 2 * D : 2 * D + HEAD]
    gk = gains[:, 2 * D + HEAD :]
    gqk = jnp.concatenate([jnp.concatenate([gq, gq], axis=1), jnp.concatenate([gk, gk], axis=1)], axis=0)
    wqkv = w1.reshape(D, QKV)
    wd = wd.reshape(-1, D)
    row = jnp.arange(ROWS, dtype=jnp.int32)
    length_row = lax.dynamic_index_in_dim(seq_lengths, g, 0, keepdims=False)
    order_row = lax.dynamic_index_in_dim(slot_order, g, 0, keepdims=False)
    ends = jnp.cumsum(length_row)
    start = jnp.max(jnp.where(row[:, None] >= ends[None, :], ends[None, :], 0), axis=1)
    frequency = jnp.exp(jnp.arange(HEAD // 2, dtype=F32) * (-2.0 * math.log(ROPE_THETA) / HEAD))
    angles = frequency[:, None] * (row - start).astype(F32)[None, :]
    cs = jnp.concatenate([jnp.cos(angles), jnp.sin(angles)], axis=0)
    slots = jnp.arange(ROWS // SLOT, dtype=jnp.int32)
    inv = jnp.sum(jnp.where(order_row[None, :] == slots[:, None], slots[None, :], 0), axis=1)

    h, raw, q, kv, mix, mixf, lse, dy_all, w2, wo = attn_fwd(
        n, lengths, x_all, wqkv, ga, gqk, cs, out_grad, w2, wo.reshape(groups, r, D)
    )
    wgu = w2.reshape(D, -1)
    wo = wo.reshape(D, D)
    res, mown, _, h2_all = mid(n, mix, tokens, wo, gf)
    po, dh2, dwgu, dwd = ffn(inv, h2_all, dy_all, wgu, wd)
    dslots = dy_all.reshape(ROWS // SLOT, SLOT, D)
    dy_own = jnp.concatenate(
        [lax.dynamic_index_in_dim(dslots, inv[2 * p + k], 0, keepdims=False) for k in range(2)], axis=0
    )
    gmid, dgf, dwo, dmh = back_mid(n, dh2, dy_own, res, mown, wo, gf)
    dh1, dwqkv, dgqk, result, two, t2, od = attn_bwd(
        n,
        lengths,
        dmh,
        q,
        kv,
        lse,
        mixf,
        h,
        raw,
        wqkv,
        gqk,
        cs,
        po,
        res,
        dwo.reshape(groups, GROUP, r, D),
        dwgu.reshape(groups, GROUP, r, -1),
        dwd.reshape(groups, wdk, ffc // wdk, D),
    )
    gtok, o1, o2, oo, og = final(
        n,
        dh1,
        tokens,
        gmid,
        ga,
        dgf,
        dgqk,
        dwqkv.reshape(groups, GROUP, r, QKV),
        two.reshape(groups, wok, r // wok, D),
        t2,
    )
    oo = oo.reshape(r, D)
    od = od.reshape(ffc, D)
    o1 = o1.transpose(1, 0, 2).astype(F32)
    gwq = o1[:, :, :128].reshape(r, -1)
    gwk = o1[:, :, 128 : 128 + HEAD].reshape(r, -1)
    gwv = o1[:, :, 128 + HEAD :].reshape(r, -1)
    o2 = o2.reshape(GROUP, r, 2, groups, ffc).transpose(2, 1, 3, 0, 4).reshape(2, r, -1).astype(F32)
    gains_out = lax.dynamic_slice(og.reshape(-1), (device * share,), (share,))
    return result, gtok, gwq, gwk, gwv, oo, o2[0], o2[1], od, gains_out


def solution(mesh):
    n = mesh.shape["dp"]
    row = P("dp", None)
    return jax.shard_map(
        functools.partial(body, n),
        mesh=mesh,
        in_specs=(row,) * 8 + (P("dp"), P(), P(), row),
        out_specs=(row,) * 9 + (P("dp"),),
        check_vma=False,
    )
```

time: 480 us -> 353 us (0.74)
  Pallas kernels: 437 us -> 307 us
    pallas_call x1, Pallas kernels: 132 us -> 41.7 us  [gather_all(): pl.pallas_call(functools.partial(gather_kernel, n), out_shape=(SDS((GROUP...]
    pallas_call x1, Pallas kernels: 119 us -> 43.1 us  [final(): pl.pallas_call(functools.partial(final_kernel, n), out_shape=(SDS((BLOCK,...]
    pallas_call x2, Pallas kernels: 47 us -> 114 us  [the longest x1 69.6 us: attn_bwd(): pl.pallas_call(functools.partial(attn_bwd_kernel, n), grid=(nb,), in_spec...]
    pallas_call x1, Pallas kernels: 67.4 us -> 36.8 us  [back_mid(): pl.pallas_call(functools.partial(back_mid_kernel, n), out_shape=(SDS((BLO...]
    unnamed x66 -> x58, local copies, waits for them, and re-layouts: 12.4 us -> 13.1 us
where the time goes in v2:
time: 353 us
  Pallas kernels  307 us (87%)
  local copies, waits for them, and re-layouts  34.1 us (10%)
  other arithmetic  5.93 us (2%)
  between operations  4.99 us (1%)
    pallas_call x1, Pallas kernels, attn_bwd(): pl.pallas_call(functools.partial(attn_bwd_kernel, n), grid=(nb,), in_spec...  69.6 us
    pallas_call x1, Pallas kernels, attn_fwd(): pl.pallas_call(functools.partial(attn_fwd_kernel, n), grid=(nb,), in_spec...  44.2 us
    pallas_call x1, Pallas kernels, final(): pl.pallas_call(functools.partial(final_kernel, n), out_shape=(SDS((BLOCK,...  43.1 us
    pallas_call x1, Pallas kernels, gather_all(): pl.pallas_call(functools.partial(gather_kernel, n), out_shape=(SDS((GROUP...  41.7 us
    pallas_call x1, Pallas kernels, ffn(): pl.pallas_call(ffn_kernel, grid_spec=pltpu.PrefetchScalarGridSpec(num_sca...  39.9 us
    pallas_call x1, Pallas kernels, back_mid(): pl.pallas_call(functools.partial(back_mid_kernel, n), out_shape=(SDS((BLO...  36.8 us
    pallas_call x1, Pallas kernels, mid(): pl.pallas_call(functools.partial(mid_kernel, n), out_shape=(SDS((BLOCK, D...  32.1 us
    unnamed x58, local copies, waits for them, and re-layouts  13.1 us

profile of v2, /device:TPU:0, one launch (start us, length us, event | category | flops | bytes accessed | tf_op | source)
XLA Modules:
  0.0 352.5 jit_solution(10859923306872847480)
XLA Ops:
  4.6 1.8 stack.10
  8.5 1.8 reshape.143.a2
  11.0 41.7 %gather_all.1 = (bf16[8,256,1024]{2,1,0:T(8,128)(2,1)}, bf16[4,8,32,256]{3,2,1,0:T(8,128)(2,1)}, bf16[8,32,1152]{2,1,0:T(8,128)(2,1)}, bf16[4,2,16,1024]{3,2,1,0...) custom-call(bf16[256,1024]{1,0:T(8,128)(2,1)} %x.7, ...), custom_call_target="tpu_custom_call" | custom-call | tf_op jit(solution)/shard_map/gather_all/pallas_call | solution.py:377
  52.7 0.9 slice_reduce_fusion
  54.2 1.0 multiply_cosine_fusion
  55.3 1.2 copy-done.10
  56.6 1.0 copy-done.12
  57.6 0.9 copy-done.13
  58.6 44.2 %attn_fwd.1 = (bf16[8,256,1024]{2,1,0:T(8,128)(2,1)}, f32[8,256,256]{2,1,0:T(8,128)}, bf16[8,256,128]{2,1,0:T(8,128)(2,1)S(1)}, bf16[8,256,128]{2,1,0:T(8,128)(2...) custom-call(s32[4,4]{1,0:T(4,128)S(1)} %copy-done.14, ...), custom_call_target="tpu_custom_call" | custom-call | flops 4000000000 | bytes 16777216 | tf_op jit(solution)/shard_map/attn_fwd/pallas_call | solution.py:524
  102.8 1.0 copy-done.15
  106.0 1.6 copy-done.2
  107.6 32.1 %mid.1 = (f32[256,1024]{1,0:T(8,128)S(1)}, bf16[256,1024]{1,0:T(8,128)(2,1)S(1)}, bf16[256,1024]{1,0:T(8,128)(2,1)}, bf16[8,256,1024]{2,1,0:T(8,128)(2,1)}) custom-call(bf16[8,256,128]{2,1,0:T(8,128)(2,1)S(1)} %get-tuple-element.54.mix, bf16[256,1024]{1,0:T(8,128)(2,1)S(1)} %copy-done.3, bf16[1024,1024]{1,0:T(8,128)(2,1)S(1)} %bitcast.50, ...), custom_call_target="tpu_custom_call" | custom-call | tf_op jit(solution)/shard_map/mid/pallas_call | solution.py:598
  139.8 1.0 copy-done.4
  141.5 39.9 %ffn.1 = (bf16[8,256,1024]{2,1,0:T(8,128)(2,1)}, bf16[8,256,1024]{2,1,0:T(8,128)(2,1)}, bf16[1024,1152]{1,0:T(8,128)(2,1)}, bf16[576,1024]{1,0:T(8,128)(2,1)}) custom-call(s32[16]{0:T(128)} %select_reduce_fusion.1.inv_ref, bf16[8,256,1024]{2,1,0:T(8,128)(2,1)} %get-tuple-element.56.h_ref, bf16[16,128,1024]{2,1,0:T(8,128)(2,1)} %bitcast.61, ...), custom_call_target="tpu_custom_call" | custom-call | flops 24000000000 | bytes 25165824 | tf_op jit(solution)/shard_map/ffn/pallas_call | solution.py:653
  185.9 1.1 dynamic-slice_bitcast_fusion.1
  187.8 36.8 %back_mid.1 = (f32[256,1024]{1,0:T(8,128)}, f32[1,1024]{1,0:T(1,128)}, bf16[1024,1024]{1,0:T(8,128)(2,1)}, bf16[8,256,128]{2,1,0:T(8,128)(2,1)}) custom-call(bf16[8,256,1024]{2,1,0:T(8,128)(2,1)} %get-tuple-element.60.dh, bf16[256,1024]{1,0:T(8,128)(2,1)} %pad_maximum_fusion.1.dyo, f32[256,1024]{1,0:T(8,128)} %copy-done.4, bf16[256,1024]{1,0:T(8,128)(2,1)} %copy-done.6, ...), custom_call_target="tpu_custom_call" | custom-call | tf_op jit(solution)/shard_map/back_mid/pallas_call | solution.py:717
  224.6 69.6 %attn_bwd.1 = (bf16[8,256,1024]{2,1,0:T(8,128)(2,1)}, bf16[1024,256]{1,0:T(8,128)(2,1)}, f32[8,128]{1,0:T(8,128)}, bf16[256,1024]{1,0:T(8,128)(2,1)}, bf16[4,32,...) custom-call(s32[4,4]{1,0:T(4,128)} %len_ref.3, ...), custom_call_target="tpu_custom_call" | custom-call | flops 8000000000 | bytes 16777216 | tf_op jit(solution)/shard_map/attn_bwd/pallas_call | solution.py:847
  294.3 43.1 %final.1 = (f32[256,1024]{1,0:T(8,128)}, bf16[8,32,256]{2,1,0:T(8,128)(2,1)}, bf16[8,32,1152]{2,1,0:T(8,128)(2,1)}, f32[2,16,1024]{2,1,0:T(8,128)}, f32[24,128]{1,0:T(8,128)}) custom-call(bf16[8,256,1024]{2,1,0:T(8,128)(2,1)} %get-tuple-element.75.dh, bf16[256,1024]{1,0:T(8,128)(2,1)} %x.7, f32[256,1024]{1,0:T(8,128)} %get-tuple-element.76.gmid, ...), custom_call_target="tpu_custom_call" | custom-call | tf_op jit(solution)/shard_map/final/pallas_call | solution.py:962
  337.4 1.0 convert_bitcast_fusion
  340.8 2.9 reshape.165
  344.7 1.3 squeeze.27
  346.7 1.3 squeeze.28
  348.0 1.3 dynamic_slice.30
  350.1 1.0 copy.55
  (85 shorter events, 17.9 us)
Async XLA Ops:
  0.6 3.2 copy-start
  0.7 6.0 %copy-start.23 = (bf16[32,4608]{1,0:T(8,128)(2,1)S(1)}, bf16[32,4608]{1,0:T(8,128)(2,1)}, u32[]{:S(2)}) copy-start(bf16[32,4608]{1,0:T(8,128)(2,1)} %param.17) | copy-start | bytes 884740
  7.5 2.8 copy-start.26
  7.7 46.2 %copy-start.14 = (s32[4,4]{1,0:T(4,128)S(1)}, s32[4,4]{1,0:T(4,128)}, u32[]{:S(2)}) copy-start(s32[4,4]{1,0:T(4,128)} %len_ref.3) | copy-start | bytes 196
  8.5 46.8 %copy-start.11 = (bf16[256,1024]{1,0:T(8,128)(2,1)S(1)}, bf16[256,1024]{1,0:T(8,128)(2,1)}, u32[]{:S(2)}) copy-start(bf16[256,1024]{1,0:T(8,128)(2,1)} %dy.1) | copy-start | bytes 1572868
  53.7 49.0 %copy-start.8 = (f32[1,1024]{1,0:T(1,128)}, f32[1,1024]{1,0:T(1,128)S(1)}, u32[]{:S(2)}) copy-start(f32[1,1024]{1,0:T(1,128)S(1)} %get-tuple-element.95.ga_ref.ga) | copy-start | bytes 12292
  53.8 52.2 %copy-start.7 = (f32[1,1024]{1,0:T(1,128)}, f32[1,1024]{1,0:T(1,128)S(1)}, u32[]{:S(2)}) copy-start(f32[1,1024]{1,0:T(1,128)S(1)} %get-tuple-element.94.gf) | copy-start | bytes 12292
  53.9 48.8 %copy-start.9 = (f32[2,128]{1,0:T(2,128)}, f32[2,128]{1,0:T(2,128)S(1)}, u32[]{:S(2)}) copy-start(f32[2,128]{1,0:T(2,128)S(1)} %maximum_maximum_fusion.gqk_ref) | copy-start | bytes 3076
  55.3 47.5 %copy-start.5 = (f32[64,2048]{1,0:T(8,128)}, f32[64,2048]{1,0:T(8,128)S(1)}, u32[]{:S(2)}) copy-start(f32[64,2048]{1,0:T(8,128)S(1)} %pad_maximum_fusion.cs_ref) | copy-start | bytes 1572868
  55.3 1.3 copy-start.10
  56.6 1.0 copy-start.12
  57.6 0.9 copy-start.13
  58.5 47.4 %copy-start.3 = (bf16[256,1024]{1,0:T(8,128)(2,1)S(1)}, bf16[256,1024]{1,0:T(8,128)(2,1)}, u32[]{:S(2)}) copy-start(bf16[256,1024]{1,0:T(8,128)(2,1)} %x.7) | copy-start | bytes 1572868
  102.8 1.0 copy-start.15
  103.8 0.8 copy-start.16
  106.0 1.6 copy-start.2
  139.7 1.0 copy-start.4
  141.5 39.9 %copy-start.25 = (s32[16]{0:T(128)S(1)}, s32[16]{0:T(128)}, u32[]{:S(2)}) copy-start(s32[16]{0:T(128)} %select_reduce_fusion.1.inv_ref) | copy-start | bytes 196
  337.4 3.4 copy-start.21
  344.7 4.6 %copy-start.22 = (bf16[256,1024]{1,0:T(8,128)(2,1)S(1)}, bf16[256,1024]{1,0:T(8,128)(2,1)}, u32[]{:S(2)}) copy-start(bf16[256,1024]{1,0:T(8,128)(2,1)} %get-tuple-element.112) | copy-start | bytes 1572868
  346.7 3.4 copy-start.19
  346.7 4.4 %copy-start.24 = (f32[2,16,1024]{2,1,0:T(8,128)S(1)}, f32[2,16,1024]{2,1,0:T(8,128)}, u32[]{:S(2)}) copy-start(f32[2,16,1024]{2,1,0:T(8,128)} %get-tuple-element.84) | copy-start | bytes 393220
  346.7 5.0 %copy-start.20 = (f32[9,16,1024]{2,1,0:T(8,128)S(1)}, f32[9,16,1024]{2,1,0:T(8,128)}, u32[]{:S(2)}) copy-start(f32[9,16,1024]{2,1,0:T(8,128)} %get-tuple-element.86) | copy-start | bytes 1769476
  346.7 5.9 %copy-start.1 = (bf16[32,1024]{1,0:T(8,128)(2,1)S(1)}, bf16[32,1024]{1,0:T(8,128)(2,1)}, u32[]{:S(2)}) copy-start(bf16[32,1024]{1,0:T(8,128)(2,1)} %param.13) | copy-start | bytes 196612
  (3 other events, 2.2 us)

commit v3 on v2

--- a/solution.py
+++ b/solution.py
@@ -104,7 +104,14 @@
         ]
 
     def start(self):
-        start_all([self.x[0], self.y[1], self.x[1], self.y[0]] + self.o + self.local)
+        self.start_first()
+        self.start_second()
+
+    def start_first(self):
+        start_all([self.x[0], self.y[1]] + self.o + self.local)
+
+    def start_second(self):
+        start_all([self.x[1], self.y[0]])
 
     def relay1(self):
         self.x[0].wait_recv()
@@ -123,10 +130,18 @@
             self.r[h].wait_recv()
             self.fd[h].start()
 
+    def arrive(self, copies):
+        for c in copies:
+            c.wait_recv()
+
+    def sent(self):
+        for c in self.x + self.y + self.r + self.o + self.fx + self.fy + self.fd:
+            c.wait_send()
+        wait_all(self.local)
+
     def finish(self):
-        wait_all(self.o + self.fx + self.fy + self.fd + self.local)
-        for c in self.x + self.y + self.r:
-            c.wait_send()
+        self.arrive(self.o + self.fx + self.fy + self.fd)
+        self.sent()
 
 
 class Ring:
@@ -248,9 +263,6 @@
     ]
 
 
-ORDER = (6, 2, 4, 0)
-
-
 class PlaneReduce:
     def __init__(self, me, part, sib, send, relay, fx, fy, ss, rs):
         p = lax.rem(me, GROUP)
@@ -262,25 +274,34 @@
         def cp(a, b, i, dev):
             return rcopy(a, b, ss.at[i], rs.at[i], dev)
 
-        self.first = [cp(part(p ^ (m ^ 1)), sib.at[i], i, me ^ 1) for i, m in enumerate(ORDER)]
+        self.first = [cp(part(p ^ (2 * i + 1)), sib.at[i], i, me ^ 1) for i in range(4)]
         self.diag = [cp(send.at[0, hs(0)], relay.at[0], 4, xn), cp(send.at[0, hs(1)], relay.at[1], 5, yn)]
         self.toy = [cp(send.at[2, hs(h)], fy.at[hs(h)], 6 + h, yn) for h in range(2)]
         self.tox = [cp(send.at[1, hs(h)], fx.at[hs(h)], 8 + h, xn) for h in range(2)]
 
     def start(self):
-        start_all(self.first)
+        start_all([self.first[i] for i in (3, 1, 2, 0)])
 
     def chip(self, i):
         self.first[i].wait_recv()
-        return self.part(self.p ^ ORDER[i])[...].astype(F32) + self.sib[i].astype(F32)
-
-    def phase1(self):
-        self.send[0] = self.chip(0).astype(BF16)
+        return self.part(self.p ^ (2 * i))[...].astype(F32) + self.sib[i].astype(F32)
+
+    def chip_d(self):
+        self.send[0] = self.chip(3).astype(BF16)
         start_all(self.diag)
+
+    def chip_x(self):
         self.send[1] = self.chip(1).astype(BF16)
         self.tox[0].start()
+
+    def chip_y(self):
         self.send[2] = self.chip(2).astype(BF16)
         self.toy[1].start()
+
+    def phase1(self):
+        self.chip_d()
+        self.chip_x()
+        self.chip_y()
 
     def phase2(self):
         self.diag[0].wait_recv()
@@ -293,7 +314,7 @@
         self.tox[1].start()
 
     def phase3(self):
-        own = self.chip(3)
+        own = self.chip(0)
         for c in self.toy + self.tox:
             c.wait_recv()
         own = own + self.fx[...].astype(F32) + self.fy[...].astype(F32)
@@ -568,13 +589,30 @@
     )(lengths, x_all, wqkv, ga, gqk, cs, dy, w2, wo)
 
 
-def mid_kernel(n, mix, x, wo, gf, res, mown, h2, h2all, mbuf, ps, pr, hs, hr, ls):
+def norm_back(dyv, xv, gain):
+    r = lax.rsqrt(jnp.mean(xv * xv, axis=-1, keepdims=True) + EPSILON)
+    xr = xv * r
+    gy = dyv * gain
+    dx = r * (gy - xr * jnp.mean(gy * xr, axis=-1, keepdims=True))
+    return dx, jnp.sum(dyv * xr, axis=0, keepdims=True)
+
+
+def ffn_block_kernel(n, inv, mix, x, wo, gf, w2, wd, dy, res, gmid, dgf, dwo, dmh, po, dw2, dwd, mbuf, h2, wgs, wds, dys, acts, dgus, part, mown, stage, ps, pr, hs, hr, os_, qs, qr, *red_refs):
     me, p, g, groups, zq, zg = places(n)
     barrier([me ^ m for m in range(1, GROUP)])
+    fl = wd.shape[0]
+    fp = wds.shape[0]
     pc = start_all(
         [rcopy(mix.at[p ^ m], mbuf.at[p], ps.at[m - 1], pr.at[m - 1], me ^ m) for m in range(1, GROUP)]
     )
     mbuf[p] = mix[p]
+    gap = jnp.zeros((D, fp - fl), BF16)
+    wgs[:, :fl] = w2[:, :fl]
+    wgs[:, fl:fp] = gap
+    wgs[:, fp : fp + fl] = w2[:, fl:]
+    wgs[:, fp + fl :] = gap
+    wds[:fl] = wd[...]
+    wds[fl:] = jnp.zeros((fp - fl, D), BF16)
     for c in pc:
         c.wait_recv()
     m = jnp.concatenate([mbuf[b] for b in range(GROUP)], axis=1)
@@ -582,157 +620,150 @@
     z = x[...].astype(F32) + nn(m, wo[...])
     res[...] = z
     r = lax.rsqrt(jnp.mean(z * z, axis=-1, keepdims=True) + EPSILON)
-    h2[...] = (z * r * gf[...]).astype(BF16)
+    h2[p] = (z * r * gf[...]).astype(BF16)
     hb = halves(BLOCK)
-    hg = PlaneGather(me, p, lambda h: h2.at[hb(h)], lambda b, h: h2all.at[b, hb(h)], hs, hr, ls)
-    hg.start()
-    hg.relay1()
-    hg.relay2()
-    hg.relay3()
-    hg.finish()
+    hg = PlaneGather(me, p, lambda h: h2.at[p, hb(h)], lambda b, h: h2.at[b, hb(h)], hs, hr)
+    red = PlaneReduce(me, lambda b: part.at[b], *red_refs)
+    hg.start_first()
+
+    def block(t, carry):
+        @pl.when(t == 1)
+        def _():
+            hg.start_second()
+            hg.arrive(hg.o)
+
+        @pl.when(t == 2)
+        def _():
+            red.first[0].start()
+            hg.relay1()
+            hg.relay2()
+
+        @pl.when(t == 3)
+        def _():
+            hg.arrive(hg.fx)
+
+        @pl.when(t == 4)
+        def _():
+            red.first[1].start()
+
+        @pl.when(t == 5)
+        def _():
+            hg.arrive(hg.fy)
+            red.chip_x()
+
+        @pl.when(t == 6)
+        def _():
+            red.first[2].start()
+            hg.relay3()
+
+        @pl.when(t == 7)
+        def _():
+            red.chip_y()
+            hg.arrive(hg.fd)
+
+        b = p ^ t
+        h = h2[b]
+        dyb = jnp.concatenate([dy[inv[2 * b]], dy[inv[2 * b + 1]]], axis=0)
+        dys[b] = dyb
+        gu = nn(h, wgs[...])
+        da = nt(dyb, wds[...])
+        gp, up = gu[:, :fp], gu[:, fp:]
+        sig = 1.0 / (1.0 + jnp.exp(-gp))
+        sg = gp * sig
+        acts[b] = (sg * up).astype(BF16)
+        dgu = jnp.concatenate(
+            [(da * up * (sig * (1.0 + gp * (1.0 - sig)))).astype(BF16), (da * sg).astype(BF16)], axis=1
+        )
+        dgus[b] = dgu
+        part[b] = nt(dgu, wgs[...]).astype(BF16)
+        return carry
+
+    lax.fori_loop(0, GROUP, block, 0)
+    red.first[3].start()
+    a_all = acts[...].reshape(ROWS, fp)
+    dwd[...] = tn(a_all, dys[...].reshape(ROWS, D))[:fl].astype(BF16)
+    red.chip_d()
+
+    def out(b, carry):
+        slot = lax.rem(b, 2)
+
+        @pl.when(b > 1)
+        def _():
+            pltpu.make_async_copy(stage.at[slot], po.at[b - 2], os_.at[slot]).wait()
+
+        stage[slot] = nn(acts[b], wds[...]).astype(BF16)
+        pltpu.make_async_copy(stage.at[slot], po.at[b], os_.at[slot]).start()
+        return carry
+
+    lax.fori_loop(0, GROUP, out, 0)
+    for b in range(GROUP - 2, GROUP):
+        pltpu.make_async_copy(stage.at[b % 2], po.at[b], os_.at[b % 2]).wait()
+    red.phase2()
+    h_all = h2[...].reshape(ROWS, D)
+    dg_all = dgus[...].reshape(ROWS, 2 * fp)
+    dw2[:, :fl] = tn(h_all, dg_all[:, :fp])[:, :fl].astype(BF16)
+    dw2[:, fl:] = tn(h_all, dg_all[:, fp:])[:, :fl].astype(BF16)
+    dx, dgain = norm_back(red.phase3(), res[...], gf[...])
+    dyo = dys[p].astype(F32)
+    gm = dyo + dx
+    gmid[...] = gm
+    dgf[...] = dgain
+    gl = gm.astype(BF16)
+    dm = nt(gl, wo[...]).astype(BF16)
+    for b in range(GROUP):
+        mbuf[b] = dm[:, 128 * b : 128 * (b + 1)]
     for c in pc:
         c.wait_send()
-
-
-def mid(n, mix, x, wo, gf):
+    qc = start_all(
+        [rcopy(mbuf.at[p ^ m], dmh.at[p], qs.at[m - 1], qr.at[m - 1], me ^ m) for m in range(1, GROUP)]
+    )
+    dmh[p] = mbuf[p]
+    dwo[...] = tn(mown[...], gl).astype(BF16)
+    wait_all(qc)
+    hg.sent()
+
+
+def ffn_block(n, inv, mix, x, wo, gf, w2, wd, dy):
+    fl = wd.shape[0]
+    fp = -(-fl // 128) * 128
+    vm = lambda *s: pltpu.VMEM(s, BF16)
     return pl.pallas_call(
-        functools.partial(mid_kernel, n),
-        out_shape=(SDS((BLOCK, D), F32), SDS((BLOCK, D), BF16), SDS((BLOCK, D), BF16), SDS((GROUP, BLOCK, D), BF16)),
-        in_specs=[VM] * 4,
-        out_specs=(VM, VM, VM, ANY),
+        functools.partial(ffn_block_kernel, n),
+        out_shape=(
+            SDS((BLOCK, D), F32),
+            SDS((BLOCK, D), F32),
+            SDS((1, D), F32),
+            SDS((D, D), BF16),
+            SDS((GROUP, BLOCK, 128), BF16),
+            SDS((GROUP, BLOCK, D), BF16),
+            SDS((D, 2 * fl), BF16),
+            SDS((fl, D), BF16),
+        ),
+        in_specs=[SM] + [VM] * 7,
+        out_specs=(VM, VM, VM, VM, VM, ANY, VM, VM),
         scratch_shapes=[
-            pltpu.VMEM((GROUP, BLOCK, 128), BF16),
+            vm(GROUP, BLOCK, 128),
+            vm(GROUP, BLOCK, D),
+            vm(D, 2 * fp),
+            vm(fp, D),
+            vm(GROUP, BLOCK, D),
+            vm(GROUP, BLOCK, fp),
+            vm(GROUP, BLOCK, 2 * fp),
+            vm(GROUP, BLOCK, D),
+            vm(BLOCK, D),
+            vm(2, BLOCK, D),
             DMA((7,)),
             DMA((7,)),
             DMA((14,)),
             DMA((14,)),
             DMA((2,)),
-        ],
-        compiler_params=pltpu.CompilerParams(collective_id=2, has_side_effects=True, vmem_limit_bytes=48 << 20),
-        name="mid",
-    )(mix, x, wo, gf)
-
-
-def ffn_kernel(inv_ref, h_ref, da_ref, db_ref, wgu_ref, wd_ref, po_ref, dh_ref, dwgu_ref, dwd_ref, agu, ad):
-    i = pl.program_id(0)
-    fl = wd_ref.shape[0]
-
-    @pl.when(i == 0)
-    def _():
-        agu[...] = jnp.zeros_like(agu)
-        ad[...] = jnp.zeros_like(ad)
-
-    h = h_ref[0]
-    dy = jnp.concatenate([da_ref[0], db_ref[0]], axis=0)
-    gp = nn(h, wgu_ref[:, :fl])
-    up = nn(h, wgu_ref[:, fl:])
-    sig = 1.0 / (1.0 + jnp.exp(-gp))
-    sg = gp * sig
-    act = (sg * up).astype(BF16)
-    po_ref[0] = nn(act, wd_ref[...]).astype(BF16)
-    da = nt(dy, wd_ref[...])
-    dg = (da * up * (sig * (1.0 + gp * (1.0 - sig)))).astype(BF16)
-    du = (da * sg).astype(BF16)
-    dh_ref[0] = (nt(dg, wgu_ref[:, :fl]) + nt(du, wgu_ref[:, fl:])).astype(BF16)
-    ad[...] += tn(act, dy)
-    agu[:, :fl] += tn(h, dg)
-    agu[:, fl:] += tn(h, du)
-
-    @pl.when(i == pl.num_programs(0) - 1)
-    def _():
-        dwgu_ref[...] = agu[...].astype(BF16)
-        dwd_ref[...] = ad[...].astype(BF16)
-
-
-def ffn(inv, h2all, dyall, wgu, wd):
-    nb = ROWS // BLOCK
-    fl = wd.shape[0]
-    blk = pl.BlockSpec((1, BLOCK, D), lambda i, inv: (i, 0, 0))
-    one = pl.Buffered(1)
-    slots = dyall.reshape(ROWS // SLOT, SLOT, D)
-    return pl.pallas_call(
-        ffn_kernel,
-        grid_spec=pltpu.PrefetchScalarGridSpec(
-            num_scalar_prefetch=1,
-            grid=(nb,),
-            in_specs=[
-                blk,
-                pl.BlockSpec((1, SLOT, D), lambda i, inv: (inv[2 * i], 0, 0)),
-                pl.BlockSpec((1, SLOT, D), lambda i, inv: (inv[2 * i + 1], 0, 0)),
-                pl.BlockSpec((D, 2 * fl), lambda i, inv: (0, 0), pipeline_mode=one),
-                pl.BlockSpec((fl, D), lambda i, inv: (0, 0), pipeline_mode=one),
-            ],
-            out_specs=(
-                blk,
-                blk,
-                pl.BlockSpec((D, 2 * fl), lambda i, inv: (0, 0), pipeline_mode=one),
-                pl.BlockSpec((fl, D), lambda i, inv: (0, 0), pipeline_mode=one),
-            ),
-            scratch_shapes=[pltpu.VMEM((D, 2 * fl), F32), pltpu.VMEM((fl, D), F32)],
-        ),
-        out_shape=(
-            SDS((nb, BLOCK, D), BF16),
-            SDS((nb, BLOCK, D), BF16),
-            SDS((D, 2 * fl), BF16),
-            SDS((fl, D), BF16),
-        ),
-        compiler_params=pltpu.CompilerParams(dimension_semantics=("arbitrary",), vmem_limit_bytes=56 << 20),
-        cost_estimate=pl.CostEstimate(flops=24 * 10**9, bytes_accessed=24 << 20, transcendentals=10**6),
-        name="ffn",
-    )(inv, h2all, slots, slots, wgu, wd)
-
-
-def norm_back(dyv, xv, gain):
-    r = lax.rsqrt(jnp.mean(xv * xv, axis=-1, keepdims=True) + EPSILON)
-    xr = xv * r
-    gy = dyv * gain
-    dx = r * (gy - xr * jnp.mean(gy * xr, axis=-1, keepdims=True))
-    return dx, jnp.sum(dyv * xr, axis=0, keepdims=True)
-
-
-def back_mid_kernel(n, dh, dyo, res, mown, wo, gf, gmid, dgf, dwo, dmh, sib, send, rel, fx, fy, ss, rs, dmix, ps, pr):
-    me, p, g, groups, zq, zg = places(n)
-    barrier([me ^ m for m in range(1, GROUP)])
-    red = PlaneReduce(me, lambda b: dh.at[b], sib, send, rel, fx, fy, ss, rs)
-    red.start()
-    red.phase1()
-    red.phase2()
-    dx, dgain = norm_back(red.phase3(), res[...], gf[...])
-    gm = dyo[...].astype(F32) + dx
-    gmid[...] = gm
-    dgf[...] = dgain
-    gl = gm.astype(BF16)
-    dm = nt(gl, wo[...]).astype(BF16)
-    for b in range(GROUP):
-        dmix[b] = dm[:, 128 * b : 128 * (b + 1)]
-    pc = start_all(
-        [rcopy(dmix.at[p ^ m], dmh.at[p], ps.at[m - 1], pr.at[m - 1], me ^ m) for m in range(1, GROUP)]
-    )
-    dmh[p] = dmix[p]
-    dwo[...] = tn(mown[...], gl).astype(BF16)
-    wait_all(pc)
-
-
-def back_mid(n, dh, dyo, res, mown, wo, gf):
-    return pl.pallas_call(
-        functools.partial(back_mid_kernel, n),
-        out_shape=(
-            SDS((BLOCK, D), F32),
-            SDS((1, D), F32),
-            SDS((D, D), BF16),
-            SDS((GROUP, BLOCK, 128), BF16),
-        ),
-        in_specs=[VM] * 6,
-        out_specs=(VM,) * 4,
-        scratch_shapes=plane_scratch((BLOCK, D))
-        + [
-            pltpu.VMEM((GROUP, BLOCK, 128), BF16),
             DMA((7,)),
             DMA((7,)),
-        ],
-        compiler_params=pltpu.CompilerParams(collective_id=3, has_side_effects=True, vmem_limit_bytes=58 << 20),
-        name="back_mid",
-    )(dh, dyo, res, mown, wo, gf)
+        ]
+        + plane_scratch((BLOCK, D)),
+        compiler_params=pltpu.CompilerParams(collective_id=2, has_side_effects=True, vmem_limit_bytes=62 << 20),
+        name="ffn_block",
+    )(inv, mix, x, wo, gf, w2, wd, dy.reshape(ROWS // SLOT, SLOT, D))
 
 
 def attn_bwd_kernel(n, len_ref, dm_ref, q_ref, kvall_ref, lse_ref, mixf_ref, h_ref, raw_ref, w_ref, gqk_ref, cs_ref, po, res, dwo, dw2, dwd, dh_ref, dw_ref, dg_ref, result, two, t2, od, k_s, v_s, dkv, dqt, dws, *rest):
@@ -1036,13 +1067,7 @@
     )
     wgu = w2.reshape(D, -1)
     wo = wo.reshape(D, D)
-    res, mown, _, h2_all = mid(n, mix, tokens, wo, gf)
-    po, dh2, dwgu, dwd = ffn(inv, h2_all, dy_all, wgu, wd)
-    dslots = dy_all.reshape(ROWS // SLOT, SLOT, D)
-    dy_own = jnp.concatenate(
-        [lax.dynamic_index_in_dim(dslots, inv[2 * p + k], 0, keepdims=False) for k in range(2)], axis=0
-    )
-    gmid, dgf, dwo, dmh = back_mid(n, dh2, dy_own, res, mown, wo, gf)
+    res, gmid, dgf, dwo, dmh, po, dwgu, dwd = ffn_block(n, inv, mix, tokens, wo, gf, wgu, wd, dy_all)
     dh1, dwqkv, dgqk, result, two, t2, od = attn_bwd(
         n,
         lengths,

time: 353 us -> 309 us (0.88)
  Pallas kernels: 307 us -> 270 us
  between operations: 4.99 us -> 0.99 us
    pallas_call x3 -> x1, Pallas kernels: 109 us -> 71.7 us  [ffn_block(): pl.pallas_call(functools.partial(ffn_block_kernel, n), out_shape=(SDS((BL...]
    unnamed x58 -> x44, local copies, waits for them, and re-layouts: 13.1 us -> 11.4 us
where the time goes in v3:
time: 309 us; the launch traced here: 308 us
  Pallas kernels  270 us (87%)
  local copies, waits for them, and re-layouts  31.3 us (10%)
  other arithmetic  5.69 us (2%)
    pallas_call x1, Pallas kernels, ffn_block(): pl.pallas_call(functools.partial(ffn_block_kernel, n), out_shape=(SDS((BL...  71.7 us
    pallas_call x1, Pallas kernels, attn_bwd(): pl.pallas_call(functools.partial(attn_bwd_kernel, n), grid=(nb,), in_spec...  69.5 us
    pallas_call x1, Pallas kernels, attn_fwd(): pl.pallas_call(functools.partial(attn_fwd_kernel, n), grid=(nb,), in_spec...  44.1 us
    pallas_call x1, Pallas kernels, final(): pl.pallas_call(functools.partial(final_kernel, n), out_shape=(SDS((BLOCK,...  43.3 us
    pallas_call x1, Pallas kernels, gather_all(): pl.pallas_call(functools.partial(gather_kernel, n), out_shape=(SDS((GROUP...  41.7 us
    unnamed x44, local copies, waits for them, and re-layouts  11.4 us

profile of v3, /device:TPU:0, one launch (start us, length us, event | category | flops | bytes accessed | tf_op | source)
XLA Modules:
  0.0 308.2 jit_solution(2541709182927136695)
XLA Ops:
  3.0 1.3 pad_convert_fusion.gt
  4.4 0.9 reshape.140
  5.3 0.9 reshape.141
  6.9 1.0 multiply_cosine_fusion
  8.0 0.9 stack.9
  9.1 0.9 stack.10
  10.9 1.9 reshape.142.a2
  12.8 41.7 %gather_all.1 = (bf16[8,256,1024]{2,1,0:T(8,128)(2,1)}, bf16[4,8,32,256]{3,2,1,0:T(8,128)(2,1)}, bf16[8,32,1152]{2,1,0:T(8,128)(2,1)}, bf16[4,2,16,1024]{3,2,1,0...) custom-call(bf16[256,1024]{1,0:T(8,128)(2,1)} %x.7, ...), custom_call_target="tpu_custom_call" | custom-call | tf_op jit(solution)/shard_map/gather_all/pallas_call | solution.py:398
  54.5 0.9 slice_reduce_fusion
  56.3 1.1 copy-done.5
  57.4 1.0 copy-done.7
  58.4 0.9 copy-done.8
  59.4 44.1 %attn_fwd.1 = (bf16[8,256,1024]{2,1,0:T(8,128)(2,1)}, f32[8,256,256]{2,1,0:T(8,128)}, bf16[8,256,128]{2,1,0:T(8,128)(2,1)S(1)}, bf16[8,256,128]{2,1,0:T(8,128)(2...) custom-call(s32[4,4]{1,0:T(4,128)S(1)} %copy-done.9, ...), custom_call_target="tpu_custom_call" | custom-call | flops 4000000000 | bytes 16777216 | tf_op jit(solution)/shard_map/attn_fwd/pallas_call | solution.py:545
  104.4 1.0 copy-done.10
  107.6 71.7 %ffn_block.1 = (f32[256,1024]{1,0:T(8,128)}, f32[256,1024]{1,0:T(8,128)}, f32[1,1024]{1,0:T(1,128)}, bf16[1024,1024]{1,0:T(8,128)(2,1)}, bf16[8,256,128]{2,1,0:T...) custom-call(s32[16]{0:T(128)} %select_reduce_fusion.1.inv, ...), custom_call_target="tpu_custom_call" | custom-call | tf_op jit(solution)/shard_map/ffn_block/pallas_call | solution.py:730
  179.2 69.5 %attn_bwd.1 = (bf16[8,256,1024]{2,1,0:T(8,128)(2,1)}, bf16[1024,256]{1,0:T(8,128)(2,1)}, f32[8,128]{1,0:T(8,128)}, bf16[256,1024]{1,0:T(8,128)(2,1)}, bf16[4,32,...) custom-call(s32[4,4]{1,0:T(4,128)} %len_ref.3, ...), custom_call_target="tpu_custom_call" | custom-call | flops 8000000000 | bytes 16777216 | tf_op jit(solution)/shard_map/attn_bwd/pallas_call | solution.py:878
  248.7 43.3 %final.1 = (f32[256,1024]{1,0:T(8,128)}, bf16[8,32,256]{2,1,0:T(8,128)(2,1)}, bf16[8,32,1152]{2,1,0:T(8,128)(2,1)}, f32[2,16,1024]{2,1,0:T(8,128)}, f32[24,128]{1,0:T(8,128)}) custom-call(bf16[8,256,1024]{2,1,0:T(8,128)(2,1)} %get-tuple-element.69.dh, bf16[256,1024]{1,0:T(8,128)(2,1)} %x.7, f32[256,1024]{1,0:T(8,128)} %get-tuple-element.70.gmid, ...), custom_call_target="tpu_custom_call" | custom-call | tf_op jit(solution)/shard_map/final/pallas_call | solution.py:993
  292.0 1.3 dynamic_slice.13
  293.4 0.9 convert_bitcast_fusion
  296.7 2.9 reshape.164
  300.6 1.3 squeeze.11
  302.6 1.3 squeeze.10
  303.9 1.9 copy.54
  305.8 1.0 copy.55
  (66 shorter events, 13.7 us)
Async XLA Ops:
  0.6 3.7 %copy-start = (bf16[32,1024]{1,0:T(8,128)(2,1)S(1)}, bf16[32,1024]{1,0:T(8,128)(2,1)}, u32[]{:S(2)}) copy-start(bf16[32,1024]{1,0:T(8,128)(2,1)} %param.13) | copy-start | bytes 196612
  0.7 8.4 %copy-start.18 = (bf16[32,4608]{1,0:T(8,128)(2,1)S(1)}, bf16[32,4608]{1,0:T(8,128)(2,1)}, u32[]{:S(2)}) copy-start(bf16[32,4608]{1,0:T(8,128)(2,1)} %param.18) | copy-start | bytes 884740
  0.7 7.3 %copy-start.17 = (bf16[32,4608]{1,0:T(8,128)(2,1)S(1)}, bf16[32,4608]{1,0:T(8,128)(2,1)}, u32[]{:S(2)}) copy-start(bf16[32,4608]{1,0:T(8,128)(2,1)} %param.17) | copy-start | bytes 884740
  8.0 48.4 %copy-start.2 = (f32[64,2048]{1,0:T(8,128)}, f32[64,2048]{1,0:T(8,128)S(1)}, u32[]{:S(2)}) copy-start(f32[64,2048]{1,0:T(8,128)S(1)} %pad_maximum_fusion.cs_ref) | copy-start | bytes 1572868
  10.1 46.2 %copy-start.6 = (bf16[256,1024]{1,0:T(8,128)(2,1)S(1)}, bf16[256,1024]{1,0:T(8,128)(2,1)}, u32[]{:S(2)}) copy-start(bf16[256,1024]{1,0:T(8,128)(2,1)} %dy.1) | copy-start | bytes 1572868
  10.2 46.2 %copy-start.9 = (s32[4,4]{1,0:T(4,128)S(1)}, s32[4,4]{1,0:T(4,128)}, u32[]{:S(2)}) copy-start(s32[4,4]{1,0:T(4,128)} %len_ref.3) | copy-start | bytes 196
  56.2 47.3 %copy-start.3 = (f32[1,1024]{1,0:T(1,128)}, f32[1,1024]{1,0:T(1,128)S(1)}, u32[]{:S(2)}) copy-start(f32[1,1024]{1,0:T(1,128)S(1)} %get-tuple-element.87.ga_ref.ga) | copy-start | bytes 12292
  56.3 1.1 copy-start.5
  57.4 1.0 copy-start.7
  58.4 0.9 copy-start.8
  59.4 44.2 %copy-start.4 = (f32[2,128]{1,0:T(2,128)}, f32[2,128]{1,0:T(2,128)S(1)}, u32[]{:S(2)}) copy-start(f32[2,128]{1,0:T(2,128)S(1)} %maximum_maximum_fusion.gqk_ref) | copy-start | bytes 3076
  103.6 0.8 copy-start.1
  104.4 1.0 copy-start.10
  105.3 0.8 copy-start.11
  106.1 0.8 copy-start.12
  106.9 0.7 copy-start.13
  292.0 4.7 %copy-start.16 = (bf16[8,32,1152]{2,1,0:T(8,128)(2,1)S(1)}, bf16[8,32,1152]{2,1,0:T(8,128)(2,1)}, u32[]{:S(2)}) copy-start(bf16[8,32,1152]{2,1,0:T(8,128)(2,1)} %get-tuple-element.79) | copy-start | bytes 1769476
  301.9 3.8 %copy-start.14 = (f32[256,1024]{1,0:T(8,128)S(1)}, f32[256,1024]{1,0:T(8,128)}, u32[]{:S(2)}) copy-start(f32[256,1024]{1,0:T(8,128)} %get-tuple-element.103) | copy-start | bytes 3145732
  302.6 4.2 %copy-start.19 = (f32[2,16,1024]{2,1,0:T(8,128)S(1)}, f32[2,16,1024]{2,1,0:T(8,128)}, u32[]{:S(2)}) copy-start(f32[2,16,1024]{2,1,0:T(8,128)} %get-tuple-element.78) | copy-start | bytes 393220
  302.6 4.8 %copy-start.15 = (f32[9,16,1024]{2,1,0:T(8,128)S(1)}, f32[9,16,1024]{2,1,0:T(8,128)}, u32[]{:S(2)}) copy-start(f32[9,16,1024]{2,1,0:T(8,128)} %get-tuple-element.80) | copy-start | bytes 1769476

commit v4 on v3

--- a/solution.py
+++ b/solution.py
@@ -19,6 +19,7 @@
 BLOCK = 256
 QKV = 256
 WINDOW = 4
+VMEM_LIMIT = 62 << 20
 EPSILON = 1e-05
 ROPE_THETA = 1000000.0
 SCALE = 1.0 / math.sqrt(HEAD)
@@ -29,6 +30,7 @@
 DMA = pltpu.SemaphoreType.DMA
 VM = pl.BlockSpec(memory_space=pltpu.VMEM)
 ANY = pl.BlockSpec(memory_space=pl.ANY)
+HB = pl.BlockSpec(memory_space=pltpu.HBM)
 SM = pl.BlockSpec(memory_space=pltpu.SMEM)
 SDS = jax.ShapeDtypeStruct
 
@@ -72,6 +74,14 @@
     for c in copies:
         c.start()
     return copies
+
+
+def bring(pairs, sem):
+    return start_all([pltpu.make_async_copy(a, b, sem.at[i]) for i, (a, b) in enumerate(pairs)])
+
+
+def in_hbm(*arrays):
+    return [pltpu.with_memory_space_constraint(a, pltpu.HBM) for a in arrays]
 
 
 def wait_all(copies):
@@ -337,27 +347,29 @@
     ]
 
 
-def gather_kernel(n, x, a1, a2, wo, wd, gt, xo, a1o, a2o, woo, wdo, gto, ls, xs, xr, ps, pr, zs, zr):
+def gather_kernel(n, len_ref, x_, wq_, wk_, wv_, wg_, wu_, wo_, wd_, gn_, xo, a1o, a2o, woo, wdo, gvec, cs, x, gn, wq, wk, wv, wo, wd, wg, wu, a1, a2, gt, gto, fs, ls, xs, xr, ps, pr, zs, zr):
     me, p, g, groups, zq, zg = places(n)
+    fetch = bring(
+        (
+            (x_, x),
+            (gn_, gn),
+            (wq_, wq),
+            (wk_, wk),
+            (wv_, wv),
+            (wo_, wo),
+            (wd_, wd),
+            (wg_, wg),
+            (wu_, wu),
+        ),
+        fs,
+    )
+    share = gn.shape[1]
+    ffc = wg.shape[1] // (groups * GROUP)
     barrier([me ^ m for m in range(1, GROUP)] + zq)
-    local = [
-        pltpu.make_async_copy(a1.at[p], a1o.at[g, p], ls.at[0]),
-        pltpu.make_async_copy(gt, gto.at[g, p], ls.at[1]),
-        pltpu.make_async_copy(a2.at[p], a2o.at[p], ls.at[2]),
-    ]
-    start_all(local)
-    pc = {}
-
-    def exchange(k, src, dst):
-        for m in range(1, GROUP):
-            pc[k, m] = rcopy(src(p ^ m), dst, ps.at[k, m - 1], pr.at[k, m - 1], me ^ m)
-            pc[k, m].start()
-
-    exchange(0, lambda b: a1.at[b], a1o.at[g, p])
-    exchange(1, lambda b: gt, gto.at[g, p])
     hx = halves(BLOCK)
     xg = PlaneGather(me, p, lambda h: x.at[hx(h)], lambda b, h: xo.at[b, hx(h)], xs, xr, ls.at[pl.ds(5, 2)])
-    xg.start()
+    fetch[0].wait()
+    xg.start_first()
 
     def ring(k, src, dst, local=None):
         hk = halves(dst.shape[1])
@@ -369,45 +381,91 @@
         ring(2, wd, wdo, ls.at[3]),
         ring(3, wo, woo, ls.at[4]),
     ]
+    pc = {}
+
+    def exchange(k, src, dst):
+        for m in range(1, GROUP):
+            pc[k, m] = rcopy(src(p ^ m), dst, ps.at[k, m - 1], pr.at[k, m - 1], me ^ m)
+            pc[k, m].start()
+
+    fetch[1].wait()
+    gt[...] = jnp.zeros_like(gt)
+    gt[0:1, :share] = gn[...].astype(F32)
+    exchange(1, lambda b: gt, gto.at[g, p])
+    gto[g, p] = gt[...]
+    wait_all(fetch[2:5])
+    for b in range(GROUP):
+        a1[b, :, :128] = wq[:, 128 * b : 128 * (b + 1)]
+        at = slice(HEAD * b, HEAD * (b + 1))
+        a1[b, :, 128:] = jnp.concatenate([wk[:, at], wv[:, at]], axis=1)
+    exchange(0, lambda b: a1.at[b], a1o.at[g, p])
+    wait_all(fetch[5:7])
+    rings[3].start()
     rings[2].start()
-    rings[3].start()
+    wait_all(fetch[7:])
+    for b in range(GROUP):
+        at = [slice((GROUP * k + b) * ffc, (GROUP * k + b + 1) * ffc) for k in range(groups)]
+        a2[b] = jnp.concatenate([wg[:, k] for k in at] + [wu[:, k] for k in at], axis=1)
     exchange(2, lambda b: a2.at[b], a2o.at[p])
+    xg.start_second()
+    local = [
+        pltpu.make_async_copy(a1.at[p], a1o.at[g, p], ls.at[0]),
+        pltpu.make_async_copy(a2.at[p], a2o.at[p], ls.at[2]),
+    ]
+    start_all(local)
+    local[0].wait()
     for k in range(2):
         for m in range(1, GROUP):
             pc[k, m].wait_recv()
-        local[k].wait()
         rings[k].start()
     xg.relay1()
+    row = lax.broadcasted_iota(jnp.int32, (1, ROWS), 1)
+    position = (row - seq_start(row, len_ref, g)).astype(F32)
+    index = lax.broadcasted_iota(jnp.int32, (HEAD // 2, 1), 0).astype(F32)
+    angles = jnp.exp(index * (-2.0 * math.log(ROPE_THETA) / HEAD)) * position
+    cs[: HEAD // 2] = jnp.cos(angles)
+    cs[HEAD // 2 :] = jnp.sin(angles)
+    xg.relay2()
     for k in (3, 0, 1, 2):
         rings[k].relay()
-    xg.relay2()
     xg.relay3()
     for m in range(1, GROUP):
         pc[2, m].wait_recv()
-    local[2].wait()
+    local[1].wait()
     for c in pc.values():
         c.wait_send()
     for k in range(4):
         rings[k].finish()
+    gvec[...] = jnp.concatenate(
+        [gto[k, b, 0:1, :share] for k in range(groups) for b in range(GROUP)], axis=1
+    )
     xg.finish()
 
 
-def gather_all(n, x, a1, a2, wo, wd, gt):
+def gather_all(n, lengths, x, wq, wk, wv, wg, wu, wo, wd, gn):
     groups = n // GROUP
-    r = a1.shape[1]
+    r = wq.shape[0]
+    wide = 2 * wg.shape[1] // GROUP
     return pl.pallas_call(
         functools.partial(gather_kernel, n),
         out_shape=(
             SDS((GROUP, BLOCK, D), BF16),
-            SDS((groups, GROUP, r, a1.shape[-1]), BF16),
-            SDS((GROUP, r, a2.shape[-1]), BF16),
+            SDS((groups, GROUP, r, QKV), BF16),
+            SDS((GROUP, r, wide), BF16),
             SDS((groups,) + wo.shape, BF16),
             SDS((groups,) + wd.shape, BF16),
-            SDS((groups, GROUP, 8, 128), F32),
+            SDS((1, gn.shape[1] * n), F32),
+            SDS((HEAD, ROWS), F32),
         ),
-        in_specs=[ANY] * 6,
-        out_specs=(ANY,) * 6,
-        scratch_shapes=[
+        in_specs=[SM] + [HB] * 9,
+        out_specs=(HB,) * 5 + (VM, VM),
+        scratch_shapes=[pltpu.VMEM(w.shape, BF16) for w in (x, gn, wq, wk, wv, wo, wd, wg, wu)]
+        + [
+            pltpu.VMEM((GROUP, r, QKV), BF16),
+            pltpu.VMEM((GROUP, r, wide), BF16),
+            pltpu.VMEM((8, 128), F32),
+            pltpu.VMEM((groups, GROUP, 8, 128), F32),
+            DMA((9,)),
             DMA((7,)),
             DMA((14,)),
             DMA((14,)),
@@ -416,9 +474,9 @@
             DMA((4, ring_count(n))),
             DMA((4, ring_count(n))),
         ],
-        compiler_params=pltpu.CompilerParams(collective_id=1, has_side_effects=True),
+        compiler_params=pltpu.CompilerParams(collective_id=1, has_side_effects=True, vmem_limit_bytes=VMEM_LIMIT),
         name="gather_all",
-    )(x, a1, a2, wo, wd, gt)
+    )(lengths, x, wq, wk, wv, wg, wu, wo, wd, gn)
 
 
 def swap_halves(v):
@@ -434,6 +492,14 @@
     a = jnp.sum(jnp.where(low, v, 0.0), axis=-1, keepdims=True)
     b = jnp.sum(jnp.where(low, 0.0, v), axis=-1, keepdims=True)
     return jnp.where(low, a, b) * (1.0 / HEAD)
+
+
+def head_gains(g_ref):
+    t = g_ref[:, 2 * D :]
+    t = jnp.broadcast_to(t, (8, 128))
+    lane = lax.broadcasted_iota(jnp.int32, (8, 128), 1)
+    other = pltpu.roll(t, HEAD, 1)
+    return jnp.where(lane < HEAD, t, other)[0:1, :], jnp.where(lane < HEAD, other, t)[0:1, :]
 
 
 def seq_start(row, len_ref, g):
@@ -452,7 +518,7 @@
     return jnp.concatenate([c, c, c, c], axis=1), jnp.concatenate([-s, s, -s, s], axis=1)
 
 
-def attn_fwd_kernel(n, len_ref, x_ref, w_ref, ga_ref, gqk_ref, cs_ref, dy, w2, wo, h_ref, raw_ref, q_ref, kv_ref, mix_ref, mixf_ref, lse_ref, dyo, w2o, woo, k_s, v_s, acc, ls, ds_, dr, os_, orr, zs, zr):
+def attn_fwd_kernel(n, len_ref, x_ref, w_ref, g_ref, cs_ref, dy_, w2_, wo_, h_ref, raw_ref, q_ref, kv_ref, mix_ref, mixf_ref, lse_ref, dyo, w2o, woo, k_s, v_s, acc, dy, w2, wo, fs, ls, ds_, dr, os_, orr, zs, zr):
     i = pl.program_id(0)
     me, p, g, groups, zq, zg = places(n)
     hd, hw, ho = halves(BLOCK), halves(w2.shape[0]), halves(wo.shape[0])
@@ -462,9 +528,13 @@
 
     @pl.when(i == 0)
     def _():
+        fetch = bring(((dy_, dy), (w2_, w2), (wo_, wo)), fs)
         barrier([me ^ m for m in (1, 2, 4)] + zq)
+        fetch[1].wait()
+        zg_.start()
+        fetch[0].wait()
         dg.start()
-        zg_.start()
+        fetch[2].wait()
         og.start()
 
     @pl.when(i == 3)
@@ -487,15 +557,16 @@
 
     xb = x_ref[0].astype(F32)
     r = lax.rsqrt(jnp.mean(xb * xb, axis=-1, keepdims=True) + EPSILON)
-    h = (xb * r * ga_ref[...]).astype(BF16)
+    h = (xb * r * g_ref[:, :D]).astype(BF16)
+    gq, gk = head_gains(g_ref)
     h_ref[0] = h
     raw = nn(h, w_ref[...])
     raw_ref[0] = raw
     ct, st = tables(cs_ref)
     qraw, kvraw = raw[:, :128], raw[:, 128:]
-    qn = qraw * lax.rsqrt(head_mean(qraw * qraw) + EPSILON) * gqk_ref[0:1, :]
+    qn = qraw * lax.rsqrt(head_mean(qraw * qraw) + EPSILON) * gq
     q = (qn * ct + swap_halves(qn) * st).astype(BF16)
-    kn = kvraw * lax.rsqrt(head_mean(kvraw * kvraw) + EPSILON) * gqk_ref[1:2, :]
+    kn = kvraw * lax.rsqrt(head_mean(kvraw * kvraw) + EPSILON) * gk
     k = (kn * ct + swap_halves(kn) * st).astype(BF16)
     lane = lax.broadcasted_iota(jnp.int32, (BLOCK, 128), 1)
     kv = jnp.where(lane < HEAD, k.astype(F32), kvraw).astype(BF16)
@@ -537,7 +608,7 @@
         og.finish()
 
 
-def attn_fwd(n, lengths, x_all, wqkv, ga, gqk, cs, dy, w2, wo):
+def attn_fwd(n, lengths, x_all, wqkv, gvec, cs, dy, w2, wo):
     groups = n // GROUP
     blk = lambda c: pl.BlockSpec((1, BLOCK, c), lambda i: (i, 0, 0))
     whole = lambda s: pl.BlockSpec(s, lambda i: (0,) * len(s), pipeline_mode=pl.Buffered(1))
@@ -549,14 +620,13 @@
             SM,
             blk(D),
             whole((D, QKV)),
-            whole((1, D)),
-            whole((2, 128)),
+            whole(gvec.shape),
             pl.BlockSpec((HEAD, BLOCK), lambda i: (0, i)),
-            ANY,
-            ANY,
-            ANY,
+            HB,
+            HB,
+            HB,
         ],
-        out_specs=(blk(D), blk(QKV), blk(128), blk(128), blk(128), blk(128), pl.BlockSpec((1, 8, 2 * BLOCK), lambda i: (i, 0, 0)), ANY, ANY, ANY),
+        out_specs=(blk(D), blk(QKV), blk(128), blk(128), blk(128), blk(128), pl.BlockSpec((1, 8, 2 * BLOCK), lambda i: (i, 0, 0)), HB, HB, HB),
         out_shape=(
             SDS((nb, BLOCK, D), BF16),
             SDS((nb, BLOCK, QKV), F32),
@@ -573,6 +643,10 @@
             pltpu.VMEM((ROWS, HEAD), BF16),
             pltpu.VMEM((ROWS, 128), BF16),
             pltpu.VMEM((2 * BLOCK, 128), F32),
+            pltpu.VMEM(dy.shape, BF16),
+            pltpu.VMEM(w2.shape, BF16),
+            pltpu.VMEM(wo.shape, BF16),
+            DMA((3,)),
             DMA((5,)),
             DMA((14,)),
             DMA((14,)),
@@ -582,11 +656,11 @@
             DMA((ring_count(n),)),
         ],
         compiler_params=pltpu.CompilerParams(
-            collective_id=5, has_side_effects=True, dimension_semantics=("arbitrary",), vmem_limit_bytes=48 << 20
+            collective_id=5, has_side_effects=True, dimension_semantics=("arbitrary",), vmem_limit_bytes=VMEM_LIMIT
         ),
         cost_estimate=pl.CostEstimate(flops=4 * 10**9, bytes_accessed=16 << 20, transcendentals=4 * 10**6),
         name="attn_fwd",
-    )(lengths, x_all, wqkv, ga, gqk, cs, dy, w2, wo)
+    )(lengths, *in_hbm(x_all, wqkv, gvec, cs), dy, w2, wo)
 
 
 def norm_back(dyv, xv, gain):
@@ -597,15 +671,24 @@
     return dx, jnp.sum(dyv * xr, axis=0, keepdims=True)
 
 
-def ffn_block_kernel(n, inv, mix, x, wo, gf, w2, wd, dy, res, gmid, dgf, dwo, dmh, po, dw2, dwd, mbuf, h2, wgs, wds, dys, acts, dgus, part, mown, stage, ps, pr, hs, hr, os_, qs, qr, *red_refs):
+def ffn_block_kernel(n, order, mix, x_, wo_, g_ref, w2_, wd_, dy_, res, gmid, dgf, dwo, dmh, po, dw2, od, x, wo, w2, wd, dy, fs, mbuf, h2, wgs, wds, dys, acts, dgus, part, mown, stage, dwd, ps, pr, hs, hr, os_, qs, qr, *red_refs):
     me, p, g, groups, zq, zg = places(n)
-    barrier([me ^ m for m in range(1, GROUP)])
+    barrier([me ^ m for m in range(1, GROUP)] + zq)
+    fetch = bring(((w2_, w2), (wd_, wd), (x_, x), (wo_, wo), (mix.at[p], mbuf.at[p]), (dy_, dy)), fs)
+    gf = g_ref.at[:, D : 2 * D]
+
+    def holder(q):
+        s = 0
+        for k in range(ROWS // SLOT):
+            s = jnp.where(order[g, k] == q, k, s)
+        return s
+
     fl = wd.shape[0]
     fp = wds.shape[0]
     pc = start_all(
         [rcopy(mix.at[p ^ m], mbuf.at[p], ps.at[m - 1], pr.at[m - 1], me ^ m) for m in range(1, GROUP)]
     )
-    mbuf[p] = mix[p]
+    wait_all(fetch[:2])
     gap = jnp.zeros((D, fp - fl), BF16)
     wgs[:, :fl] = w2[:, :fl]
     wgs[:, fl:fp] = gap
@@ -615,6 +698,7 @@
     wds[fl:] = jnp.zeros((fp - fl, D), BF16)
     for c in pc:
         c.wait_recv()
+    wait_all(fetch[2:5])
     m = jnp.concatenate([mbuf[b] for b in range(GROUP)], axis=1)
     mown[...] = m
     z = x[...].astype(F32) + nn(m, wo[...])
@@ -623,8 +707,10 @@
     h2[p] = (z * r * gf[...]).astype(BF16)
     hb = halves(BLOCK)
     hg = PlaneGather(me, p, lambda h: h2.at[p, hb(h)], lambda b, h: h2.at[b, hb(h)], hs, hr)
-    red = PlaneReduce(me, lambda b: part.at[b], *red_refs)
+    red = PlaneReduce(me, lambda b: part.at[b], *red_refs[:7])
+    ring = RingReduce(n, p, g, dwd, *red_refs[7:])
     hg.start_first()
+    fetch[5].wait()
 
     def block(t, carry):
         @pl.when(t == 1)
@@ -663,7 +749,7 @@
 
         b = p ^ t
         h = h2[b]
-        dyb = jnp.concatenate([dy[inv[2 * b]], dy[inv[2 * b + 1]]], axis=0)
+        dyb = jnp.concatenate([dy[holder(2 * b)], dy[holder(2 * b + 1)]], axis=0)
         dys[b] = dyb
         gu = nn(h, wgs[...])
         da = nt(dyb, wds[...])
@@ -681,7 +767,11 @@
     lax.fori_loop(0, GROUP, block, 0)
     red.first[3].start()
     a_all = acts[...].reshape(ROWS, fp)
-    dwd[...] = tn(a_all, dys[...].reshape(ROWS, D))[:fl].astype(BF16)
+    dw = tn(a_all, dys[...].reshape(ROWS, D))[:fl].astype(BF16)
+    each = fl // groups
+    for k in range(groups):
+        dwd[k] = dw[k * each : (k + 1) * each].reshape(dwd.shape[1:])
+    ring.start()
     red.chip_d()
 
     def out(b, carry):
@@ -703,6 +793,7 @@
     dg_all = dgus[...].reshape(ROWS, 2 * fp)
     dw2[:, :fl] = tn(h_all, dg_all[:, :fp])[:, :fl].astype(BF16)
     dw2[:, fl:] = tn(h_all, dg_all[:, fp:])[:, :fl].astype(BF16)
+    ring.relay()
     dx, dgain = norm_back(red.phase3(), res[...], gf[...])
     dyo = dys[p].astype(F32)
     gm = dyo + dx
@@ -721,10 +812,12 @@
     dwo[...] = tn(mown[...], gl).astype(BF16)
     wait_all(qc)
     hg.sent()
-
-
-def ffn_block(n, inv, mix, x, wo, gf, w2, wd, dy):
+    od[...] = ring.finish()
+
+
+def ffn_block(n, order, mix, x, wo, gvec, w2, wd, dy, blk):
     fl = wd.shape[0]
+    groups = n // GROUP
     fp = -(-fl // 128) * 128
     vm = lambda *s: pltpu.VMEM(s, BF16)
     return pl.pallas_call(
@@ -737,11 +830,17 @@
             SDS((GROUP, BLOCK, 128), BF16),
             SDS((GROUP, BLOCK, D), BF16),
             SDS((D, 2 * fl), BF16),
-            SDS((fl, D), BF16),
+            SDS(blk, F32),
         ),
-        in_specs=[SM] + [VM] * 7,
-        out_specs=(VM, VM, VM, VM, VM, ANY, VM, VM),
+        in_specs=[SM, HB, HB, HB, VM, HB, HB, HB],
+        out_specs=(VM, VM, VM, VM, VM, HB, VM, VM),
         scratch_shapes=[
+            vm(BLOCK, D),
+            vm(D, D),
+            vm(D, 2 * fl),
+            vm(fl, D),
+            vm(ROWS // SLOT, SLOT, D),
+            DMA((6,)),
             vm(GROUP, BLOCK, 128),
             vm(GROUP, BLOCK, D),
             vm(D, 2 * fp),
@@ -752,6 +851,7 @@
             vm(GROUP, BLOCK, D),
             vm(BLOCK, D),
             vm(2, BLOCK, D),
+            vm(groups, *blk),
             DMA((7,)),
             DMA((7,)),
             DMA((14,)),
@@ -760,13 +860,14 @@
             DMA((7,)),
             DMA((7,)),
         ]
-        + plane_scratch((BLOCK, D)),
-        compiler_params=pltpu.CompilerParams(collective_id=2, has_side_effects=True, vmem_limit_bytes=62 << 20),
+        + plane_scratch((BLOCK, D))
+        + ring_scratch(n, blk),
+        compiler_params=pltpu.CompilerParams(collective_id=2, has_side_effects=True, vmem_limit_bytes=VMEM_LIMIT),
         name="ffn_block",
-    )(inv, mix, x, wo, gf, w2, wd, dy.reshape(ROWS // SLOT, SLOT, D))
-
-
-def attn_bwd_kernel(n, len_ref, dm_ref, q_ref, kvall_ref, lse_ref, mixf_ref, h_ref, raw_ref, w_ref, gqk_ref, cs_ref, po, res, dwo, dw2, dwd, dh_ref, dw_ref, dg_ref, result, two, t2, od, k_s, v_s, dkv, dqt, dws, *rest):
+    )(order, mix, x, wo, gvec, w2, wd, dy.reshape(ROWS // SLOT, SLOT, D))
+
+
+def attn_bwd_kernel(n, len_ref, dm_ref, q_ref, kvall_ref, lse_ref, mixf_ref, h_ref, raw_ref, w_ref, g_ref, cs_ref, po, res, dwo, dw2, dgf, dh_ref, dw_ref, gpart, result, two, t2, k_s, v_s, dkv, dqt, dws, dg_ref, *rest):
     step_id = pl.program_id(0)
     nb = ROWS // BLOCK
     i = nb - 1 - step_id
@@ -774,7 +875,6 @@
     ored = PlaneReduce(me, lambda b: po.at[b], *rest[:7])
     wred = PlaneReduce(me, lambda b: dwo.at[:, b], *rest[7:14])
     ring2 = RingReduce(n, p, g, dw2, *rest[14:20])
-    ringd = RingReduce(n, p, g, dwd, *rest[20:26])
 
     @pl.when(step_id == 0)
     def _():
@@ -782,7 +882,6 @@
         ored.start()
         ring2.start()
         wred.start()
-        ringd.start()
 
     @pl.when(step_id == 1)
     def _():
@@ -796,7 +895,6 @@
 
     @pl.when(step_id == 4)
     def _():
-        ringd.relay()
         wred.phase2()
 
 
@@ -853,8 +951,9 @@
         gy = dn * gain
         return r * (gy - vr * head_mean(gy * vr)), jnp.sum(dn * vr, axis=0, keepdims=True)
 
-    dqr, dgq = pull(dq, raw[:, :128], gqk_ref[0:1, :])
-    dkr, dgk = pull(dkvb * SCALE, raw[:, 128:], gqk_ref[1:2, :])
+    gq, gk = head_gains(g_ref)
+    dqr, dgq = pull(dq, raw[:, :128], gq)
+    dkr, dgk = pull(dkvb * SCALE, raw[:, 128:], gk)
     dg_ref[0:1, :] += dgq
     dg_ref[1:2, :] += dgk
     dqkv = jnp.concatenate([dqr, jnp.where(lane < HEAD, dkr, dkvb)], axis=1).astype(BF16)
@@ -867,10 +966,24 @@
         result[...] = (ored.phase3() + res[...]).astype(BF16)
         two[...] = wred.phase3().astype(BF16)
         t2[...] = ring2.finish().astype(BF16)
-        od[...] = ringd.finish()
-
-
-def attn_bwd(n, lengths, dmh, q, kv, lse, mixf, h, raw, wqkv, gqk, cs, po, res, dwo, dw2, dwd):
+        dga = lax.dot_general(
+            jnp.ones((8, QKV), F32),
+            w_ref[...].astype(F32) * dws[...],
+            (((1,), (1,)), ((), ())),
+            precision=lax.Precision.HIGHEST,
+            preferred_element_type=F32,
+        )
+        dga = dga[0:1, :] / g_ref[:, :D]
+        gpart[...] = jnp.zeros_like(gpart)
+        for b in range(8):
+            gpart[b : b + 1, :] = dga[:, 128 * b : 128 * (b + 1)]
+            gpart[8 + b : 9 + b, :] = dgf[:, 128 * b : 128 * (b + 1)]
+        turned = pltpu.roll(dg_ref[...], HEAD, 1)
+        low = lax.broadcasted_iota(jnp.int32, (1, 128), 1) < HEAD
+        gpart[16:17, :] = jnp.where(low, dg_ref[0:1, :] + turned[0:1, :], turned[1:2, :])
+
+
+def attn_bwd(n, lengths, dmh, q, kv, lse, mixf, h, raw, wqkv, gvec, cs, po, res, dwo, dw2, dgf):
     nb = ROWS // BLOCK
     groups = n // GROUP
     blk = lambda c: pl.BlockSpec((1, BLOCK, c), lambda i: (nb - 1 - i, 0, 0))
@@ -888,31 +1001,29 @@
             blk(D),
             blk(QKV),
             whole((D, QKV)),
-            whole((2, 128)),
+            whole(gvec.shape),
             pl.BlockSpec((HEAD, BLOCK), lambda i: (0, nb - 1 - i)),
             whole(po.shape),
             whole(res.shape),
             whole(dwo.shape),
             whole(dw2.shape),
-            whole(dwd.shape),
+            whole(dgf.shape),
         ],
         out_specs=(
             blk(D),
             whole((D, QKV)),
-            whole((8, 128)),
+            whole((24, 128)),
             whole((BLOCK, D)),
             whole((groups,) + dwo.shape[2:]),
             whole(dw2.shape[1:]),
-            whole(dwd.shape[1:]),
         ),
         out_shape=(
             SDS((nb, BLOCK, D), BF16),
             SDS((D, QKV), BF16),
-            SDS((8, 128), F32),
+            SDS((24, 128), F32),
             SDS((BLOCK, D), BF16),
             SDS((groups,) + dwo.shape[2:], BF16),
             SDS(dw2.shape[1:], BF16),
-            SDS(dwd.shape[1:], F32),
         ),
         scratch_shapes=[
             pltpu.VMEM((ROWS, HEAD), BF16),
@@ -920,27 +1031,29 @@
             pltpu.VMEM((ROWS, 128), F32),
             pltpu.VMEM((2 * BLOCK, HEAD), F32),
             pltpu.VMEM((D, QKV), F32),
+            pltpu.VMEM((8, 128), F32),
         ]
         + plane_scratch((BLOCK, D))
         + plane_scratch((groups,) + dwo.shape[2:])
-        + ring_scratch(n, dw2.shape[1:])
-        + ring_scratch(n, dwd.shape[1:]),
+        + ring_scratch(n, dw2.shape[1:]),
         compiler_params=pltpu.CompilerParams(
-            collective_id=6, has_side_effects=True, dimension_semantics=("arbitrary",), vmem_limit_bytes=60 << 20
+            collective_id=6, has_side_effects=True, dimension_semantics=("arbitrary",), vmem_limit_bytes=VMEM_LIMIT
         ),
         cost_estimate=pl.CostEstimate(flops=8 * 10**9, bytes_accessed=16 << 20, transcendentals=4 * 10**6),
         name="attn_bwd",
-    )(lengths, dmh, q, kv, lse, mixf, h, raw, wqkv, gqk, cs, po, res, dwo, dw2, dwd)
-
-
-def final_kernel(n, dh, x, gmid, ga, dgf, dgqk, dw1, two, t2, gtok, o1, o2, oo, og, t1, gpart, gin, gsum, gz, ps, pr, gs, gr, *rest):
+    )(lengths, dmh, q, kv, lse, mixf, h, raw, wqkv, gvec, cs, po, res, dwo, dw2, dgf)
+
+
+def final_kernel(n, dh, x, gmid, g_ref, dw1, two, t2, gpart, gtok, o1, o2, oo, og, t1, gin, gsum, gz, ps, pr, gs, gr, *rest):
     me, p, g, groups, zq, zg = places(n)
     nz = groups - 1
+    share = g_ref.shape[1] // n
     barrier([me ^ m for m in range(1, GROUP)] + zq)
     red = PlaneReduce(me, lambda b: dh.at[b], *rest[:7])
     ring1 = RingReduce(n, p, g, dw1, *rest[7:13])
     ringo = RingReduce(n, p, g, two, *rest[13:19])
     red.start()
+    gc = start_all([rcopy(gpart, gin.at[m - 1], gs.at[m - 1], gr.at[m - 1], me ^ m) for m in range(1, GROUP)])
     ring1.start()
     ringo.start()
     pc = []
@@ -954,40 +1067,38 @@
 
     red.phase1()
     exchange(1, t2, o2)
-    ring1.relay()
-    ringo.relay()
-    red.phase2()
-    t1[...] = ring1.finish().astype(BF16)
-    exchange(0, t1, o1)
-    dx, dga = norm_back(red.phase3(), x[...].astype(F32), ga[...])
-    gtok[...] = gmid[...] + dx
-    gpart[...] = jnp.zeros_like(gpart)
-    for b in range(8):
-        gpart[b : b + 1, :] = dga[:, 128 * b : 128 * (b + 1)]
-        gpart[8 + b : 9 + b, :] = dgf[:, 128 * b : 128 * (b + 1)]
-    lane = lax.broadcasted_iota(jnp.int32, (1, 128), 1)
-    dgq = dgqk[0:1, :]
-    dgq = dgq + pltpu.roll(jnp.broadcast_to(dgq, (8, 128)), HEAD, 1)[0:1, :]
-    dgk = pltpu.roll(jnp.broadcast_to(dgqk[1:2, :], (8, 128)), HEAD, 1)[0:1, :]
-    gpart[16:17, :] = jnp.where(lane < HEAD, dgq, dgk)
-    gc = start_all([rcopy(gpart, gin.at[m - 1], gs.at[m - 1], gr.at[m - 1], me ^ m) for m in range(1, GROUP)])
-    oo[...] = ringo.finish()
     tot = gpart[...]
     for m in range(1, GROUP):
         gc[m - 1].wait_recv()
         tot = tot + gin[m - 1]
     gsum[...] = tot
     gzc = start_all([rcopy(gsum, gz.at[s], gs.at[7 + s], gr.at[7 + s], zq[s]) for s in range(nz)])
+    ring1.relay()
+    ringo.relay()
+    red.phase2()
+    t1[...] = ring1.finish().astype(BF16)
+    exchange(0, t1, o1)
+    oo[...] = ringo.finish()
     for s in range(nz):
         gzc[s].wait_recv()
         tot = tot + gz[s]
-    og[...] = tot
+    gsum_row = me * share
+    for c in gzc:
+        c.wait_send()
+    gsum[...] = tot
+    first = gsum_row // 128
+    off = lax.rem(gsum_row, 128)
+    lane = lax.broadcasted_iota(jnp.int32, (8, 128), 1)
+    turn = lambda row: pltpu.roll(jnp.broadcast_to(gsum[pl.ds(row, 1), :], (8, 128)), lax.rem(128 - off, 128), 1)
+    og[...] = jnp.where(lane < 128 - off, turn(first), turn(first + 1))
+    dx, _ = norm_back(red.phase3(), x[...].astype(F32), g_ref[:, :D])
+    gtok[...] = gmid[...] + dx
     wait_all(pc)
-    for c in gc + gzc:
+    for c in gc:
         c.wait_send()
 
 
-def final(n, dh, x, gmid, ga, dgf, dgqk, dw1, two, t2):
+def final(n, dh, x, gmid, gvec, dw1, two, t2, gpart):
     groups = n // GROUP
     nz = groups - 1
     return pl.pallas_call(
@@ -997,13 +1108,12 @@
             SDS(dw1.shape[1:], BF16),
             SDS(t2.shape, BF16),
             SDS(two.shape[1:], F32),
-            SDS((24, 128), F32),
+            SDS((8, 128), F32),
         ),
-        in_specs=[VM] * 9,
+        in_specs=[VM] * 8,
         out_specs=(VM,) * 5,
         scratch_shapes=[
             pltpu.VMEM(dw1.shape[1:], BF16),
-            pltpu.VMEM((24, 128), F32),
             pltpu.VMEM((7, 24, 128), F32),
             pltpu.VMEM((24, 128), F32),
             pltpu.VMEM((nz, 24, 128), F32),
@@ -1015,62 +1125,87 @@
         + plane_scratch((BLOCK, D))
         + ring_scratch(n, dw1.shape[1:])
         + ring_scratch(n, two.shape[1:]),
-        compiler_params=pltpu.CompilerParams(collective_id=4, has_side_effects=True, vmem_limit_bytes=58 << 20),
+        compiler_params=pltpu.CompilerParams(collective_id=4, has_side_effects=True, vmem_limit_bytes=VMEM_LIMIT),
         name="final",
-    )(dh, x, gmid, ga, dgf, dgqk, dw1, two, t2)
+    )(dh, x, gmid, gvec, dw1, two, t2, gpart)
+
+
+def unpack_kernel(groups, result, gtok, o1, o2, oo, od, og, result_o, gtok_o, gq, gk, gv, go, gg, gu, gd, gn):
+    result_o[...] = result[...]
+    gtok_o[...] = gtok[...]
+    go[...] = oo[...]
+    gd[...] = od[...]
+    gn[...] = og[0:1, : gn.shape[1]]
+    for b in range(GROUP):
+        gq[:, 128 * b : 128 * (b + 1)] = o1[b, :, :128].astype(F32)
+    for out, at in ((gk, slice(128, 128 + HEAD)), (gv, slice(128 + HEAD, 256))):
+        for c in range(GROUP // 2):
+            pair = [o1[2 * c + k, :, at].astype(F32) for k in range(2)]
+            out[:, 128 * c : 128 * (c + 1)] = jnp.concatenate(pair, axis=1)
+    ffc = gg.shape[1] // (groups * GROUP)
+    for k, out in enumerate((gg, gu)):
+        parts = [
+            o2[b, :, (k * groups + c) * ffc : (k * groups + c + 1) * ffc].astype(F32)
+            for c in range(groups)
+            for b in range(GROUP)
+        ]
+        out[...] = jnp.concatenate(parts, axis=1)
+
+
+def unpack(n, result, gtok, o1, o2, oo, od, og, share):
+    r = oo.shape[0]
+    return pl.pallas_call(
+        functools.partial(unpack_kernel, n // GROUP),
+        out_shape=(
+            SDS(result.shape, BF16),
+            SDS(gtok.shape, F32),
+            SDS((r, D), F32),
+            SDS((r, D // 2), F32),
+            SDS((r, D // 2), F32),
+            SDS((r, D), F32),
+            SDS((r, FF), F32),
+            SDS((r, FF), F32),
+            SDS(od.shape, F32),
+            SDS((1, share), F32),
+        ),
+        in_specs=[VM] * 7,
+        out_specs=(VM,) * 10,
+        compiler_params=pltpu.CompilerParams(vmem_limit_bytes=VMEM_LIMIT),
+        name="unpack",
+    )(result, gtok, o1, o2, oo, od, og)
 
 
 def body(n, tokens, w_query, key_weight, w_value, w_out, w_gate, w_up, w_down, norm_gains, seq_lengths, slot_order, out_grad):
     groups = n // GROUP
     r = w_query.shape[0]
     ffc = w_down.shape[0]
-    device = lax.axis_index("dp")
-    g, p = device // GROUP, device % GROUP
-    lengths = seq_lengths
-    a1 = jnp.concatenate(
-        [
-            w_query.reshape(r, GROUP, 128),
-            key_weight.reshape(r, GROUP, HEAD),
-            w_value.reshape(r, GROUP, HEAD),
-        ],
-        axis=2,
-    ).transpose(1, 0, 2)
-    wgu = jnp.stack([w_gate, w_up], axis=1).reshape(r, 2, groups, GROUP, ffc)
-    a2 = wgu.transpose(3, 0, 1, 2, 4).reshape(GROUP, r, 2 * groups * ffc)
     share = norm_gains.shape[0]
-    gt = jnp.pad(norm_gains.astype(F32)[None, :], ((0, 7), (0, 128 - share)))
     wok = r // 16 if r % 16 == 0 else 1
     wdk = ffc // 16 if ffc % 16 == 0 else 1
-    x_all, w1, w2, wo, wd, gains = gather_all(
-        n, tokens, a1, a2, w_out.reshape(wok, r // wok, D), w_down.reshape(wdk, ffc // wdk, D), gt
+    wo_blk, wd_blk = (wok, r // wok, D), (wdk, ffc // wdk, D)
+    x_all, w1, w2, wo, wd, gvec, cs = gather_all(
+        n,
+        seq_lengths,
+        tokens,
+        w_query,
+        key_weight,
+        w_value,
+        w_gate,
+        w_up,
+        w_out.reshape(wo_blk),
+        w_down.reshape(wd_blk),
+        norm_gains.reshape(1, share),
     )
-    gains = gains[:, :, 0, :share].reshape(1, -1)
-    ga, gf = gains[:, :D], gains[:, D : 2 * D]
-    gq = gains[:, 2 * D : 2 * D + HEAD]
-    gk = gains[:, 2 * D + HEAD :]
-    gqk = jnp.concatenate([jnp.concatenate([gq, gq], axis=1), jnp.concatenate([gk, gk], axis=1)], axis=0)
     wqkv = w1.reshape(D, QKV)
-    wd = wd.reshape(-1, D)
-    row = jnp.arange(ROWS, dtype=jnp.int32)
-    length_row = lax.dynamic_index_in_dim(seq_lengths, g, 0, keepdims=False)
-    order_row = lax.dynamic_index_in_dim(slot_order, g, 0, keepdims=False)
-    ends = jnp.cumsum(length_row)
-    start = jnp.max(jnp.where(row[:, None] >= ends[None, :], ends[None, :], 0), axis=1)
-    frequency = jnp.exp(jnp.arange(HEAD // 2, dtype=F32) * (-2.0 * math.log(ROPE_THETA) / HEAD))
-    angles = frequency[:, None] * (row - start).astype(F32)[None, :]
-    cs = jnp.concatenate([jnp.cos(angles), jnp.sin(angles)], axis=0)
-    slots = jnp.arange(ROWS // SLOT, dtype=jnp.int32)
-    inv = jnp.sum(jnp.where(order_row[None, :] == slots[:, None], slots[None, :], 0), axis=1)
-
     h, raw, q, kv, mix, mixf, lse, dy_all, w2, wo = attn_fwd(
-        n, lengths, x_all, wqkv, ga, gqk, cs, out_grad, w2, wo.reshape(groups, r, D)
+        n, seq_lengths, x_all, wqkv, gvec, cs, out_grad, w2, wo.reshape(groups, r, D)
     )
-    wgu = w2.reshape(D, -1)
-    wo = wo.reshape(D, D)
-    res, gmid, dgf, dwo, dmh, po, dwgu, dwd = ffn_block(n, inv, mix, tokens, wo, gf, wgu, wd, dy_all)
-    dh1, dwqkv, dgqk, result, two, t2, od = attn_bwd(
+    res, gmid, dgf, dwo, dmh, po, dwgu, od = ffn_block(
+        n, slot_order, mix, tokens, wo.reshape(D, D), gvec, w2.reshape(D, -1), wd.reshape(-1, D), dy_all, wd_blk
+    )
+    dh1, dwqkv, gpart, result, two, t2 = attn_bwd(
         n,
-        lengths,
+        seq_lengths,
         dmh,
         q,
         kv,
@@ -1079,35 +1214,27 @@
         h,
         raw,
         wqkv,
-        gqk,
+        gvec,
         cs,
         po,
         res,
         dwo.reshape(groups, GROUP, r, D),
         dwgu.reshape(groups, GROUP, r, -1),
-        dwd.reshape(groups, wdk, ffc // wdk, D),
+        dgf,
     )
     gtok, o1, o2, oo, og = final(
         n,
         dh1,
         tokens,
         gmid,
-        ga,
-        dgf,
-        dgqk,
+        gvec,
         dwqkv.reshape(groups, GROUP, r, QKV),
-        two.reshape(groups, wok, r // wok, D),
+        two.reshape((groups,) + wo_blk),
         t2,
+        gpart,
     )
-    oo = oo.reshape(r, D)
-    od = od.reshape(ffc, D)
-    o1 = o1.transpose(1, 0, 2).astype(F32)
-    gwq = o1[:, :, :128].reshape(r, -1)
-    gwk = o1[:, :, 128 : 128 + HEAD].reshape(r, -1)
-    gwv = o1[:, :, 128 + HEAD :].reshape(r, -1)
-    o2 = o2.reshape(GROUP, r, 2, groups, ffc).transpose(2, 1, 3, 0, 4).reshape(2, r, -1).astype(F32)
-    gains_out = lax.dynamic_slice(og.reshape(-1), (device * share,), (share,))
-    return result, gtok, gwq, gwk, gwv, oo, o2[0], o2[1], od, gains_out
+    outs = unpack(n, result, gtok, o1, o2, oo.reshape(r, D), od.reshape(ffc, D), og, share)
+    return outs[:-1] + (outs[-1].reshape(share),)
 
 
 def solution(mesh):

time: 309 us -> 250 us (0.81)
  local copies, waits for them, and re-layouts: 31.3 us -> 0 us
  Pallas kernels: 270 us -> 249 us
  other arithmetic: 5.69 us -> 0 us
    pallas_call x1, Pallas kernels: 69.5 us -> 51.4 us  [attn_bwd(): pl.pallas_call(functools.partial(attn_bwd_kernel, n), grid=(nb,), in_spec...]
    unnamed x44 -> x0, local copies, waits for them, and re-layouts: 11.4 us -> none
    pallas_call x1, Pallas kernels: 43.3 us -> 37.1 us  [final(): pl.pallas_call(functools.partial(final_kernel, n), out_shape=(SDS((BLOCK,...]
    reshape x9 -> x0, local copies, waits for them, and re-layouts: 5.77 us -> none  [the longest x1 1.89 us: body(): a2 = wgu.transpose(3, 0, 1, 2, 4).reshape(GROUP, r, 2 * groups * ffc)]
    pallas_call x0 -> x1, Pallas kernels: none -> 3.93 us  [unpack(): pl.pallas_call(functools.partial(unpack_kernel, n // GROUP), out_shape=(S...]
    slice x9 -> x0, local copies, waits for them, and re-layouts: 3.46 us -> none  [the longest x3 1.58 us: body(): return (result, gtok, gwq, gwk, gwv, oo, o2[0], o2[1], od, gains_out)]
where the time goes in v4:
time: 250 us
  Pallas kernels  249 us (100%)
    pallas_call x1, Pallas kernels, ffn_block(): pl.pallas_call(functools.partial(ffn_block_kernel, n), out_shape=(SDS((BL...  68.8 us
    pallas_call x1, Pallas kernels, attn_bwd(): pl.pallas_call(functools.partial(attn_bwd_kernel, n), grid=(nb,), in_spec...  51.4 us
    pallas_call x1, Pallas kernels, attn_fwd(): pl.pallas_call(functools.partial(attn_fwd_kernel, n), grid=(nb,), in_spec...  44.2 us
    pallas_call x1, Pallas kernels, gather_all(): pl.pallas_call(functools.partial(gather_kernel, n), out_shape=(SDS((GROUP...  43.6 us
    pallas_call x1, Pallas kernels, final(): pl.pallas_call(functools.partial(final_kernel, n), out_shape=(SDS((BLOCK,...  37.1 us

profile of v4, /device:TPU:0, one launch (start us, length us, event | category | flops | bytes accessed | tf_op | source)
XLA Modules:
  0.0 249.7 jit_solution(10822518320604600674)
XLA Ops:
  0.6 43.6 %gather_all.1 = (bf16[8,256,1024]{2,1,0:T(8,128)(2,1)}, bf16[4,8,32,256]{3,2,1,0:T(8,128)(2,1)}, bf16[8,32,1152]{2,1,0:T(8,128)(2,1)}, bf16[4,2,16,1024]{3,2,1,0...) custom-call(s32[4,4]{1,0:T(4,128)} %len_ref.5, bf16[256,1024]{1,0:T(8,128)(2,1)} %x.1, ...), custom_call_target="tpu_custom_call" | custom-call | tf_op jit(solution)/shard_map/gather_all/pallas_call | solution.py:449
  44.2 44.2 %attn_fwd.1 = (bf16[8,256,1024]{2,1,0:T(8,128)(2,1)}, f32[8,256,256]{2,1,0:T(8,128)}, bf16[8,256,128]{2,1,0:T(8,128)(2,1)}, bf16[8,256,128]{2,1,0:T(8,128)(2,1)}...) custom-call(s32[4,4]{1,0:T(4,128)} %len_ref.5, ...), custom_call_target="tpu_custom_call" | custom-call | flops 4000000000 | bytes 16777216 | tf_op jit(solution)/shard_map/attn_fwd/pallas_call | solution.py:616
  88.5 68.8 %ffn_block.1 = (f32[256,1024]{1,0:T(8,128)}, f32[256,1024]{1,0:T(8,128)}, f32[1,1024]{1,0:T(1,128)}, bf16[1024,1024]{1,0:T(8,128)(2,1)}, bf16[8,256,128]{2,1,0:T...) custom-call(s32[4,16]{1,0:T(4,128)} %order.1, ...), custom_call_target="tpu_custom_call" | custom-call | tf_op jit(solution)/shard_map/ffn_block/pallas_call | solution.py:823
  157.2 51.4 %attn_bwd.1 = (bf16[8,256,1024]{2,1,0:T(8,128)(2,1)}, bf16[1024,256]{1,0:T(8,128)(2,1)}, f32[24,128]{1,0:T(8,128)}, bf16[256,1024]{1,0:T(8,128)(2,1)}, bf16[4,32...) custom-call(s32[4,4]{1,0:T(4,128)} %len_ref.5, bf16[8,256,128]{2,1,0:T(8,128)(2,1)} %get-tuple-element.67.dm_ref, ...), custom_call_target="tpu_custom_call" | custom-call | flops 8000000000 | bytes 16777216 | tf_op jit(solution)/shard_map/attn_bwd/pallas_call | solution.py:991
  208.6 37.1 %final.1 = (f32[256,1024]{1,0:T(8,128)}, bf16[8,32,256]{2,1,0:T(8,128)(2,1)}, bf16[8,32,1152]{2,1,0:T(8,128)(2,1)}, f32[2,16,1024]{2,1,0:T(8,128)}, f32[8,128]{1,0:T(8,128)}) custom-call(bf16[8,256,1024]{2,1,0:T(8,128)(2,1)} %get-tuple-element.80.dh, bf16[256,1024]{1,0:T(8,128)(2,1)} %x.1, f32[256,1024]{1,0:T(8,128)} %get-tuple-element.81.gmid, ...), custom_call_target="tpu_custom_call" | custom-call | tf_op jit(solution)/shard_map/final/pallas_call | solution.py:1104
  245.8 3.9 %unpack.1 = (bf16[256,1024]{1,0:T(8,128)(2,1)}, f32[256,1024]{1,0:T(8,128)}, f32[32,1024]{1,0:T(8,128)}, f32[32,512]{1,0:T(8,128)}, f32[32,512]{1,0:T(8,128)}, /...) custom-call(bf16[256,1024]{1,0:T(8,128)(2,1)} %get-tuple-element.79.r, ...), custom_call_target="tpu_custom_call" | custom-call | tf_op jit(solution)/shard_map/unpack/pallas_call | solution.py:1157

commit v5 on v4

--- a/solution.py
+++ b/solution.py
@@ -199,10 +199,10 @@
     return max(6, n // GROUP - 1)
 
 
-def halves(length):
+def halves(length, base=0):
     cut = length // 2
-    part = (pl.ds(0, cut), pl.ds(cut, length - cut))
-    return lambda h: slice(None) if h is None else part[h]
+    part = (pl.ds(base, cut), pl.ds(base + cut, length - cut))
+    return lambda h: pl.ds(base, length) if h is None else part[h]
 
 
 class RingReduce:
@@ -347,7 +347,7 @@
     ]
 
 
-def gather_kernel(n, len_ref, x_, wq_, wk_, wv_, wg_, wu_, wo_, wd_, gn_, xo, a1o, a2o, woo, wdo, gvec, cs, x, gn, wq, wk, wv, wo, wd, wg, wu, a1, a2, gt, gto, fs, ls, xs, xr, ps, pr, zs, zr):
+def gather_kernel(n, len_ref, x_, wq_, wk_, wv_, wg_, wu_, wo_, wd_, gn_, xo, a1o, b1o, b2o, woo, wdo, gvec, ct, st, x, gn, wq, wk, wv, wo, wd, wg, wu, a1, b1, b2, gt, gto, fs, ls, xs, xr, ps, pr, zs, zr):
     me, p, g, groups, zq, zg = places(n)
     fetch = bring(
         (
@@ -357,7 +357,7 @@
             (wk_, wk),
             (wv_, wv),
             (wo_, wo),
-            (wd_, wd),
+            (wd_.at[pl.ds(0, wd.shape[0])], wd),
             (wg_, wg),
             (wu_, wu),
         ),
@@ -365,6 +365,7 @@
     )
     share = gn.shape[1]
     ffc = wg.shape[1] // (groups * GROUP)
+    big = 2 * ffc // 3
     barrier([me ^ m for m in range(1, GROUP)] + zq)
     hx = halves(BLOCK)
     xg = PlaneGather(me, p, lambda h: x.at[hx(h)], lambda b, h: xo.at[b, hx(h)], xs, xr, ls.at[pl.ds(5, 2)])
@@ -403,14 +404,17 @@
     rings[3].start()
     rings[2].start()
     wait_all(fetch[7:])
-    for b in range(GROUP):
-        at = [slice((GROUP * k + b) * ffc, (GROUP * k + b + 1) * ffc) for k in range(groups)]
-        a2[b] = jnp.concatenate([wg[:, k] for k in at] + [wu[:, k] for k in at], axis=1)
-    exchange(2, lambda b: a2.at[b], a2o.at[p])
+    for buf, low, high in ((b1, 0, big), (b2, big, ffc)):
+        for b in range(GROUP):
+            at = [slice((GROUP * k + b) * ffc + low, (GROUP * k + b) * ffc + high) for k in range(groups)]
+            buf[b] = jnp.concatenate([wg[:, k] for k in at] + [wu[:, k] for k in at], axis=1)
+    exchange(2, lambda b: b1.at[b], b1o.at[p])
+    exchange(3, lambda b: b2.at[b], b2o.at[p])
     xg.start_second()
     local = [
         pltpu.make_async_copy(a1.at[p], a1o.at[g, p], ls.at[0]),
-        pltpu.make_async_copy(a2.at[p], a2o.at[p], ls.at[2]),
+        pltpu.make_async_copy(b1.at[p], b1o.at[p], ls.at[2]),
+        pltpu.make_async_copy(b2.at[p], b2o.at[p], ls.at[1]),
     ]
     start_all(local)
     local[0].wait()
@@ -423,15 +427,17 @@
     position = (row - seq_start(row, len_ref, g)).astype(F32)
     index = lax.broadcasted_iota(jnp.int32, (HEAD // 2, 1), 0).astype(F32)
     angles = jnp.exp(index * (-2.0 * math.log(ROPE_THETA) / HEAD)) * position
-    cs[: HEAD // 2] = jnp.cos(angles)
-    cs[HEAD // 2 :] = jnp.sin(angles)
+    c, s = jnp.cos(angles).T, jnp.sin(angles).T
+    ct[...] = jnp.concatenate([c, c, c, c], axis=1)
+    st[...] = jnp.concatenate([-s, s, -s, s], axis=1)
     xg.relay2()
     for k in (3, 0, 1, 2):
         rings[k].relay()
     xg.relay3()
-    for m in range(1, GROUP):
-        pc[2, m].wait_recv()
-    local[1].wait()
+    for k in (2, 3):
+        for m in range(1, GROUP):
+            pc[k, m].wait_recv()
+    wait_all(local[1:])
     for c in pc.values():
         c.wait_send()
     for k in range(4):
@@ -446,31 +452,39 @@
     groups = n // GROUP
     r = wq.shape[0]
     wide = 2 * wg.shape[1] // GROUP
+    wide1 = 2 * wide // 3
+    wd1 = (2 * wd.shape[0] // 3,) + wd.shape[1:]
     return pl.pallas_call(
         functools.partial(gather_kernel, n),
         out_shape=(
             SDS((GROUP, BLOCK, D), BF16),
             SDS((groups, GROUP, r, QKV), BF16),
-            SDS((GROUP, r, wide), BF16),
+            SDS((GROUP, r, wide1), BF16),
+            SDS((GROUP, r, wide - wide1), BF16),
             SDS((groups,) + wo.shape, BF16),
-            SDS((groups,) + wd.shape, BF16),
+            SDS((groups,) + wd1, BF16),
             SDS((1, gn.shape[1] * n), F32),
-            SDS((HEAD, ROWS), F32),
+            SDS((ROWS, 128), F32),
+            SDS((ROWS, 128), F32),
         ),
         in_specs=[SM] + [HB] * 9,
-        out_specs=(HB,) * 5 + (VM, VM),
-        scratch_shapes=[pltpu.VMEM(w.shape, BF16) for w in (x, gn, wq, wk, wv, wo, wd, wg, wu)]
+        out_specs=(HB,) * 6 + (VM, VM, VM),
+        scratch_shapes=[
+            pltpu.VMEM(w, BF16)
+            for w in (x.shape, gn.shape, wq.shape, wk.shape, wv.shape, wo.shape, wd1, wg.shape, wu.shape)
+        ]
         + [
             pltpu.VMEM((GROUP, r, QKV), BF16),
-            pltpu.VMEM((GROUP, r, wide), BF16),
+            pltpu.VMEM((GROUP, r, wide1), BF16),
+            pltpu.VMEM((GROUP, r, wide - wide1), BF16),
             pltpu.VMEM((8, 128), F32),
             pltpu.VMEM((groups, GROUP, 8, 128), F32),
             DMA((9,)),
             DMA((7,)),
             DMA((14,)),
             DMA((14,)),
-            DMA((3, 7)),
-            DMA((3, 7)),
+            DMA((4, 7)),
+            DMA((4, 7)),
             DMA((4, ring_count(n))),
             DMA((4, ring_count(n))),
         ],
@@ -487,11 +501,12 @@
 
 
 def head_mean(v):
-    lane = lax.broadcasted_iota(jnp.int32, v.shape, 1)
-    low = lane < HEAD
-    a = jnp.sum(jnp.where(low, v, 0.0), axis=-1, keepdims=True)
-    b = jnp.sum(jnp.where(low, 0.0, v), axis=-1, keepdims=True)
-    return jnp.where(low, a, b) * (1.0 / HEAD)
+    row = lax.broadcasted_iota(jnp.int32, (128, 128), 0)
+    lane = lax.broadcasted_iota(jnp.int32, (128, 128), 1)
+    same = jnp.where((row < HEAD) == (lane < HEAD), 1.0 / HEAD, 0.0).astype(BF16)
+    high = v.astype(BF16)
+    low = (v - high.astype(F32)).astype(BF16)
+    return nn(high, same) + nn(low, same)
 
 
 def head_gains(g_ref):
@@ -512,44 +527,57 @@
     return jnp.where(row >= e3, zero + e3, s)
 
 
-def tables(cs_ref):
-    t = cs_ref[...].T
-    c, s = t[:, : HEAD // 2], t[:, HEAD // 2 :]
-    return jnp.concatenate([c, c, c, c], axis=1), jnp.concatenate([-s, s, -s, s], axis=1)
-
-
-def attn_fwd_kernel(n, len_ref, x_ref, w_ref, g_ref, cs_ref, dy_, w2_, wo_, h_ref, raw_ref, q_ref, kv_ref, mix_ref, mixf_ref, lse_ref, dyo, w2o, woo, k_s, v_s, acc, dy, w2, wo, fs, ls, ds_, dr, os_, orr, zs, zr):
+def windows(i, window):
+    for low, high, count in ((0, 1, 2), (2, 3, 4), (4, 7, WINDOW + 1)):
+
+        @pl.when((i >= low) & (i <= high))
+        def _():
+            window(jnp.maximum(i - WINDOW, 0), count)
+
+
+def attn_fwd_kernel(n, len_ref, x_ref, w_ref, g_ref, ct_ref, st_ref, dy_, w2_, wo_, h_ref, raw_ref, q_ref, kv_ref, mixf_ref, lse_ref, mixo, dyo, w2o, woo, k_s, v_s, acc, dy, w2, wo, mixs, fs, ls, ds_, dr, os_, orr, zs, zr, ms, mr):
     i = pl.program_id(0)
     me, p, g, groups, zq, zg = places(n)
-    hd, hw, ho = halves(BLOCK), halves(w2.shape[0]), halves(wo.shape[0])
+    hd, hw, ho = halves(BLOCK), halves(GROUP), halves(wo.shape[0])
     dg = PlaneGather(me, p, lambda h: dy.at[hd(h)], lambda b, h: dyo.at[b, hd(h)], ds_, dr, ls.at[pl.ds(0, 2)])
     og = PlaneGather(me, p, lambda h: wo.at[ho(h)], lambda b, h: woo.at[ho(h), b], os_, orr, ls.at[pl.ds(2, 2)])
-    zg_ = Ring(n, p, g, lambda h: w2.at[hw(h)], lambda b, h: w2o.at[b, hw(h)], zs, zr, ls.at[4])
+    wring = Ring(n, p, g, lambda h: w2.at[hw(h)], lambda b, h: w2o.at[b, hw(h)], zs, zr, ls.at[5])
+    fetch = [pltpu.make_async_copy(a, b, fs.at[k]) for k, (a, b) in enumerate(((dy_, dy), (wo_, wo), (w2_, w2)))]
 
     @pl.when(i == 0)
     def _():
-        fetch = bring(((dy_, dy), (w2_, w2), (wo_, wo)), fs)
-        barrier([me ^ m for m in (1, 2, 4)] + zq)
+        start_all(fetch)
+        k_s[: WINDOW * BLOCK] = jnp.zeros((WINDOW * BLOCK, HEAD), BF16)
+        v_s[: WINDOW * BLOCK] = jnp.zeros((WINDOW * BLOCK, 128), BF16)
+        barrier([me ^ m for m in range(1, GROUP)] + zq)
+        fetch[2].wait()
+        wring.start()
+        fetch[0].wait()
+        dg.start_first()
+
+    @pl.when(i == 2)
+    def _():
+        dg.start_second()
+
+    @pl.when(i == 3)
+    def _():
+        dg.relay1()
+
+    @pl.when(i == 4)
+    def _():
         fetch[1].wait()
-        zg_.start()
-        fetch[0].wait()
-        dg.start()
-        fetch[2].wait()
-        og.start()
-
-    @pl.when(i == 3)
-    def _():
-        dg.relay1()
+        og.start_first()
 
     @pl.when(i == 5)
     def _():
-        zg_.relay()
         dg.relay2()
+        wring.relay()
+        og.start_second()
 
     @pl.when(i == 6)
     def _():
+        dg.relay3()
         og.relay1()
-        dg.relay3()
 
     @pl.when(i == 7)
     def _():
@@ -562,7 +590,7 @@
     h_ref[0] = h
     raw = nn(h, w_ref[...])
     raw_ref[0] = raw
-    ct, st = tables(cs_ref)
+    ct, st = ct_ref[...], st_ref[...]
     qraw, kvraw = raw[:, :128], raw[:, 128:]
     qn = qraw * lax.rsqrt(head_mean(qraw * qraw) + EPSILON) * gq
     q = (qn * ct + swap_halves(qn) * st).astype(BF16)
@@ -575,40 +603,46 @@
     k_s[pl.ds(i * BLOCK, BLOCK), :] = kv[:, :HEAD]
     v_s[pl.ds(i * BLOCK, BLOCK), :] = jnp.where(lane < HEAD, pltpu.roll(kvraw, HEAD, 1), 1.0).astype(BF16)
     q2 = jnp.concatenate([q[:, :HEAD], q[:, HEAD:]], axis=0)
-    acc[...] = jnp.zeros_like(acc)
     row = lax.broadcasted_iota(jnp.int32, (2 * BLOCK, 1), 0)
     qrow = i * BLOCK + jnp.where(row >= BLOCK, row - BLOCK, row)
     qstart = seq_start(qrow, len_ref, g)
-    first = jnp.maximum(i - WINDOW, 0)
-    col = lax.broadcasted_iota(jnp.int32, (2 * BLOCK, BLOCK), 1)
-
-    def step(j, carry):
-        kb = k_s[pl.ds(pl.multiple_of(j * BLOCK, BLOCK), BLOCK), :]
-        vb = v_s[pl.ds(pl.multiple_of(j * BLOCK, BLOCK), BLOCK), :]
-        s = nt(q2, kb)
-        kc = col + j * BLOCK
+
+    def window(first, count):
+        at = pl.ds(pl.multiple_of(first * BLOCK, BLOCK), count * BLOCK)
+        kc = lax.broadcasted_iota(jnp.int32, (2 * BLOCK, count * BLOCK), 1) + first * BLOCK
         ok = (kc >= qstart) & (kc <= qrow)
-        e = jnp.where(ok, jnp.exp2(s * (SCALE * LOG2E)), 0.0).astype(BF16)
-        acc[...] += nn(e, vb)
-        return carry
-
-    lax.fori_loop(first, i + 1, step, 0)
+        e = jnp.where(ok, jnp.exp2(nt(q2, k_s[at, :]) * (SCALE * LOG2E)), 0.0).astype(BF16)
+        acc[...] = nn(e, v_s[at, :])
+
+    windows(i, window)
     total = acc[:, HEAD:]
     m = acc[:, :HEAD] / total
     both = jnp.concatenate([m[:BLOCK], m[BLOCK:]], axis=1)
     mixf_ref[0] = both
-    mix_ref[0] = both.astype(BF16)
+    mixs[i] = both.astype(BF16)
+
+    @pl.when(i == p)
+    def _():
+        pltpu.make_async_copy(mixs.at[i], mixo.at[p], ls.at[4]).start()
+
+    @pl.when(i != p)
+    def _():
+        rcopy(mixs.at[i], mixo.at[p], ms.at[p ^ i], mr.at[p ^ i], me ^ p ^ i).start()
+
     lse_ref[0] = jnp.log2(total.T)[:8, :]
 
     @pl.when(i == 7)
     def _():
         og.relay3()
         dg.finish()
-        zg_.finish()
+        wring.finish()
         og.finish()
-
-
-def attn_fwd(n, lengths, x_all, wqkv, gvec, cs, dy, w2, wo):
+        for m in range(1, GROUP):
+            rcopy(mixs.at[p ^ m], mixo.at[p], ms.at[m], mr.at[m], me ^ m).wait()
+        pltpu.make_async_copy(mixs.at[p], mixo.at[p], ls.at[4]).wait()
+
+
+def attn_fwd(n, lengths, x_all, wqkv, gvec, ct, st, dy, w2, wo):
     groups = n // GROUP
     blk = lambda c: pl.BlockSpec((1, BLOCK, c), lambda i: (i, 0, 0))
     whole = lambda s: pl.BlockSpec(s, lambda i: (0,) * len(s), pipeline_mode=pl.Buffered(1))
@@ -621,20 +655,21 @@
             blk(D),
             whole((D, QKV)),
             whole(gvec.shape),
-            pl.BlockSpec((HEAD, BLOCK), lambda i: (0, i)),
+            pl.BlockSpec((BLOCK, 128), lambda i: (i, 0)),
+            pl.BlockSpec((BLOCK, 128), lambda i: (i, 0)),
             HB,
             HB,
             HB,
         ],
-        out_specs=(blk(D), blk(QKV), blk(128), blk(128), blk(128), blk(128), pl.BlockSpec((1, 8, 2 * BLOCK), lambda i: (i, 0, 0)), HB, HB, HB),
+        out_specs=(blk(D), blk(QKV), blk(128), blk(128), blk(128), pl.BlockSpec((1, 8, 2 * BLOCK), lambda i: (i, 0, 0)), HB, HB, HB, HB),
         out_shape=(
             SDS((nb, BLOCK, D), BF16),
             SDS((nb, BLOCK, QKV), F32),
             SDS((nb, BLOCK, 128), BF16),
             SDS((nb, BLOCK, 128), BF16),
-            SDS((nb, BLOCK, 128), BF16),
             SDS((nb, BLOCK, 128), F32),
             SDS((nb, 8, 2 * BLOCK), F32),
+            SDS((GROUP, BLOCK, 128), BF16),
             SDS((GROUP, BLOCK, D), BF16),
             SDS((groups,) + w2.shape, BF16),
             SDS((groups, GROUP) + wo.shape[1:], BF16),
@@ -646,21 +681,24 @@
             pltpu.VMEM(dy.shape, BF16),
             pltpu.VMEM(w2.shape, BF16),
             pltpu.VMEM(wo.shape, BF16),
+            pltpu.VMEM((GROUP, BLOCK, 128), BF16),
             DMA((3,)),
-            DMA((5,)),
+            DMA((6,)),
             DMA((14,)),
             DMA((14,)),
             DMA((14,)),
             DMA((14,)),
             DMA((ring_count(n),)),
             DMA((ring_count(n),)),
+            DMA((GROUP,)),
+            DMA((GROUP,)),
         ],
         compiler_params=pltpu.CompilerParams(
             collective_id=5, has_side_effects=True, dimension_semantics=("arbitrary",), vmem_limit_bytes=VMEM_LIMIT
         ),
         cost_estimate=pl.CostEstimate(flops=4 * 10**9, bytes_accessed=16 << 20, transcendentals=4 * 10**6),
         name="attn_fwd",
-    )(lengths, *in_hbm(x_all, wqkv, gvec, cs), dy, w2, wo)
+    )(lengths, *in_hbm(x_all, wqkv, gvec, ct, st), dy, w2, wo)
 
 
 def norm_back(dyv, xv, gain):
@@ -671,11 +709,37 @@
     return dx, jnp.sum(dyv * xr, axis=0, keepdims=True)
 
 
-def ffn_block_kernel(n, order, mix, x_, wo_, g_ref, w2_, wd_, dy_, res, gmid, dgf, dwo, dmh, po, dw2, od, x, wo, w2, wd, dy, fs, mbuf, h2, wgs, wds, dys, acts, dgus, part, mown, stage, dwd, ps, pr, hs, hr, os_, qs, qr, *red_refs):
+def unit_grads(h, dyb, wgu, wd):
+    f = wd.shape[0]
+    gu = nn(h, wgu)
+    da = nt(dyb, wd)
+    gp, up = gu[:, :f], gu[:, f:]
+    sig = 1.0 / (1.0 + jnp.exp(-gp))
+    sg = gp * sig
+    dg = (da * up * (sig * (1.0 + gp * (1.0 - sig)))).astype(BF16)
+    return (sg * up).astype(BF16), jnp.concatenate([dg, (da * sg).astype(BF16)], axis=1)
+
+
+def ffn_block_kernel(n, order, mix_, x_, wo_, g_ref, w21_, w22_, wd1_, wd2_, dy_, res, gmid, dgf, dwo, dmh, po, t21, dw22, dwd, x, wo, w21, dy, fs, mbuf, h2, h2t, w2v, w22, wdv, wds, dys, acts, dgu1, dgu2, dw21, part, mown, stage, hs, hr, os_, qs, qr, zs, zr, *red_refs):
     me, p, g, groups, zq, zg = places(n)
+    f1 = wd1_.shape[0]
+    f2 = wds.shape[0] - f1
+    fetch = bring(
+        (
+            (wd2_.at[pl.ds(wd2_.shape[0] - wdv.shape[1], wdv.shape[1])], wdv.at[g]),
+            (w22_, w2v.at[g]),
+            (mix_, mbuf),
+            (x_, x),
+            (wo_, wo),
+            (w21_, w21),
+            (wd1_, wds.at[pl.ds(0, f1)]),
+            (dy_, dy),
+        ),
+        fs,
+    )
     barrier([me ^ m for m in range(1, GROUP)] + zq)
-    fetch = bring(((w2_, w2), (wd_, wd), (x_, x), (wo_, wo), (mix.at[p], mbuf.at[p]), (dy_, dy)), fs)
     gf = g_ref.at[:, D : 2 * D]
+    r = w2v.shape[2]
 
     def holder(q):
         s = 0
@@ -683,36 +747,28 @@
             s = jnp.where(order[g, k] == q, k, s)
         return s
 
-    fl = wd.shape[0]
-    fp = wds.shape[0]
-    pc = start_all(
-        [rcopy(mix.at[p ^ m], mbuf.at[p], ps.at[m - 1], pr.at[m - 1], me ^ m) for m in range(1, GROUP)]
-    )
+    hw, h8 = halves(wdv.shape[1]), halves(GROUP)
+    wrings = [
+        Ring(n, p, g, lambda h: w2v.at[g, h8(h)], lambda b, h: w2v.at[b, h8(h)], zs.at[0], zr.at[0]),
+        Ring(n, p, g, lambda h: wdv.at[g, hw(h)], lambda b, h: wdv.at[b, hw(h)], zs.at[1], zr.at[1]),
+    ]
     wait_all(fetch[:2])
-    gap = jnp.zeros((D, fp - fl), BF16)
-    wgs[:, :fl] = w2[:, :fl]
-    wgs[:, fl:fp] = gap
-    wgs[:, fp : fp + fl] = w2[:, fl:]
-    wgs[:, fp + fl :] = gap
-    wds[:fl] = wd[...]
-    wds[fl:] = jnp.zeros((fp - fl, D), BF16)
-    for c in pc:
-        c.wait_recv()
+    for c in wrings:
+        c.start()
     wait_all(fetch[2:5])
     m = jnp.concatenate([mbuf[b] for b in range(GROUP)], axis=1)
     mown[...] = m
     z = x[...].astype(F32) + nn(m, wo[...])
     res[...] = z
-    r = lax.rsqrt(jnp.mean(z * z, axis=-1, keepdims=True) + EPSILON)
-    h2[p] = (z * r * gf[...]).astype(BF16)
+    h2[p] = (z * lax.rsqrt(jnp.mean(z * z, axis=-1, keepdims=True) + EPSILON) * gf[...]).astype(BF16)
     hb = halves(BLOCK)
     hg = PlaneGather(me, p, lambda h: h2.at[p, hb(h)], lambda b, h: h2.at[b, hb(h)], hs, hr)
     red = PlaneReduce(me, lambda b: part.at[b], *red_refs[:7])
-    ring = RingReduce(n, p, g, dwd, *red_refs[7:])
+    ring21 = RingReduce(n, p, g, dw21, *red_refs[7:])
     hg.start_first()
-    fetch[5].wait()
-
-    def block(t, carry):
+    wait_all(fetch[5:])
+
+    def first(t, carry):
         @pl.when(t == 1)
         def _():
             hg.start_second()
@@ -720,7 +776,6 @@
 
         @pl.when(t == 2)
         def _():
-            red.first[0].start()
             hg.relay1()
             hg.relay2()
 
@@ -730,95 +785,114 @@
 
         @pl.when(t == 4)
         def _():
-            red.first[1].start()
+            for c in wrings:
+                c.relay()
 
         @pl.when(t == 5)
         def _():
             hg.arrive(hg.fy)
-            red.chip_x()
 
         @pl.when(t == 6)
         def _():
-            red.first[2].start()
             hg.relay3()
 
         @pl.when(t == 7)
         def _():
+            hg.arrive(hg.fd)
+
+        b = p ^ t
+        dys[b] = jnp.concatenate([dy[holder(2 * b)], dy[holder(2 * b + 1)]], axis=0)
+        h2t[:, pl.ds(pl.multiple_of(b * BLOCK, BLOCK), BLOCK)] = h2[b].T
+        acts[b, :, :f1], dgu1[b] = unit_grads(h2[b], dys[b], w21[...], wds[:f1])
+        return carry
+
+    lax.fori_loop(0, GROUP, first, 0)
+    grad1 = nn(h2t[...], dgu1[...].reshape(ROWS, 2 * f1)).astype(BF16)
+    for k in range(groups * GROUP):
+        dw21[k // GROUP, k % GROUP] = grad1[k * r : (k + 1) * r]
+    ring21.start()
+    for c in wrings:
+        c.finish()
+    for k in range(groups * GROUP):
+        w22[k * r : (k + 1) * r] = w2v[k // GROUP, k % GROUP]
+    each = f2 // groups
+    for k in range(groups):
+        wds[f1 + k * each : f1 + (k + 1) * each] = wdv[k].reshape(each, D)
+
+    def second(t, carry):
+        @pl.when(t == 1)
+        def _():
+            red.first[3].start()
+
+        @pl.when(t == 3)
+        def _():
+            red.first[2].start()
+            red.chip_d()
+
+        @pl.when(t == 5)
+        def _():
+            red.first[1].start()
             red.chip_y()
-            hg.arrive(hg.fd)
-
-        b = p ^ t
-        h = h2[b]
-        dyb = jnp.concatenate([dy[holder(2 * b)], dy[holder(2 * b + 1)]], axis=0)
-        dys[b] = dyb
-        gu = nn(h, wgs[...])
-        da = nt(dyb, wds[...])
-        gp, up = gu[:, :fp], gu[:, fp:]
-        sig = 1.0 / (1.0 + jnp.exp(-gp))
-        sg = gp * sig
-        acts[b] = (sg * up).astype(BF16)
-        dgu = jnp.concatenate(
-            [(da * up * (sig * (1.0 + gp * (1.0 - sig)))).astype(BF16), (da * sg).astype(BF16)], axis=1
-        )
-        dgus[b] = dgu
-        part[b] = nt(dgu, wgs[...]).astype(BF16)
+
+        @pl.when(t == 7)
+        def _():
+            red.first[0].start()
+            red.chip_x()
+
+        b = p ^ (GROUP - 1 - t)
+        acts[b, :, f1:], dgu2[b] = unit_grads(h2[b], dys[b], w22[...], wds[f1:])
+        part[b] = (nt(dgu1[b], w21[...]) + nt(dgu2[b], w22[...])).astype(BF16)
         return carry
 
-    lax.fori_loop(0, GROUP, block, 0)
-    red.first[3].start()
-    a_all = acts[...].reshape(ROWS, fp)
-    dw = tn(a_all, dys[...].reshape(ROWS, D))[:fl].astype(BF16)
-    each = fl // groups
+    lax.fori_loop(0, GROUP, second, 0)
+    dw = tn(acts[...].reshape(ROWS, f1 + f2), dys[...].reshape(ROWS, D)).astype(BF16)
+    l1 = dwd.shape[1] - wdv.shape[1]
+    e1 = f1 // groups
     for k in range(groups):
-        dwd[k] = dw[k * each : (k + 1) * each].reshape(dwd.shape[1:])
-    ring.start()
-    red.chip_d()
-
-    def out(b, carry):
-        slot = lax.rem(b, 2)
-
-        @pl.when(b > 1)
-        def _():
-            pltpu.make_async_copy(stage.at[slot], po.at[b - 2], os_.at[slot]).wait()
-
-        stage[slot] = nn(acts[b], wds[...]).astype(BF16)
-        pltpu.make_async_copy(stage.at[slot], po.at[b], os_.at[slot]).start()
-        return carry
-
-    lax.fori_loop(0, GROUP, out, 0)
-    for b in range(GROUP - 2, GROUP):
-        pltpu.make_async_copy(stage.at[b % 2], po.at[b], os_.at[b % 2]).wait()
+        dwd[k, :l1] = dw[k * e1 : (k + 1) * e1].reshape((l1,) + dwd.shape[2:])
+        dwd[k, l1:] = dw[f1 + k * each : f1 + (k + 1) * each].reshape(wdv.shape[1:])
     red.phase2()
-    h_all = h2[...].reshape(ROWS, D)
-    dg_all = dgus[...].reshape(ROWS, 2 * fp)
-    dw2[:, :fl] = tn(h_all, dg_all[:, :fp])[:, :fl].astype(BF16)
-    dw2[:, fl:] = tn(h_all, dg_all[:, fp:])[:, :fl].astype(BF16)
-    ring.relay()
+    ring21.relay()
+    dw22[...] = nn(h2t[...], dgu2[...].reshape(ROWS, 2 * f2)).astype(BF16)
     dx, dgain = norm_back(red.phase3(), res[...], gf[...])
-    dyo = dys[p].astype(F32)
-    gm = dyo + dx
+    gm = dys[p].astype(F32) + dx
     gmid[...] = gm
     dgf[...] = dgain
     gl = gm.astype(BF16)
     dm = nt(gl, wo[...]).astype(BF16)
     for b in range(GROUP):
         mbuf[b] = dm[:, 128 * b : 128 * (b + 1)]
-    for c in pc:
-        c.wait_send()
     qc = start_all(
         [rcopy(mbuf.at[p ^ m], dmh.at[p], qs.at[m - 1], qr.at[m - 1], me ^ m) for m in range(1, GROUP)]
     )
     dmh[p] = mbuf[p]
     dwo[...] = tn(mown[...], gl).astype(BF16)
+
+    def out(b, carry):
+        slot = lax.rem(b, 2)
+
+        @pl.when(b > 1)
+        def _():
+            pltpu.make_async_copy(stage.at[slot], po.at[b - 2], os_.at[slot]).wait()
+
+        stage[slot] = nn(acts[b], wds[...]).astype(BF16)
+        pltpu.make_async_copy(stage.at[slot], po.at[b], os_.at[slot]).start()
+        return carry
+
+    lax.fori_loop(0, GROUP, out, 0)
+    for b in range(GROUP - 2, GROUP):
+        pltpu.make_async_copy(stage.at[b % 2], po.at[b], os_.at[b % 2]).wait()
     wait_all(qc)
     hg.sent()
-    od[...] = ring.finish()
-
-
-def ffn_block(n, order, mix, x, wo, gvec, w2, wd, dy, blk):
-    fl = wd.shape[0]
+    t21[...] = ring21.finish().astype(BF16)
+
+
+def ffn_block(n, order, mix, x, wo, gvec, w21, w22, wd1, wd, dy):
     groups = n // GROUP
-    fp = -(-fl // 128) * 128
+    r = w22.shape[1]
+    f1, f2 = w21.shape[1] // 2, w22.shape[2] // 2
+    wd2 = (wd.shape[0] // 3,) + wd.shape[1:]
+    blk = (GROUP, r, 2 * f1)
     vm = lambda *s: pltpu.VMEM(s, BF16)
     return pl.pallas_call(
         functools.partial(ffn_block_kernel, n),
@@ -829,45 +903,49 @@
             SDS((D, D), BF16),
             SDS((GROUP, BLOCK, 128), BF16),
             SDS((GROUP, BLOCK, D), BF16),
-            SDS((D, 2 * fl), BF16),
-            SDS(blk, F32),
+            SDS(blk, BF16),
+            SDS((D, 2 * f2), BF16),
+            SDS((groups,) + wd.shape, BF16),
         ),
-        in_specs=[SM, HB, HB, HB, VM, HB, HB, HB],
-        out_specs=(VM, VM, VM, VM, VM, HB, VM, VM),
+        in_specs=[SM, HB, HB, HB, VM, HB, HB, HB, HB, HB],
+        out_specs=(VM, VM, VM, VM, VM, HB, VM, VM, VM),
         scratch_shapes=[
             vm(BLOCK, D),
             vm(D, D),
-            vm(D, 2 * fl),
-            vm(fl, D),
+            vm(D, 2 * f1),
             vm(ROWS // SLOT, SLOT, D),
-            DMA((6,)),
+            DMA((8,)),
             vm(GROUP, BLOCK, 128),
             vm(GROUP, BLOCK, D),
-            vm(D, 2 * fp),
-            vm(fp, D),
+            vm(D, ROWS),
+            vm(groups, *w22.shape),
+            vm(D, 2 * f2),
+            vm(groups, *wd2),
+            vm(f1 + f2, D),
             vm(GROUP, BLOCK, D),
-            vm(GROUP, BLOCK, fp),
-            vm(GROUP, BLOCK, 2 * fp),
+            vm(GROUP, BLOCK, f1 + f2),
+            vm(GROUP, BLOCK, 2 * f1),
+            vm(GROUP, BLOCK, 2 * f2),
+            vm(groups, *blk),
             vm(GROUP, BLOCK, D),
             vm(BLOCK, D),
             vm(2, BLOCK, D),
-            vm(groups, *blk),
-            DMA((7,)),
-            DMA((7,)),
             DMA((14,)),
             DMA((14,)),
             DMA((2,)),
             DMA((7,)),
             DMA((7,)),
+            DMA((2, ring_count(n))),
+            DMA((2, ring_count(n))),
         ]
         + plane_scratch((BLOCK, D))
         + ring_scratch(n, blk),
         compiler_params=pltpu.CompilerParams(collective_id=2, has_side_effects=True, vmem_limit_bytes=VMEM_LIMIT),
         name="ffn_block",
-    )(order, mix, x, wo, gvec, w2, wd, dy.reshape(ROWS // SLOT, SLOT, D))
-
-
-def attn_bwd_kernel(n, len_ref, dm_ref, q_ref, kvall_ref, lse_ref, mixf_ref, h_ref, raw_ref, w_ref, g_ref, cs_ref, po, res, dwo, dw2, dgf, dh_ref, dw_ref, gpart, result, two, t2, k_s, v_s, dkv, dqt, dws, dg_ref, *rest):
+    )(order, mix, x, wo, gvec, w21, w22, wd1, wd, dy.reshape(ROWS // SLOT, SLOT, D))
+
+
+def attn_bwd_kernel(n, len_ref, dm_ref, q_ref, kvall_ref, lse_ref, mixf_ref, h_ref, raw_ref, w_ref, g_ref, ct_ref, st_ref, po_, res_, dwo_, dw2_, dwd_, t21_, dgf, dh_ref, dw_ref, gpart, result, two, t2, od, o21, k_s, v_s, dkv, dqt, dws, dg_ref, es, er, po, res, dwo, dw2, dwd, t21, fs, *rest):
     step_id = pl.program_id(0)
     nb = ROWS // BLOCK
     i = nb - 1 - step_id
@@ -875,13 +953,20 @@
     ored = PlaneReduce(me, lambda b: po.at[b], *rest[:7])
     wred = PlaneReduce(me, lambda b: dwo.at[:, b], *rest[7:14])
     ring2 = RingReduce(n, p, g, dw2, *rest[14:20])
+    ringd = RingReduce(n, p, g, dwd, *rest[20:26])
+    fetch = [
+        pltpu.make_async_copy(a, b, fs.at[k])
+        for k, (a, b) in enumerate(
+            ((dwd_, dwd), (dw2_, dw2), (po_, po), (dwo_, dwo), (t21_, t21), (res_, res))
+        )
+    ]
+    ex = [rcopy(t21.at[p ^ m], o21.at[p], es.at[m - 1], er.at[m - 1], me ^ m) for m in range(1, GROUP)]
+    own_copy = pltpu.make_async_copy(t21.at[p], o21.at[p], fs.at[6])
 
     @pl.when(step_id == 0)
     def _():
-        barrier([me ^ m for m in (1, 2, 4)] + zq)
-        ored.start()
-        ring2.start()
-        wred.start()
+        start_all(fetch)
+        barrier([me ^ m for m in range(1, GROUP)] + zq)
 
     @pl.when(step_id == 1)
     def _():
@@ -890,6 +975,7 @@
 
     @pl.when(step_id == 3)
     def _():
+        ringd.relay()
         ring2.relay()
         ored.phase2()
 
@@ -919,26 +1005,20 @@
     colq = lax.broadcasted_iota(jnp.int32, (1, 2 * BLOCK), 1)
     qrow = i * BLOCK + jnp.where(colq >= BLOCK, colq - BLOCK, colq)
     qstart = seq_start(qrow, len_ref, g)
-    first = jnp.maximum(i - WINDOW, 0)
-    rowk = lax.broadcasted_iota(jnp.int32, (BLOCK, 2 * BLOCK), 0)
-    dqt[...] = jnp.zeros_like(dqt)
-
-    def step(j, carry):
-        at = pl.ds(pl.multiple_of(j * BLOCK, BLOCK), BLOCK)
+
+    def window(first, count):
+        at = pl.ds(pl.multiple_of(first * BLOCK, BLOCK), count * BLOCK)
         kb, vb = k_s[at, :], v_s[at, :]
-        s = nt(kb, q2)
-        kc = rowk + j * BLOCK
+        kc = lax.broadcasted_iota(jnp.int32, (count * BLOCK, 2 * BLOCK), 0) + first * BLOCK
         ok = (kc >= qstart) & (kc <= qrow)
-        pr = jnp.where(ok, jnp.exp2(s * (SCALE * LOG2E) - lse), 0.0)
-        dp = nt(vb, do2)
-        dsc = (pr * (dp - delta)).astype(BF16)
+        pr = jnp.where(ok, jnp.exp2(nt(kb, q2) * (SCALE * LOG2E) - lse), 0.0)
+        dsc = (pr * (nt(vb, do2) - delta)).astype(BF16)
         dkv[at, :HEAD] += nn(dsc, q2)
         dkv[at, HEAD:] += nn(pr.astype(BF16), do2)
-        dqt[...] += tn(dsc, kb)
-        return carry
-
-    lax.fori_loop(first, i + 1, step, 0)
-    ct, st = tables(cs_ref)
+        dqt[...] = tn(dsc, kb)
+
+    windows(i, window)
+    ct, st = ct_ref[...], st_ref[...]
     raw = raw_ref[0]
     dq = jnp.concatenate([dqt[:BLOCK], dqt[BLOCK:]], axis=1) * SCALE
     dkvb = dkv[pl.ds(pl.multiple_of(i * BLOCK, BLOCK), BLOCK), :]
@@ -960,12 +1040,23 @@
     dh_ref[0] = nt(dqkv, w_ref[...]).astype(BF16)
     dws[...] += tn(h_ref[0], dqkv)
 
+    @pl.when(step_id == 0)
+    def _():
+        wait_all(fetch)
+        ringd.start()
+        ring2.start()
+        ored.start()
+        wred.start()
+        start_all(ex + [own_copy])
+
     @pl.when(step_id == nb - 1)
     def _():
         dw_ref[...] = dws[...].astype(BF16)
         result[...] = (ored.phase3() + res[...]).astype(BF16)
         two[...] = wred.phase3().astype(BF16)
         t2[...] = ring2.finish().astype(BF16)
+        od[...] = ringd.finish()
+        wait_all(ex + [own_copy])
         dga = lax.dot_general(
             jnp.ones((8, QKV), F32),
             w_ref[...].astype(F32) * dws[...],
@@ -983,7 +1074,7 @@
         gpart[16:17, :] = jnp.where(low, dg_ref[0:1, :] + turned[0:1, :], turned[1:2, :])
 
 
-def attn_bwd(n, lengths, dmh, q, kv, lse, mixf, h, raw, wqkv, gvec, cs, po, res, dwo, dw2, dgf):
+def attn_bwd(n, lengths, dmh, q, kv, lse, mixf, h, raw, wqkv, gvec, ct, st, po, res, dwo, dw2, dwd, t21, dgf):
     nb = ROWS // BLOCK
     groups = n // GROUP
     blk = lambda c: pl.BlockSpec((1, BLOCK, c), lambda i: (nb - 1 - i, 0, 0))
@@ -1002,11 +1093,14 @@
             blk(QKV),
             whole((D, QKV)),
             whole(gvec.shape),
-            pl.BlockSpec((HEAD, BLOCK), lambda i: (0, nb - 1 - i)),
-            whole(po.shape),
-            whole(res.shape),
-            whole(dwo.shape),
-            whole(dw2.shape),
+            pl.BlockSpec((BLOCK, 128), lambda i: (nb - 1 - i, 0)),
+            pl.BlockSpec((BLOCK, 128), lambda i: (nb - 1 - i, 0)),
+            HB,
+            HB,
+            HB,
+            HB,
+            HB,
+            HB,
             whole(dgf.shape),
         ],
         out_specs=(
@@ -1016,6 +1110,8 @@
             whole((BLOCK, D)),
             whole((groups,) + dwo.shape[2:]),
             whole(dw2.shape[1:]),
+            whole(dwd.shape[1:]),
+            HB,
         ),
         out_shape=(
             SDS((nb, BLOCK, D), BF16),
@@ -1024,6 +1120,8 @@
             SDS((BLOCK, D), BF16),
             SDS((groups,) + dwo.shape[2:], BF16),
             SDS(dw2.shape[1:], BF16),
+            SDS(dwd.shape[1:], F32),
+            SDS(t21.shape, BF16),
         ),
         scratch_shapes=[
             pltpu.VMEM((ROWS, HEAD), BF16),
@@ -1032,16 +1130,21 @@
             pltpu.VMEM((2 * BLOCK, HEAD), F32),
             pltpu.VMEM((D, QKV), F32),
             pltpu.VMEM((8, 128), F32),
+            DMA((7,)),
+            DMA((7,)),
         ]
+        + [pltpu.VMEM(a.shape, a.dtype) for a in (po, res, dwo, dw2, dwd, t21)]
+        + [DMA((7,))]
         + plane_scratch((BLOCK, D))
         + plane_scratch((groups,) + dwo.shape[2:])
-        + ring_scratch(n, dw2.shape[1:]),
+        + ring_scratch(n, dw2.shape[1:])
+        + ring_scratch(n, dwd.shape[1:]),
         compiler_params=pltpu.CompilerParams(
             collective_id=6, has_side_effects=True, dimension_semantics=("arbitrary",), vmem_limit_bytes=VMEM_LIMIT
         ),
         cost_estimate=pl.CostEstimate(flops=8 * 10**9, bytes_accessed=16 << 20, transcendentals=4 * 10**6),
         name="attn_bwd",
-    )(lengths, dmh, q, kv, lse, mixf, h, raw, wqkv, gvec, cs, po, res, dwo, dw2, dgf)
+    )(lengths, dmh, q, kv, lse, mixf, h, raw, wqkv, gvec, ct, st, po, res, dwo, dw2, dwd, t21, dgf)
 
 
 def final_kernel(n, dh, x, gmid, g_ref, dw1, two, t2, gpart, gtok, o1, o2, oo, og, t1, gin, gsum, gz, ps, pr, gs, gr, *rest):
@@ -1130,7 +1233,7 @@
     )(dh, x, gmid, gvec, dw1, two, t2, gpart)
 
 
-def unpack_kernel(groups, result, gtok, o1, o2, oo, od, og, result_o, gtok_o, gq, gk, gv, go, gg, gu, gd, gn):
+def unpack_kernel(groups, result, gtok, o1, o21, o22, oo, od, og, result_o, gtok_o, gq, gk, gv, go, gg, gu, gd, gn):
     result_o[...] = result[...]
     gtok_o[...] = gtok[...]
     go[...] = oo[...]
@@ -1144,15 +1247,18 @@
             out[:, 128 * c : 128 * (c + 1)] = jnp.concatenate(pair, axis=1)
     ffc = gg.shape[1] // (groups * GROUP)
     for k, out in enumerate((gg, gu)):
+        big = 2 * ffc // 3
+        piece = lambda src, b, c, w: src[b, :, (k * groups + c) * w : (k * groups + c + 1) * w].astype(F32)
         parts = [
-            o2[b, :, (k * groups + c) * ffc : (k * groups + c + 1) * ffc].astype(F32)
+            piece(src, b, c, w)
             for c in range(groups)
             for b in range(GROUP)
+            for src, w in ((o21, big), (o22, ffc - big))
         ]
         out[...] = jnp.concatenate(parts, axis=1)
 
 
-def unpack(n, result, gtok, o1, o2, oo, od, og, share):
+def unpack(n, result, gtok, o1, o21, o22, oo, od, og, share):
     r = oo.shape[0]
     return pl.pallas_call(
         functools.partial(unpack_kernel, n // GROUP),
@@ -1168,11 +1274,11 @@
             SDS(od.shape, F32),
             SDS((1, share), F32),
         ),
-        in_specs=[VM] * 7,
+        in_specs=[VM] * 8,
         out_specs=(VM,) * 10,
         compiler_params=pltpu.CompilerParams(vmem_limit_bytes=VMEM_LIMIT),
         name="unpack",
-    )(result, gtok, o1, o2, oo, od, og)
+    )(result, gtok, o1, o21, o22, oo, od, og)
 
 
 def body(n, tokens, w_query, key_weight, w_value, w_out, w_gate, w_up, w_down, norm_gains, seq_lengths, slot_order, out_grad):
@@ -1181,9 +1287,9 @@
     ffc = w_down.shape[0]
     share = norm_gains.shape[0]
     wok = r // 16 if r % 16 == 0 else 1
-    wdk = ffc // 16 if ffc % 16 == 0 else 1
+    wdk = 9 if ffc % 144 == 0 else 3
     wo_blk, wd_blk = (wok, r // wok, D), (wdk, ffc // wdk, D)
-    x_all, w1, w2, wo, wd, gvec, cs = gather_all(
+    x_all, w1, w21, w22, wo, wd1, gvec, ct, st = gather_all(
         n,
         seq_lengths,
         tokens,
@@ -1197,13 +1303,23 @@
         norm_gains.reshape(1, share),
     )
     wqkv = w1.reshape(D, QKV)
-    h, raw, q, kv, mix, mixf, lse, dy_all, w2, wo = attn_fwd(
-        n, seq_lengths, x_all, wqkv, gvec, cs, out_grad, w2, wo.reshape(groups, r, D)
+    h, raw, q, kv, mixf, lse, mix, dy_all, w21, wo = attn_fwd(
+        n, seq_lengths, x_all, wqkv, gvec, ct, st, out_grad, w21, wo.reshape(groups, r, D)
     )
-    res, gmid, dgf, dwo, dmh, po, dwgu, od = ffn_block(
-        n, slot_order, mix, tokens, wo.reshape(D, D), gvec, w2.reshape(D, -1), wd.reshape(-1, D), dy_all, wd_blk
+    res, gmid, dgf, dwo, dmh, po, t21, dw22, dwd = ffn_block(
+        n,
+        slot_order,
+        mix,
+        tokens,
+        wo.reshape(D, D),
+        gvec,
+        w21.reshape(D, -1),
+        w22,
+        wd1.reshape(-1, D),
+        w_down.reshape(wd_blk),
+        dy_all,
     )
-    dh1, dwqkv, gpart, result, two, t2 = attn_bwd(
+    dh1, dwqkv, gpart, result, two, t2, od, o21 = attn_bwd(
         n,
         seq_lengths,
         dmh,
@@ -1215,14 +1331,17 @@
         raw,
         wqkv,
         gvec,
-        cs,
+        ct,
+        st,
         po,
         res,
         dwo.reshape(groups, GROUP, r, D),
-        dwgu.reshape(groups, GROUP, r, -1),
+        dw22.reshape(groups, GROUP, r, -1),
+        dwd,
+        t21,
         dgf,
     )
-    gtok, o1, o2, oo, og = final(
+    gtok, o1, o22, oo, og = final(
         n,
         dh1,
         tokens,
@@ -1233,7 +1352,7 @@
         t2,
         gpart,
     )
-    outs = unpack(n, result, gtok, o1, o2, oo.reshape(r, D), od.reshape(ffc, D), og, share)
+    outs = unpack(n, result, gtok, o1, o21, o22, oo.reshape(r, D), od.reshape(ffc, D), og, share)
     return outs[:-1] + (outs[-1].reshape(share),)
 
 

time: 250 us -> 234 us (0.936)
  Pallas kernels: 249 us -> 233 us
    pallas_call x1, Pallas kernels: 51.4 us -> 44.3 us  [attn_bwd(): pl.pallas_call(functools.partial(attn_bwd_kernel, n), grid=(nb,), in_spec...]
    pallas_call x1, Pallas kernels: 37.1 us -> 32.4 us  [final(): pl.pallas_call(functools.partial(final_kernel, n), out_shape=(SDS((BLOCK,...]
    pallas_call x1, Pallas kernels: 44.2 us -> 40.8 us  [attn_fwd(): pl.pallas_call(functools.partial(attn_fwd_kernel, n), grid=(nb,), in_spec...]
    pallas_call x1, Pallas kernels: 43.6 us -> 41 us  [gather_all(): pl.pallas_call(functools.partial(gather_kernel, n), out_shape=(SDS((GROUP...]
where the time goes in v5:
time: 234 us
  Pallas kernels  233 us (100%)
    pallas_call x1, Pallas kernels, ffn_block(): pl.pallas_call(functools.partial(ffn_block_kernel, n), out_shape=(SDS((BL...  70.9 us
    pallas_call x1, Pallas kernels, attn_bwd(): pl.pallas_call(functools.partial(attn_bwd_kernel, n), grid=(nb,), in_spec...  44.3 us
    pallas_call x1, Pallas kernels, gather_all(): pl.pallas_call(functools.partial(gather_kernel, n), out_shape=(SDS((GROUP...  41 us
    pallas_call x1, Pallas kernels, attn_fwd(): pl.pallas_call(functools.partial(attn_fwd_kernel, n), grid=(nb,), in_spec...  40.8 us
    pallas_call x1, Pallas kernels, final(): pl.pallas_call(functools.partial(final_kernel, n), out_shape=(SDS((BLOCK,...  32.4 us

profile of v5, /device:TPU:0, one launch (start us, length us, event | category | flops | bytes accessed | tf_op | source)
XLA Modules:
  0.0 234.1 jit_solution(18057102554589463263)
XLA Ops:
  0.6 41.0 %gather_all.1 = (bf16[8,256,1024]{2,1,0:T(8,128)(2,1)}, bf16[4,8,32,256]{3,2,1,0:T(8,128)(2,1)}, bf16[8,32,768]{2,1,0:T(8,128)(2,1)}, bf16[8,32,384]{2,1,0:T(8,1...) custom-call(s32[4,4]{1,0:T(4,128)} %len_ref.5, ...), custom_call_target="tpu_custom_call" | custom-call | tf_op jit(solution)/shard_map/gather_all/pallas_call | solution.py:457
  41.7 40.8 %attn_fwd.1 = (bf16[8,256,1024]{2,1,0:T(8,128)(2,1)}, f32[8,256,256]{2,1,0:T(8,128)}, bf16[8,256,128]{2,1,0:T(8,128)(2,1)}, bf16[8,256,128]{2,1,0:T(8,128)(2,1)}...) custom-call(s32[4,4]{1,0:T(4,128)} %len_ref.5, ...), custom_call_target="tpu_custom_call" | custom-call | flops 4000000000 | bytes 16777216 | tf_op jit(solution)/shard_map/attn_fwd/pallas_call | solution.py:650
  82.5 70.9 %ffn_block.1 = (f32[256,1024]{1,0:T(8,128)}, f32[256,1024]{1,0:T(8,128)}, f32[1,1024]{1,0:T(1,128)}, bf16[1024,1024]{1,0:T(8,128)(2,1)}, bf16[8,256,128]{2,1,0:T...) custom-call(s32[4,16]{1,0:T(4,128)} %order.1, ...), custom_call_target="tpu_custom_call" | custom-call | tf_op jit(solution)/shard_map/ffn_block/pallas_call | solution.py:897
  153.4 44.3 %attn_bwd.1 = (bf16[8,256,1024]{2,1,0:T(8,128)(2,1)}, bf16[1024,256]{1,0:T(8,128)(2,1)}, f32[24,128]{1,0:T(8,128)}, bf16[256,1024]{1,0:T(8,128)(2,1)}, bf16[4,32...) custom-call(s32[4,4]{1,0:T(4,128)} %len_ref.5, ...), custom_call_target="tpu_custom_call" | custom-call | flops 8000000000 | bytes 16777216 | tf_op jit(solution)/shard_map/attn_bwd/pallas_call | solution.py:1082
  197.7 32.4 %final.1 = (f32[256,1024]{1,0:T(8,128)}, bf16[8,32,256]{2,1,0:T(8,128)(2,1)}, bf16[8,32,384]{2,1,0:T(8,128)(2,1)}, f32[2,16,1024]{2,1,0:T(8,128)}, f32[8,128]{1,0:T(8,128)}) custom-call(bf16[8,256,1024]{2,1,0:T(8,128)(2,1)} %get-tuple-element.89.dh, bf16[256,1024]{1,0:T(8,128)(2,1)} %x.1, f32[256,1024]{1,0:T(8,128)} %get-tuple-element.90.gmid, ...), custom_call_target="tpu_custom_call" | custom-call | tf_op jit(solution)/shard_map/final/pallas_call | solution.py:1207
  230.1 4.0 %unpack.1 = (bf16[256,1024]{1,0:T(8,128)(2,1)}, f32[256,1024]{1,0:T(8,128)}, f32[32,1024]{1,0:T(8,128)}, f32[32,512]{1,0:T(8,128)}, f32[32,512]{1,0:T(8,128)}, /...) custom-call(bf16[256,1024]{1,0:T(8,128)(2,1)} %get-tuple-element.88.r, ...), custom_call_target="tpu_custom_call" | custom-call | tf_op jit(solution)/shard_map/unpack/pallas_call | solution.py:1263

commit v6 on v5

--- a/solution.py
+++ b/solution.py
@@ -80,10 +80,6 @@
     return start_all([pltpu.make_async_copy(a, b, sem.at[i]) for i, (a, b) in enumerate(pairs)])
 
 
-def in_hbm(*arrays):
-    return [pltpu.with_memory_space_constraint(a, pltpu.HBM) for a in arrays]
-
-
 def wait_all(copies):
     for c in copies:
         c.wait()
@@ -274,8 +270,9 @@
 
 
 class PlaneReduce:
-    def __init__(self, me, part, sib, send, relay, fx, fy, ss, rs):
+    def __init__(self, me, part, sib, send, relay, fx, fy, ss, rs, own=None):
         p = lax.rem(me, GROUP)
+        self.own = own or (lambda i: part(p ^ (2 * i)))
         xn, yn = me ^ 2, me ^ 4
         hs = halves(sib.shape[1])
         self.hs, self.p, self.part = hs, p, part
@@ -294,7 +291,7 @@
 
     def chip(self, i):
         self.first[i].wait_recv()
-        return self.part(self.p ^ (2 * i))[...].astype(F32) + self.sib[i].astype(F32)
+        return self.own(i)[...].astype(F32) + self.sib[i].astype(F32)
 
     def chip_d(self):
         self.send[0] = self.chip(3).astype(BF16)
@@ -347,11 +344,53 @@
     ]
 
 
-def gather_kernel(n, len_ref, x_, wq_, wk_, wv_, wg_, wu_, wo_, wd_, gn_, xo, a1o, b1o, b2o, woo, wdo, gvec, ct, st, x, gn, wq, wk, wv, wo, wd, wg, wu, a1, b1, b2, gt, gto, fs, ls, xs, xr, ps, pr, zs, zr):
+def swap_halves(v):
+    lane = lax.broadcasted_iota(jnp.int32, v.shape, 1)
+    low = lax.rem(lane, HEAD) < HEAD // 2
+    width = v.shape[1]
+    return jnp.where(low, pltpu.roll(v, width - HEAD // 2, 1), pltpu.roll(v, HEAD // 2, 1))
+
+
+def head_mean(v):
+    row = lax.broadcasted_iota(jnp.int32, (128, 128), 0)
+    lane = lax.broadcasted_iota(jnp.int32, (128, 128), 1)
+    same = jnp.where((row < HEAD) == (lane < HEAD), 1.0 / HEAD, 0.0).astype(BF16)
+    high = v.astype(BF16)
+    low = (v - high.astype(F32)).astype(BF16)
+    return nn(high, same) + nn(low, same)
+
+
+def head_gains(g_ref):
+    t = g_ref[:, 2 * D :]
+    t = jnp.broadcast_to(t, (8, 128))
+    lane = lax.broadcasted_iota(jnp.int32, (8, 128), 1)
+    other = pltpu.roll(t, HEAD, 1)
+    return jnp.where(lane < HEAD, t, other)[0:1, :], jnp.where(lane < HEAD, other, t)[0:1, :]
+
+
+def seq_start(row, len_ref, g):
+    e1 = len_ref[g, 0]
+    e2 = e1 + len_ref[g, 1]
+    e3 = e2 + len_ref[g, 2]
+    zero = row * 0
+    s = jnp.where(row >= e1, zero + e1, zero)
+    s = jnp.where(row >= e2, zero + e2, s)
+    return jnp.where(row >= e3, zero + e3, s)
+
+
+def windows(i, window):
+    for low, high, count in ((0, 1, 2), (2, 3, 4), (4, 7, WINDOW + 1)):
+
+        @pl.when((i >= low) & (i <= high))
+        def _():
+            window(jnp.maximum(i - WINDOW, 0), count)
+
+
+def front_kernel(n, len_ref, x_, wq_, wk_, wv_, wg_, wu_, wo_, wd_, gn_, dy_, h_o, raw_o, q_o, kv_o, mixf_o, lse_o, mixo, dyo, w21o, w22o, woo, wdo, wqkv_o, gvec, ct, st, xa, gn, wq, wk, wv, wo, wd, wg, wu, dy, a1, b1, b2, gt, gto, w1v, woz, wqkv, h_s, raw_s, q_s, kv_s, mixf_s, lse_s, mixs, k_s, v_s, acc, fs, ls, xs, xr, ds_, dr, os_, orr, ps, pr, zs, zr, ms, mr, outs):
     me, p, g, groups, zq, zg = places(n)
     fetch = bring(
         (
-            (x_, x),
+            (x_, xa.at[p]),
             (gn_, gn),
             (wq_, wq),
             (wk_, wk),
@@ -360,15 +399,19 @@
             (wd_.at[pl.ds(0, wd.shape[0])], wd),
             (wg_, wg),
             (wu_, wu),
+            (dy_, dy),
         ),
         fs,
     )
     share = gn.shape[1]
     ffc = wg.shape[1] // (groups * GROUP)
     big = 2 * ffc // 3
+    r = wq.shape[0]
     barrier([me ^ m for m in range(1, GROUP)] + zq)
-    hx = halves(BLOCK)
-    xg = PlaneGather(me, p, lambda h: x.at[hx(h)], lambda b, h: xo.at[b, hx(h)], xs, xr, ls.at[pl.ds(5, 2)])
+    hx, ho = halves(BLOCK), halves(groups)
+    xg = PlaneGather(me, p, lambda h: xa.at[p, hx(h)], lambda b, h: xa.at[b, hx(h)], xs, xr)
+    dg = PlaneGather(me, p, lambda h: dy.at[hx(h)], lambda b, h: dyo.at[b, hx(h)], ds_, dr, ls.at[pl.ds(0, 2)])
+    og = PlaneGather(me, p, lambda h: woz.at[ho(h)], lambda b, h: woo.at[ho(h), b], os_, orr, ls.at[pl.ds(2, 2)])
     fetch[0].wait()
     xg.start_first()
 
@@ -376,18 +419,19 @@
         hk = halves(dst.shape[1])
         return Ring(n, p, g, lambda h: src.at[hk(h)], lambda b, h: dst.at[b, hk(h)], zs.at[k], zr.at[k], local)
 
-    rings = [
-        ring(0, a1o.at[g], a1o),
-        ring(1, gto.at[g], gto),
-        ring(2, wd, wdo, ls.at[3]),
-        ring(3, wo, woo, ls.at[4]),
-    ]
+    wring, gring = ring(0, w1v.at[g], w1v), ring(1, gto.at[g], gto)
+    dring, oring = ring(2, wd, wdo, ls.at[4]), ring(3, wo, woz, ls.at[5])
+    uring = ring(4, w21o.at[g], w21o)
     pc = {}
 
     def exchange(k, src, dst):
         for m in range(1, GROUP):
             pc[k, m] = rcopy(src(p ^ m), dst, ps.at[k, m - 1], pr.at[k, m - 1], me ^ m)
             pc[k, m].start()
+
+    def arrived(k):
+        for m in range(1, GROUP):
+            pc[k, m].wait_recv()
 
     fetch[1].wait()
     gt[...] = jnp.zeros_like(gt)
@@ -399,30 +443,33 @@
         a1[b, :, :128] = wq[:, 128 * b : 128 * (b + 1)]
         at = slice(HEAD * b, HEAD * (b + 1))
         a1[b, :, 128:] = jnp.concatenate([wk[:, at], wv[:, at]], axis=1)
-    exchange(0, lambda b: a1.at[b], a1o.at[g, p])
+    exchange(0, lambda b: a1.at[b], w1v.at[g, p])
+    w1v[g, p] = a1[p]
     wait_all(fetch[5:7])
-    rings[3].start()
-    rings[2].start()
-    wait_all(fetch[7:])
+    oring.start()
+    dring.start()
+    wait_all(fetch[7:9])
     for buf, low, high in ((b1, 0, big), (b2, big, ffc)):
         for b in range(GROUP):
             at = [slice((GROUP * k + b) * ffc + low, (GROUP * k + b) * ffc + high) for k in range(groups)]
             buf[b] = jnp.concatenate([wg[:, k] for k in at] + [wu[:, k] for k in at], axis=1)
-    exchange(2, lambda b: b1.at[b], b1o.at[p])
-    exchange(3, lambda b: b2.at[b], b2o.at[p])
+    exchange(2, lambda b: b1.at[b], w21o.at[g, p])
+    exchange(3, lambda b: b2.at[b], w22o.at[p])
     xg.start_second()
-    local = [
-        pltpu.make_async_copy(a1.at[p], a1o.at[g, p], ls.at[0]),
-        pltpu.make_async_copy(b1.at[p], b1o.at[p], ls.at[2]),
-        pltpu.make_async_copy(b2.at[p], b2o.at[p], ls.at[1]),
-    ]
-    start_all(local)
-    local[0].wait()
-    for k in range(2):
-        for m in range(1, GROUP):
-            pc[k, m].wait_recv()
-        rings[k].start()
+    local = start_all(
+        [
+            pltpu.make_async_copy(b1.at[p], w21o.at[g, p], ls.at[6]),
+            pltpu.make_async_copy(b2.at[p], w22o.at[p], ls.at[7]),
+        ]
+    )
+    arrived(0)
+    wring.start()
+    arrived(1)
+    gring.start()
     xg.relay1()
+    arrived(2)
+    wait_all(local)
+    uring.start()
     row = lax.broadcasted_iota(jnp.int32, (1, ROWS), 1)
     position = (row - seq_start(row, len_ref, g)).astype(F32)
     index = lax.broadcasted_iota(jnp.int32, (HEAD // 2, 1), 0).astype(F32)
@@ -430,275 +477,196 @@
     c, s = jnp.cos(angles).T, jnp.sin(angles).T
     ct[...] = jnp.concatenate([c, c, c, c], axis=1)
     st[...] = jnp.concatenate([-s, s, -s, s], axis=1)
+    k_s[: WINDOW * BLOCK] = jnp.zeros((WINDOW * BLOCK, HEAD), BF16)
+    v_s[: WINDOW * BLOCK] = jnp.zeros((WINDOW * BLOCK, 128), BF16)
     xg.relay2()
-    for k in (3, 0, 1, 2):
-        rings[k].relay()
+    fetch[9].wait()
+    dg.start_first()
+    for c in (oring, wring, gring):
+        c.relay()
     xg.relay3()
-    for k in (2, 3):
-        for m in range(1, GROUP):
-            pc[k, m].wait_recv()
-    wait_all(local[1:])
-    for c in pc.values():
-        c.wait_send()
-    for k in range(4):
-        rings[k].finish()
+    dg.start_second()
+    dring.relay()
+    wring.finish()
+    gring.finish()
+    for k in range(groups * GROUP):
+        wqkv[k * r : (k + 1) * r] = w1v[k // GROUP, k % GROUP]
     gvec[...] = jnp.concatenate(
         [gto[k, b, 0:1, :share] for k in range(groups) for b in range(GROUP)], axis=1
     )
-    xg.finish()
-
-
-def gather_all(n, lengths, x, wq, wk, wv, wg, wu, wo, wd, gn):
+    xg.arrive(xg.o + xg.fx + xg.fy + xg.fd)
+    gq, gk = head_gains(gvec)
+    results = ((h_s, h_o), (raw_s, raw_o), (q_s, q_o), (kv_s, kv_o), (mixf_s, mixf_o), (lse_s, lse_o))
+
+    def block(i, carry):
+        @pl.when(i == 1)
+        def _():
+            oring.finish()
+            og.start_first()
+
+        @pl.when(i == 2)
+        def _():
+            dg.relay1()
+            og.start_second()
+
+        @pl.when(i == 4)
+        def _():
+            dg.relay2()
+            uring.relay()
+
+        @pl.when(i == 5)
+        def _():
+            og.relay1()
+
+        @pl.when(i == 6)
+        def _():
+            dg.relay3()
+
+        @pl.when(i == 7)
+        def _():
+            og.relay2()
+
+        at = pl.ds(pl.multiple_of(i * BLOCK, BLOCK), BLOCK)
+        xb = xa[i].astype(F32)
+        h = (xb * lax.rsqrt(jnp.mean(xb * xb, axis=-1, keepdims=True) + EPSILON) * gvec[:, :D]).astype(BF16)
+        h_s[i] = h
+        raw = nn(h, wqkv[...])
+        raw_s[i] = raw
+        cb, sb = ct[at, :], st[at, :]
+        qraw, kvraw = raw[:, :128], raw[:, 128:]
+        qn = qraw * lax.rsqrt(head_mean(qraw * qraw) + EPSILON) * gq
+        q = (qn * cb + swap_halves(qn) * sb).astype(BF16)
+        kn = kvraw * lax.rsqrt(head_mean(kvraw * kvraw) + EPSILON) * gk
+        k = (kn * cb + swap_halves(kn) * sb).astype(BF16)
+        lane = lax.broadcasted_iota(jnp.int32, (BLOCK, 128), 1)
+        kv = jnp.where(lane < HEAD, k.astype(F32), kvraw).astype(BF16)
+        q_s[i] = q
+        kv_s[i] = kv
+        k_s[at, :] = kv[:, :HEAD]
+        v_s[at, :] = jnp.where(lane < HEAD, pltpu.roll(kvraw, HEAD, 1), 1.0).astype(BF16)
+        q2 = jnp.concatenate([q[:, :HEAD], q[:, HEAD:]], axis=0)
+        rows = lax.broadcasted_iota(jnp.int32, (2 * BLOCK, 1), 0)
+        qrow = i * BLOCK + jnp.where(rows >= BLOCK, rows - BLOCK, rows)
+        qstart = seq_start(qrow, len_ref, g)
+
+        def window(first, count):
+            span = pl.ds(pl.multiple_of(first * BLOCK, BLOCK), count * BLOCK)
+            kc = lax.broadcasted_iota(jnp.int32, (2 * BLOCK, count * BLOCK), 1) + first * BLOCK
+            ok = (kc >= qstart) & (kc <= qrow)
+            e = jnp.where(ok, jnp.exp2(nt(q2, k_s[span, :]) * (SCALE * LOG2E)), 0.0).astype(BF16)
+            acc[...] = nn(e, v_s[span, :])
+
+        windows(i, window)
+        total = acc[:, HEAD:]
+        m = acc[:, :HEAD] / total
+        both = jnp.concatenate([m[:BLOCK], m[BLOCK:]], axis=1)
+        mixf_s[i] = both
+        lse_s[i] = jnp.log2(total.T)[:8, :]
+        mixs[i] = both.astype(BF16)
+
+        @pl.when(i == p)
+        def _():
+            pltpu.make_async_copy(mixs.at[i], mixo.at[p], ls.at[8]).start()
+
+        @pl.when(i != p)
+        def _():
+            rcopy(mixs.at[i], mixo.at[p], ms.at[p ^ i], mr.at[p ^ i], me ^ p ^ i).start()
+
+        for k, (a, b) in enumerate(results):
+            pltpu.make_async_copy(a.at[i], b.at[i], outs.at[k, i]).start()
+        return carry
+
+    lax.fori_loop(0, GROUP, block, 0)
+    wq_out = pltpu.make_async_copy(wqkv, wqkv_o, ls.at[9])
+    wq_out.start()
+    og.relay3()
+    for c in pc.values():
+        c.wait_send()
+    arrived(3)
+    for c in (dring, uring):
+        c.finish()
+    xg.sent()
+    dg.finish()
+    og.finish()
+    for m in range(1, GROUP):
+        rcopy(mixs.at[p ^ m], mixo.at[p], ms.at[m], mr.at[m], me ^ m).wait()
+    pltpu.make_async_copy(mixs.at[p], mixo.at[p], ls.at[8]).wait()
+    for k, (a, b) in enumerate(results):
+        for i in range(GROUP):
+            pltpu.make_async_copy(a.at[i], b.at[i], outs.at[k, i]).wait()
+    wq_out.wait()
+
+
+def front(n, lengths, x, wq, wk, wv, wg, wu, wo, wd, gn, dy):
     groups = n // GROUP
     r = wq.shape[0]
     wide = 2 * wg.shape[1] // GROUP
     wide1 = 2 * wide // 3
     wd1 = (2 * wd.shape[0] // 3,) + wd.shape[1:]
+    vm = lambda *s: pltpu.VMEM(s, BF16)
+    vf = lambda *s: pltpu.VMEM(s, F32)
     return pl.pallas_call(
-        functools.partial(gather_kernel, n),
+        functools.partial(front_kernel, n),
         out_shape=(
             SDS((GROUP, BLOCK, D), BF16),
-            SDS((groups, GROUP, r, QKV), BF16),
-            SDS((GROUP, r, wide1), BF16),
+            SDS((GROUP, BLOCK, QKV), F32),
+            SDS((GROUP, BLOCK, 128), BF16),
+            SDS((GROUP, BLOCK, 128), BF16),
+            SDS((GROUP, BLOCK, 128), F32),
+            SDS((GROUP, 8, 2 * BLOCK), F32),
+            SDS((GROUP, BLOCK, 128), BF16),
+            SDS((GROUP, BLOCK, D), BF16),
+            SDS((groups, GROUP, r, wide1), BF16),
             SDS((GROUP, r, wide - wide1), BF16),
-            SDS((groups,) + wo.shape, BF16),
+            SDS((groups, GROUP) + wo.shape, BF16),
             SDS((groups,) + wd1, BF16),
+            SDS((D, QKV), BF16),
             SDS((1, gn.shape[1] * n), F32),
             SDS((ROWS, 128), F32),
             SDS((ROWS, 128), F32),
         ),
-        in_specs=[SM] + [HB] * 9,
-        out_specs=(HB,) * 6 + (VM, VM, VM),
-        scratch_shapes=[
-            pltpu.VMEM(w, BF16)
-            for w in (x.shape, gn.shape, wq.shape, wk.shape, wv.shape, wo.shape, wd1, wg.shape, wu.shape)
-        ]
+        in_specs=[SM] + [HB] * 10,
+        out_specs=(HB,) * 13 + (VM,) * 3,
+        scratch_shapes=[vm(GROUP, BLOCK, D)]
+        + [vm(*s) for s in (gn.shape, wq.shape, wk.shape, wv.shape, wo.shape, wd1, wg.shape, wu.shape, dy.shape)]
         + [
-            pltpu.VMEM((GROUP, r, QKV), BF16),
-            pltpu.VMEM((GROUP, r, wide1), BF16),
-            pltpu.VMEM((GROUP, r, wide - wide1), BF16),
-            pltpu.VMEM((8, 128), F32),
-            pltpu.VMEM((groups, GROUP, 8, 128), F32),
-            DMA((9,)),
-            DMA((7,)),
+            vm(GROUP, r, QKV),
+            vm(GROUP, r, wide1),
+            vm(GROUP, r, wide - wide1),
+            vf(8, 128),
+            vf(groups, GROUP, 8, 128),
+            vm(groups, GROUP, r, QKV),
+            vm(groups, *wo.shape),
+            vm(D, QKV),
+            vm(GROUP, BLOCK, D),
+            vf(GROUP, BLOCK, QKV),
+            vm(GROUP, BLOCK, 128),
+            vm(GROUP, BLOCK, 128),
+            vf(GROUP, BLOCK, 128),
+            vf(GROUP, 8, 2 * BLOCK),
+            vm(GROUP, BLOCK, 128),
+            vm(ROWS, HEAD),
+            vm(ROWS, 128),
+            vf(2 * BLOCK, 128),
+            DMA((10,)),
+            DMA((10,)),
+            DMA((14,)),
+            DMA((14,)),
+            DMA((14,)),
+            DMA((14,)),
             DMA((14,)),
             DMA((14,)),
             DMA((4, 7)),
             DMA((4, 7)),
-            DMA((4, ring_count(n))),
-            DMA((4, ring_count(n))),
+            DMA((5, ring_count(n))),
+            DMA((5, ring_count(n))),
+            DMA((GROUP,)),
+            DMA((GROUP,)),
+            DMA((6, GROUP)),
         ],
         compiler_params=pltpu.CompilerParams(collective_id=1, has_side_effects=True, vmem_limit_bytes=VMEM_LIMIT),
-        name="gather_all",
-    )(lengths, x, wq, wk, wv, wg, wu, wo, wd, gn)
-
-
-def swap_halves(v):
-    lane = lax.broadcasted_iota(jnp.int32, v.shape, 1)
-    low = lax.rem(lane, HEAD) < HEAD // 2
-    width = v.shape[1]
-    return jnp.where(low, pltpu.roll(v, width - HEAD // 2, 1), pltpu.roll(v, HEAD // 2, 1))
-
-
-def head_mean(v):
-    row = lax.broadcasted_iota(jnp.int32, (128, 128), 0)
-    lane = lax.broadcasted_iota(jnp.int32, (128, 128), 1)
-    same = jnp.where((row < HEAD) == (lane < HEAD), 1.0 / HEAD, 0.0).astype(BF16)
-    high = v.astype(BF16)
-    low = (v - high.astype(F32)).astype(BF16)
-    return nn(high, same) + nn(low, same)
-
-
-def head_gains(g_ref):
-    t = g_ref[:, 2 * D :]
-    t = jnp.broadcast_to(t, (8, 128))
-    lane = lax.broadcasted_iota(jnp.int32, (8, 128), 1)
-    other = pltpu.roll(t, HEAD, 1)
-    return jnp.where(lane < HEAD, t, other)[0:1, :], jnp.where(lane < HEAD, other, t)[0:1, :]
-
-
-def seq_start(row, len_ref, g):
-    e1 = len_ref[g, 0]
-    e2 = e1 + len_ref[g, 1]
-    e3 = e2 + len_ref[g, 2]
-    zero = row * 0
-    s = jnp.where(row >= e1, zero + e1, zero)
-    s = jnp.where(row >= e2, zero + e2, s)
-    return jnp.where(row >= e3, zero + e3, s)
-
-
-def windows(i, window):
-    for low, high, count in ((0, 1, 2), (2, 3, 4), (4, 7, WINDOW + 1)):
-
-        @pl.when((i >= low) & (i <= high))
-        def _():
-            window(jnp.maximum(i - WINDOW, 0), count)
-
-
-def attn_fwd_kernel(n, len_ref, x_ref, w_ref, g_ref, ct_ref, st_ref, dy_, w2_, wo_, h_ref, raw_ref, q_ref, kv_ref, mixf_ref, lse_ref, mixo, dyo, w2o, woo, k_s, v_s, acc, dy, w2, wo, mixs, fs, ls, ds_, dr, os_, orr, zs, zr, ms, mr):
-    i = pl.program_id(0)
-    me, p, g, groups, zq, zg = places(n)
-    hd, hw, ho = halves(BLOCK), halves(GROUP), halves(wo.shape[0])
-    dg = PlaneGather(me, p, lambda h: dy.at[hd(h)], lambda b, h: dyo.at[b, hd(h)], ds_, dr, ls.at[pl.ds(0, 2)])
-    og = PlaneGather(me, p, lambda h: wo.at[ho(h)], lambda b, h: woo.at[ho(h), b], os_, orr, ls.at[pl.ds(2, 2)])
-    wring = Ring(n, p, g, lambda h: w2.at[hw(h)], lambda b, h: w2o.at[b, hw(h)], zs, zr, ls.at[5])
-    fetch = [pltpu.make_async_copy(a, b, fs.at[k]) for k, (a, b) in enumerate(((dy_, dy), (wo_, wo), (w2_, w2)))]
-
-    @pl.when(i == 0)
-    def _():
-        start_all(fetch)
-        k_s[: WINDOW * BLOCK] = jnp.zeros((WINDOW * BLOCK, HEAD), BF16)
-        v_s[: WINDOW * BLOCK] = jnp.zeros((WINDOW * BLOCK, 128), BF16)
-        barrier([me ^ m for m in range(1, GROUP)] + zq)
-        fetch[2].wait()
-        wring.start()
-        fetch[0].wait()
-        dg.start_first()
-
-    @pl.when(i == 2)
-    def _():
-        dg.start_second()
-
-    @pl.when(i == 3)
-    def _():
-        dg.relay1()
-
-    @pl.when(i == 4)
-    def _():
-        fetch[1].wait()
-        og.start_first()
-
-    @pl.when(i == 5)
-    def _():
-        dg.relay2()
-        wring.relay()
-        og.start_second()
-
-    @pl.when(i == 6)
-    def _():
-        dg.relay3()
-        og.relay1()
-
-    @pl.when(i == 7)
-    def _():
-        og.relay2()
-
-    xb = x_ref[0].astype(F32)
-    r = lax.rsqrt(jnp.mean(xb * xb, axis=-1, keepdims=True) + EPSILON)
-    h = (xb * r * g_ref[:, :D]).astype(BF16)
-    gq, gk = head_gains(g_ref)
-    h_ref[0] = h
-    raw = nn(h, w_ref[...])
-    raw_ref[0] = raw
-    ct, st = ct_ref[...], st_ref[...]
-    qraw, kvraw = raw[:, :128], raw[:, 128:]
-    qn = qraw * lax.rsqrt(head_mean(qraw * qraw) + EPSILON) * gq
-    q = (qn * ct + swap_halves(qn) * st).astype(BF16)
-    kn = kvraw * lax.rsqrt(head_mean(kvraw * kvraw) + EPSILON) * gk
-    k = (kn * ct + swap_halves(kn) * st).astype(BF16)
-    lane = lax.broadcasted_iota(jnp.int32, (BLOCK, 128), 1)
-    kv = jnp.where(lane < HEAD, k.astype(F32), kvraw).astype(BF16)
-    q_ref[0] = q
-    kv_ref[0] = kv
-    k_s[pl.ds(i * BLOCK, BLOCK), :] = kv[:, :HEAD]
-    v_s[pl.ds(i * BLOCK, BLOCK), :] = jnp.where(lane < HEAD, pltpu.roll(kvraw, HEAD, 1), 1.0).astype(BF16)
-    q2 = jnp.concatenate([q[:, :HEAD], q[:, HEAD:]], axis=0)
-    row = lax.broadcasted_iota(jnp.int32, (2 * BLOCK, 1), 0)
-    qrow = i * BLOCK + jnp.where(row >= BLOCK, row - BLOCK, row)
-    qstart = seq_start(qrow, len_ref, g)
-
-    def window(first, count):
-        at = pl.ds(pl.multiple_of(first * BLOCK, BLOCK), count * BLOCK)
-        kc = lax.broadcasted_iota(jnp.int32, (2 * BLOCK, count * BLOCK), 1) + first * BLOCK
-        ok = (kc >= qstart) & (kc <= qrow)
-        e = jnp.where(ok, jnp.exp2(nt(q2, k_s[at, :]) * (SCALE * LOG2E)), 0.0).astype(BF16)
-        acc[...] = nn(e, v_s[at, :])
-
-    windows(i, window)
-    total = acc[:, HEAD:]
-    m = acc[:, :HEAD] / total
-    both = jnp.concatenate([m[:BLOCK], m[BLOCK:]], axis=1)
-    mixf_ref[0] = both
-    mixs[i] = both.astype(BF16)
-
-    @pl.when(i == p)
-    def _():
-        pltpu.make_async_copy(mixs.at[i], mixo.at[p], ls.at[4]).start()
-
-    @pl.when(i != p)
-    def _():
-        rcopy(mixs.at[i], mixo.at[p], ms.at[p ^ i], mr.at[p ^ i], me ^ p ^ i).start()
-
-    lse_ref[0] = jnp.log2(total.T)[:8, :]
-
-    @pl.when(i == 7)
-    def _():
-        og.relay3()
-        dg.finish()
-        wring.finish()
-        og.finish()
-        for m in range(1, GROUP):
-            rcopy(mixs.at[p ^ m], mixo.at[p], ms.at[m], mr.at[m], me ^ m).wait()
-        pltpu.make_async_copy(mixs.at[p], mixo.at[p], ls.at[4]).wait()
-
-
-def attn_fwd(n, lengths, x_all, wqkv, gvec, ct, st, dy, w2, wo):
-    groups = n // GROUP
-    blk = lambda c: pl.BlockSpec((1, BLOCK, c), lambda i: (i, 0, 0))
-    whole = lambda s: pl.BlockSpec(s, lambda i: (0,) * len(s), pipeline_mode=pl.Buffered(1))
-    nb = ROWS // BLOCK
-    return pl.pallas_call(
-        functools.partial(attn_fwd_kernel, n),
-        grid=(nb,),
-        in_specs=[
-            SM,
-            blk(D),
-            whole((D, QKV)),
-            whole(gvec.shape),
-            pl.BlockSpec((BLOCK, 128), lambda i: (i, 0)),
-            pl.BlockSpec((BLOCK, 128), lambda i: (i, 0)),
-            HB,
-            HB,
-            HB,
-        ],
-        out_specs=(blk(D), blk(QKV), blk(128), blk(128), blk(128), pl.BlockSpec((1, 8, 2 * BLOCK), lambda i: (i, 0, 0)), HB, HB, HB, HB),
-        out_shape=(
-            SDS((nb, BLOCK, D), BF16),
-            SDS((nb, BLOCK, QKV), F32),
-            SDS((nb, BLOCK, 128), BF16),
-            SDS((nb, BLOCK, 128), BF16),
-            SDS((nb, BLOCK, 128), F32),
-            SDS((nb, 8, 2 * BLOCK), F32),
-            SDS((GROUP, BLOCK, 128), BF16),
-            SDS((GROUP, BLOCK, D), BF16),
-            SDS((groups,) + w2.shape, BF16),
-            SDS((groups, GROUP) + wo.shape[1:], BF16),
-        ),
-        scratch_shapes=[
-            pltpu.VMEM((ROWS, HEAD), BF16),
-            pltpu.VMEM((ROWS, 128), BF16),
-            pltpu.VMEM((2 * BLOCK, 128), F32),
-            pltpu.VMEM(dy.shape, BF16),
-            pltpu.VMEM(w2.shape, BF16),
-            pltpu.VMEM(wo.shape, BF16),
-            pltpu.VMEM((GROUP, BLOCK, 128), BF16),
-            DMA((3,)),
-            DMA((6,)),
-            DMA((14,)),
-            DMA((14,)),
-            DMA((14,)),
-            DMA((14,)),
-            DMA((ring_count(n),)),
-            DMA((ring_count(n),)),
-            DMA((GROUP,)),
-            DMA((GROUP,)),
-        ],
-        compiler_params=pltpu.CompilerParams(
-            collective_id=5, has_side_effects=True, dimension_semantics=("arbitrary",), vmem_limit_bytes=VMEM_LIMIT
-        ),
-        cost_estimate=pl.CostEstimate(flops=4 * 10**9, bytes_accessed=16 << 20, transcendentals=4 * 10**6),
-        name="attn_fwd",
-    )(lengths, *in_hbm(x_all, wqkv, gvec, ct, st), dy, w2, wo)
+        name="front",
+    )(lengths, x, wq, wk, wv, wg, wu, wo, wd, gn, dy)
 
 
 def norm_back(dyv, xv, gain):
@@ -804,6 +772,7 @@
         dys[b] = jnp.concatenate([dy[holder(2 * b)], dy[holder(2 * b + 1)]], axis=0)
         h2t[:, pl.ds(pl.multiple_of(b * BLOCK, BLOCK), BLOCK)] = h2[b].T
         acts[b, :, :f1], dgu1[b] = unit_grads(h2[b], dys[b], w21[...], wds[:f1])
+        part[b] = nt(dgu1[b], w21[...]).astype(BF16)
         return carry
 
     lax.fori_loop(0, GROUP, first, 0)
@@ -841,7 +810,7 @@
 
         b = p ^ (GROUP - 1 - t)
         acts[b, :, f1:], dgu2[b] = unit_grads(h2[b], dys[b], w22[...], wds[f1:])
-        part[b] = (nt(dgu1[b], w21[...]) + nt(dgu2[b], w22[...])).astype(BF16)
+        part[b] = (part[b].astype(F32) + nt(dgu2[b], w22[...])).astype(BF16)
         return carry
 
     lax.fori_loop(0, GROUP, second, 0)
@@ -1147,12 +1116,13 @@
     )(lengths, dmh, q, kv, lse, mixf, h, raw, wqkv, gvec, ct, st, po, res, dwo, dw2, dwd, t21, dgf)
 
 
-def final_kernel(n, dh, x, gmid, g_ref, dw1, two, t2, gpart, gtok, o1, o2, oo, og, t1, gin, gsum, gz, ps, pr, gs, gr, *rest):
+def final_kernel(n, dh, x_, gmid_, g_ref, dw1, two, t2, gpart, gtok, o1, o2, oo, og, mine, x, gmid, fs, t1, gin, gsum, gz, ps, pr, gs, gr, *rest):
     me, p, g, groups, zq, zg = places(n)
     nz = groups - 1
     share = g_ref.shape[1] // n
+    fetch = bring([(dh.at[p ^ (2 * i)], mine.at[i]) for i in (3, 1, 2, 0)] + [(x_, x), (gmid_, gmid)], fs)
     barrier([me ^ m for m in range(1, GROUP)] + zq)
-    red = PlaneReduce(me, lambda b: dh.at[b], *rest[:7])
+    red = PlaneReduce(me, lambda b: dh.at[b], *rest[:7], own=lambda i: mine.at[i])
     ring1 = RingReduce(n, p, g, dw1, *rest[7:13])
     ringo = RingReduce(n, p, g, two, *rest[13:19])
     red.start()
@@ -1168,6 +1138,7 @@
             pc.append(c)
         out[p] = src[p]
 
+    wait_all(fetch)
     red.phase1()
     exchange(1, t2, o2)
     tot = gpart[...]
@@ -1213,9 +1184,13 @@
             SDS(two.shape[1:], F32),
             SDS((8, 128), F32),
         ),
-        in_specs=[VM] * 8,
+        in_specs=[HB, HB, HB] + [VM] * 5,
         out_specs=(VM,) * 5,
         scratch_shapes=[
+            pltpu.VMEM((4, BLOCK, D), BF16),
+            pltpu.VMEM(x.shape, BF16),
+            pltpu.VMEM(gmid.shape, F32),
+            DMA((6,)),
             pltpu.VMEM(dw1.shape[1:], BF16),
             pltpu.VMEM((7, 24, 128), F32),
             pltpu.VMEM((24, 128), F32),
@@ -1289,7 +1264,7 @@
     wok = r // 16 if r % 16 == 0 else 1
     wdk = 9 if ffc % 144 == 0 else 3
     wo_blk, wd_blk = (wok, r // wok, D), (wdk, ffc // wdk, D)
-    x_all, w1, w21, w22, wo, wd1, gvec, ct, st = gather_all(
+    h, raw, q, kv, mixf, lse, mix, dy_all, w21, w22, wo, wd1, wqkv, gvec, ct, st = front(
         n,
         seq_lengths,
         tokens,
@@ -1301,10 +1276,7 @@
         w_out.reshape(wo_blk),
         w_down.reshape(wd_blk),
         norm_gains.reshape(1, share),
-    )
-    wqkv = w1.reshape(D, QKV)
-    h, raw, q, kv, mixf, lse, mix, dy_all, w21, wo = attn_fwd(
-        n, seq_lengths, x_all, wqkv, gvec, ct, st, out_grad, w21, wo.reshape(groups, r, D)
+        out_grad,
     )
     res, gmid, dgf, dwo, dmh, po, t21, dw22, dwd = ffn_block(
         n,

time: 234 us -> 227 us (0.970)
  Pallas kernels: 233 us -> 226 us
    pallas_call x2 -> x1, Pallas kernels: 81.8 us -> 78.2 us  [front(): pl.pallas_call(functools.partial(front_kernel, n), out_shape=(SDS((GROUP,...]
    pallas_call x1, Pallas kernels: 70.9 us -> 68.1 us  [ffn_block(): pl.pallas_call(functools.partial(ffn_block_kernel, n), out_shape=(SDS((BL...]
where the time goes in v6:
time: 227 us
  Pallas kernels  226 us (100%)
    pallas_call x1, Pallas kernels, front(): pl.pallas_call(functools.partial(front_kernel, n), out_shape=(SDS((GROUP,...  78.2 us
    pallas_call x1, Pallas kernels, ffn_block(): pl.pallas_call(functools.partial(ffn_block_kernel, n), out_shape=(SDS((BL...  68.1 us
    pallas_call x1, Pallas kernels, attn_bwd(): pl.pallas_call(functools.partial(attn_bwd_kernel, n), grid=(nb,), in_spec...  44.3 us
    pallas_call x1, Pallas kernels, final(): pl.pallas_call(functools.partial(final_kernel, n), out_shape=(SDS((BLOCK,...  31.3 us

profile of v6, /device:TPU:0, one launch (start us, length us, event | category | flops | bytes accessed | tf_op | source)
XLA Modules:
  0.0 226.6 jit_solution(11274513206180019593)
XLA Ops:
  0.6 78.2 %front.1 = (bf16[8,256,1024]{2,1,0:T(8,128)(2,1)}, f32[8,256,256]{2,1,0:T(8,128)}, bf16[8,256,128]{2,1,0:T(8,128)(2,1)}, bf16[8,256,128]{2,1,0:T(8,128)(2,1)}, f...) custom-call(s32[4,4]{1,0:T(4,128)} %len_ref.3, ...), custom_call_target="tpu_custom_call" | custom-call | tf_op jit(solution)/shard_map/front/pallas_call | solution.py:608
  78.8 68.1 %ffn_block.1 = (f32[256,1024]{1,0:T(8,128)}, f32[256,1024]{1,0:T(8,128)}, f32[1,1024]{1,0:T(1,128)}, bf16[1024,1024]{1,0:T(8,128)(2,1)}, bf16[8,256,128]{2,1,0:T...) custom-call(s32[4,16]{1,0:T(4,128)} %order.1, ...), custom_call_target="tpu_custom_call" | custom-call | tf_op jit(solution)/shard_map/ffn_block/pallas_call | solution.py:866
  146.9 44.3 %attn_bwd.1 = (bf16[8,256,1024]{2,1,0:T(8,128)(2,1)}, bf16[1024,256]{1,0:T(8,128)(2,1)}, f32[24,128]{1,0:T(8,128)}, bf16[256,1024]{1,0:T(8,128)(2,1)}, bf16[4,32...) custom-call(s32[4,4]{1,0:T(4,128)} %len_ref.3, ...), custom_call_target="tpu_custom_call" | custom-call | flops 8000000000 | bytes 16777216 | tf_op jit(solution)/shard_map/attn_bwd/pallas_call | solution.py:1051
  191.2 31.3 %final.1 = (f32[256,1024]{1,0:T(8,128)}, bf16[8,32,256]{2,1,0:T(8,128)(2,1)}, bf16[8,32,384]{2,1,0:T(8,128)(2,1)}, f32[2,16,1024]{2,1,0:T(8,128)}, f32[8,128]{1,0:T(8,128)}) custom-call(bf16[8,256,1024]{2,1,0:T(8,128)(2,1)} %get-tuple-element.83.dh, bf16[256,1024]{1,0:T(8,128)(2,1)} %x_.5, f32[256,1024]{1,0:T(8,128)} %get-tuple-element.84.gmid_, ...), custom_call_target="tpu_custom_call" | custom-call | tf_op jit(solution)/shard_map/final/pallas_call | solution.py:1178
  222.5 4.0 %unpack.1 = (bf16[256,1024]{1,0:T(8,128)(2,1)}, f32[256,1024]{1,0:T(8,128)}, f32[32,1024]{1,0:T(8,128)}, f32[32,512]{1,0:T(8,128)}, f32[32,512]{1,0:T(8,128)}, /...) custom-call(bf16[256,1024]{1,0:T(8,128)(2,1)} %get-tuple-element.82.r, ...), custom_call_target="tpu_custom_call" | custom-call | tf_op jit(solution)/shard_map/unpack/pallas_call | solution.py:1238

commit v7 on v6

--- a/solution.py
+++ b/solution.py
@@ -405,16 +405,13 @@
     )
     share = gn.shape[1]
     ffc = wg.shape[1] // (groups * GROUP)
-    big = 2 * ffc // 3
+    big = 5 * ffc // 9
     r = wq.shape[0]
     barrier([me ^ m for m in range(1, GROUP)] + zq)
     hx, ho = halves(BLOCK), halves(groups)
     xg = PlaneGather(me, p, lambda h: xa.at[p, hx(h)], lambda b, h: xa.at[b, hx(h)], xs, xr)
     dg = PlaneGather(me, p, lambda h: dy.at[hx(h)], lambda b, h: dyo.at[b, hx(h)], ds_, dr, ls.at[pl.ds(0, 2)])
     og = PlaneGather(me, p, lambda h: woz.at[ho(h)], lambda b, h: woo.at[ho(h), b], os_, orr, ls.at[pl.ds(2, 2)])
-    fetch[0].wait()
-    xg.start_first()
-
     def ring(k, src, dst, local=None):
         hk = halves(dst.shape[1])
         return Ring(n, p, g, lambda h: src.at[hk(h)], lambda b, h: dst.at[b, hk(h)], zs.at[k], zr.at[k], local)
@@ -433,11 +430,19 @@
         for m in range(1, GROUP):
             pc[k, m].wait_recv()
 
+
+    def pack(buf, low, high):
+        for b in range(GROUP):
+            at = [slice((GROUP * k + b) * ffc + low, (GROUP * k + b) * ffc + high) for k in range(groups)]
+            buf[b] = jnp.concatenate([wg[:, k] for k in at] + [wu[:, k] for k in at], axis=1)
+
+    fetch[0].wait()
+    xg.start_first()
     fetch[1].wait()
     gt[...] = jnp.zeros_like(gt)
     gt[0:1, :share] = gn[...].astype(F32)
+    gto[g, p] = gt[...]
     exchange(1, lambda b: gt, gto.at[g, p])
-    gto[g, p] = gt[...]
     wait_all(fetch[2:5])
     for b in range(GROUP):
         a1[b, :, :128] = wq[:, 128 * b : 128 * (b + 1)]
@@ -445,31 +450,26 @@
         a1[b, :, 128:] = jnp.concatenate([wk[:, at], wv[:, at]], axis=1)
     exchange(0, lambda b: a1.at[b], w1v.at[g, p])
     w1v[g, p] = a1[p]
-    wait_all(fetch[5:7])
+    fetch[5].wait()
     oring.start()
+    fetch[6].wait()
     dring.start()
     wait_all(fetch[7:9])
-    for buf, low, high in ((b1, 0, big), (b2, big, ffc)):
-        for b in range(GROUP):
-            at = [slice((GROUP * k + b) * ffc + low, (GROUP * k + b) * ffc + high) for k in range(groups)]
-            buf[b] = jnp.concatenate([wg[:, k] for k in at] + [wu[:, k] for k in at], axis=1)
+    pack(b1, 0, big)
     exchange(2, lambda b: b1.at[b], w21o.at[g, p])
+    local = start_all([pltpu.make_async_copy(b1.at[p], w21o.at[g, p], ls.at[6])])
+    pack(b2, big, ffc)
     exchange(3, lambda b: b2.at[b], w22o.at[p])
+    local += start_all([pltpu.make_async_copy(b2.at[p], w22o.at[p], ls.at[7])])
     xg.start_second()
-    local = start_all(
-        [
-            pltpu.make_async_copy(b1.at[p], w21o.at[g, p], ls.at[6]),
-            pltpu.make_async_copy(b2.at[p], w22o.at[p], ls.at[7]),
-        ]
-    )
     arrived(0)
     wring.start()
     arrived(1)
     gring.start()
+    arrived(2)
+    local[0].wait()
+    uring.start()
     xg.relay1()
-    arrived(2)
-    wait_all(local)
-    uring.start()
     row = lax.broadcasted_iota(jnp.int32, (1, ROWS), 1)
     position = (row - seq_start(row, len_ref, g)).astype(F32)
     index = lax.broadcasted_iota(jnp.int32, (HEAD // 2, 1), 0).astype(F32)
@@ -482,11 +482,10 @@
     xg.relay2()
     fetch[9].wait()
     dg.start_first()
-    for c in (oring, wring, gring):
+    for c in (wring, gring):
         c.relay()
     xg.relay3()
     dg.start_second()
-    dring.relay()
     wring.finish()
     gring.finish()
     for k in range(groups * GROUP):
@@ -499,6 +498,10 @@
     results = ((h_s, h_o), (raw_s, raw_o), (q_s, q_o), (kv_s, kv_o), (mixf_s, mixf_o), (lse_s, lse_o))
 
     def block(i, carry):
+        @pl.when(i == 0)
+        def _():
+            oring.relay()
+
         @pl.when(i == 1)
         def _():
             oring.finish()
@@ -509,10 +512,13 @@
             dg.relay1()
             og.start_second()
 
+        @pl.when(i == 3)
+        def _():
+            uring.relay()
+
         @pl.when(i == 4)
         def _():
             dg.relay2()
-            uring.relay()
 
         @pl.when(i == 5)
         def _():
@@ -521,6 +527,7 @@
         @pl.when(i == 6)
         def _():
             dg.relay3()
+            dring.relay()
 
         @pl.when(i == 7)
         def _():
@@ -583,6 +590,7 @@
     for c in pc.values():
         c.wait_send()
     arrived(3)
+    local[1].wait()
     for c in (dring, uring):
         c.finish()
     xg.sent()
@@ -601,8 +609,8 @@
     groups = n // GROUP
     r = wq.shape[0]
     wide = 2 * wg.shape[1] // GROUP
-    wide1 = 2 * wide // 3
-    wd1 = (2 * wd.shape[0] // 3,) + wd.shape[1:]
+    wide1 = 5 * wide // 9
+    wd1 = (5 * wd.shape[0] // 9,) + wd.shape[1:]
     vm = lambda *s: pltpu.VMEM(s, BF16)
     vf = lambda *s: pltpu.VMEM(s, F32)
     return pl.pallas_call(
@@ -688,7 +696,7 @@
     return (sg * up).astype(BF16), jnp.concatenate([dg, (da * sg).astype(BF16)], axis=1)
 
 
-def ffn_block_kernel(n, order, mix_, x_, wo_, g_ref, w21_, w22_, wd1_, wd2_, dy_, res, gmid, dgf, dwo, dmh, po, t21, dw22, dwd, x, wo, w21, dy, fs, mbuf, h2, h2t, w2v, w22, wdv, wds, dys, acts, dgu1, dgu2, dw21, part, mown, stage, hs, hr, os_, qs, qr, zs, zr, *red_refs):
+def ffn_block_kernel(n, order, mix_, x_, wo_, g_ref, w21_, w22_, wd1_, wd2_, dy_, res, gmid, dgf, dwo, dmh, po, t21, dw22, dwd1, dwd2, x, wo, w21, dy, fs, mbuf, h2, h2t, w2v, w22, wdv, wds, dys, acts1, acts2, dgu1, dgu2, dw21, part, mown, stage, hs, hr, os_, qs, qr, zs, zr, *red_refs):
     me, p, g, groups, zq, zg = places(n)
     f1 = wd1_.shape[0]
     f2 = wds.shape[0] - f1
@@ -771,7 +779,7 @@
         b = p ^ t
         dys[b] = jnp.concatenate([dy[holder(2 * b)], dy[holder(2 * b + 1)]], axis=0)
         h2t[:, pl.ds(pl.multiple_of(b * BLOCK, BLOCK), BLOCK)] = h2[b].T
-        acts[b, :, :f1], dgu1[b] = unit_grads(h2[b], dys[b], w21[...], wds[:f1])
+        acts1[b], dgu1[b] = unit_grads(h2[b], dys[b], w21[...], wds[:f1])
         part[b] = nt(dgu1[b], w21[...]).astype(BF16)
         return carry
 
@@ -809,17 +817,17 @@
             red.chip_x()
 
         b = p ^ (GROUP - 1 - t)
-        acts[b, :, f1:], dgu2[b] = unit_grads(h2[b], dys[b], w22[...], wds[f1:])
+        acts2[b], dgu2[b] = unit_grads(h2[b], dys[b], w22[...], wds[f1:])
         part[b] = (part[b].astype(F32) + nt(dgu2[b], w22[...])).astype(BF16)
         return carry
 
     lax.fori_loop(0, GROUP, second, 0)
-    dw = tn(acts[...].reshape(ROWS, f1 + f2), dys[...].reshape(ROWS, D)).astype(BF16)
-    l1 = dwd.shape[1] - wdv.shape[1]
-    e1 = f1 // groups
-    for k in range(groups):
-        dwd[k, :l1] = dw[k * e1 : (k + 1) * e1].reshape((l1,) + dwd.shape[2:])
-        dwd[k, l1:] = dw[f1 + k * each : f1 + (k + 1) * each].reshape(wdv.shape[1:])
+    dy_rows = dys[...].reshape(ROWS, D)
+    for acts, out, rows in ((acts1, dwd1, f1), (acts2, dwd2, f2)):
+        dw = tn(acts[...].reshape(ROWS, rows), dy_rows).astype(BF16)
+        part_rows = rows // groups
+        for k in range(groups):
+            out[k] = dw[k * part_rows : (k + 1) * part_rows].reshape(out.shape[1:])
     red.phase2()
     ring21.relay()
     dw22[...] = nn(h2t[...], dgu2[...].reshape(ROWS, 2 * f2)).astype(BF16)
@@ -844,7 +852,7 @@
         def _():
             pltpu.make_async_copy(stage.at[slot], po.at[b - 2], os_.at[slot]).wait()
 
-        stage[slot] = nn(acts[b], wds[...]).astype(BF16)
+        stage[slot] = (nn(acts1[b], wds[:f1]) + nn(acts2[b], wds[f1:])).astype(BF16)
         pltpu.make_async_copy(stage.at[slot], po.at[b], os_.at[slot]).start()
         return carry
 
@@ -860,7 +868,8 @@
     groups = n // GROUP
     r = w22.shape[1]
     f1, f2 = w21.shape[1] // 2, w22.shape[2] // 2
-    wd2 = (wd.shape[0] // 3,) + wd.shape[1:]
+    wd2 = (4 * wd.shape[0] // 9,) + wd.shape[1:]
+    wd1_blk = (5 * wd.shape[0] // 9,) + wd.shape[1:]
     blk = (GROUP, r, 2 * f1)
     vm = lambda *s: pltpu.VMEM(s, BF16)
     return pl.pallas_call(
@@ -874,10 +883,11 @@
             SDS((GROUP, BLOCK, D), BF16),
             SDS(blk, BF16),
             SDS((D, 2 * f2), BF16),
-            SDS((groups,) + wd.shape, BF16),
+            SDS((groups,) + wd1_blk, BF16),
+            SDS((groups,) + wd2, BF16),
         ),
         in_specs=[SM, HB, HB, HB, VM, HB, HB, HB, HB, HB],
-        out_specs=(VM, VM, VM, VM, VM, HB, VM, VM, VM),
+        out_specs=(VM, VM, VM, VM, VM, HB, VM, VM, VM, VM),
         scratch_shapes=[
             vm(BLOCK, D),
             vm(D, D),
@@ -892,7 +902,8 @@
             vm(groups, *wd2),
             vm(f1 + f2, D),
             vm(GROUP, BLOCK, D),
-            vm(GROUP, BLOCK, f1 + f2),
+            vm(GROUP, BLOCK, f1),
+            vm(GROUP, BLOCK, f2),
             vm(GROUP, BLOCK, 2 * f1),
             vm(GROUP, BLOCK, 2 * f2),
             vm(groups, *blk),
@@ -1116,7 +1127,7 @@
     )(lengths, dmh, q, kv, lse, mixf, h, raw, wqkv, gvec, ct, st, po, res, dwo, dw2, dwd, t21, dgf)
 
 
-def final_kernel(n, dh, x_, gmid_, g_ref, dw1, two, t2, gpart, gtok, o1, o2, oo, og, mine, x, gmid, fs, t1, gin, gsum, gz, ps, pr, gs, gr, *rest):
+def final_kernel(n, dh, x_, gmid_, g_ref, dw1, two, t2, gpart, dwd, gtok, o1, o2, oo, og, od, mine, x, gmid, fs, t1, gin, gsum, gz, ps, pr, gs, gr, *rest):
     me, p, g, groups, zq, zg = places(n)
     nz = groups - 1
     share = g_ref.shape[1] // n
@@ -1125,10 +1136,12 @@
     red = PlaneReduce(me, lambda b: dh.at[b], *rest[:7], own=lambda i: mine.at[i])
     ring1 = RingReduce(n, p, g, dw1, *rest[7:13])
     ringo = RingReduce(n, p, g, two, *rest[13:19])
+    ringd = RingReduce(n, p, g, dwd, *rest[19:25])
     red.start()
     gc = start_all([rcopy(gpart, gin.at[m - 1], gs.at[m - 1], gr.at[m - 1], me ^ m) for m in range(1, GROUP)])
     ring1.start()
     ringo.start()
+    ringd.start()
     pc = []
 
     def exchange(k, src, out):
@@ -1153,6 +1166,7 @@
     t1[...] = ring1.finish().astype(BF16)
     exchange(0, t1, o1)
     oo[...] = ringo.finish()
+    ringd.relay()
     for s in range(nz):
         gzc[s].wait_recv()
         tot = tot + gz[s]
@@ -1167,12 +1181,13 @@
     og[...] = jnp.where(lane < 128 - off, turn(first), turn(first + 1))
     dx, _ = norm_back(red.phase3(), x[...].astype(F32), g_ref[:, :D])
     gtok[...] = gmid[...] + dx
+    od[...] = ringd.finish()
     wait_all(pc)
     for c in gc:
         c.wait_send()
 
 
-def final(n, dh, x, gmid, gvec, dw1, two, t2, gpart):
+def final(n, dh, x, gmid, gvec, dw1, two, t2, gpart, dwd):
     groups = n // GROUP
     nz = groups - 1
     return pl.pallas_call(
@@ -1183,9 +1198,10 @@
             SDS(t2.shape, BF16),
             SDS(two.shape[1:], F32),
             SDS((8, 128), F32),
+            SDS(dwd.shape[1:], F32),
         ),
-        in_specs=[HB, HB, HB] + [VM] * 5,
-        out_specs=(VM,) * 5,
+        in_specs=[HB, HB, HB] + [VM] * 6,
+        out_specs=(VM,) * 6,
         scratch_shapes=[
             pltpu.VMEM((4, BLOCK, D), BF16),
             pltpu.VMEM(x.shape, BF16),
@@ -1202,17 +1218,19 @@
         ]
         + plane_scratch((BLOCK, D))
         + ring_scratch(n, dw1.shape[1:])
-        + ring_scratch(n, two.shape[1:]),
+        + ring_scratch(n, two.shape[1:])
+        + ring_scratch(n, dwd.shape[1:]),
         compiler_params=pltpu.CompilerParams(collective_id=4, has_side_effects=True, vmem_limit_bytes=VMEM_LIMIT),
         name="final",
-    )(dh, x, gmid, gvec, dw1, two, t2, gpart)
-
-
-def unpack_kernel(groups, result, gtok, o1, o21, o22, oo, od, og, result_o, gtok_o, gq, gk, gv, go, gg, gu, gd, gn):
+    )(dh, x, gmid, gvec, dw1, two, t2, gpart, dwd)
+
+
+def unpack_kernel(groups, result, gtok, o1, o21, o22, oo, od, od2, og, result_o, gtok_o, gq, gk, gv, go, gg, gu, gd, gn):
     result_o[...] = result[...]
     gtok_o[...] = gtok[...]
     go[...] = oo[...]
-    gd[...] = od[...]
+    gd[: od.shape[0]] = od[...]
+    gd[od.shape[0] :] = od2[...]
     gn[...] = og[0:1, : gn.shape[1]]
     for b in range(GROUP):
         gq[:, 128 * b : 128 * (b + 1)] = o1[b, :, :128].astype(F32)
@@ -1222,7 +1240,7 @@
             out[:, 128 * c : 128 * (c + 1)] = jnp.concatenate(pair, axis=1)
     ffc = gg.shape[1] // (groups * GROUP)
     for k, out in enumerate((gg, gu)):
-        big = 2 * ffc // 3
+        big = 5 * ffc // 9
         piece = lambda src, b, c, w: src[b, :, (k * groups + c) * w : (k * groups + c + 1) * w].astype(F32)
         parts = [
             piece(src, b, c, w)
@@ -1233,7 +1251,7 @@
         out[...] = jnp.concatenate(parts, axis=1)
 
 
-def unpack(n, result, gtok, o1, o21, o22, oo, od, og, share):
+def unpack(n, result, gtok, o1, o21, o22, oo, od, od2, og, share):
     r = oo.shape[0]
     return pl.pallas_call(
         functools.partial(unpack_kernel, n // GROUP),
@@ -1246,14 +1264,14 @@
             SDS((r, D), F32),
             SDS((r, FF), F32),
             SDS((r, FF), F32),
-            SDS(od.shape, F32),
+            SDS((od.shape[0] + od2.shape[0], D), F32),
             SDS((1, share), F32),
         ),
-        in_specs=[VM] * 8,
+        in_specs=[VM] * 9,
         out_specs=(VM,) * 10,
         compiler_params=pltpu.CompilerParams(vmem_limit_bytes=VMEM_LIMIT),
         name="unpack",
-    )(result, gtok, o1, o21, o22, oo, od, og)
+    )(result, gtok, o1, o21, o22, oo, od, od2, og)
 
 
 def body(n, tokens, w_query, key_weight, w_value, w_out, w_gate, w_up, w_down, norm_gains, seq_lengths, slot_order, out_grad):
@@ -1262,7 +1280,7 @@
     ffc = w_down.shape[0]
     share = norm_gains.shape[0]
     wok = r // 16 if r % 16 == 0 else 1
-    wdk = 9 if ffc % 144 == 0 else 3
+    wdk = 9
     wo_blk, wd_blk = (wok, r // wok, D), (wdk, ffc // wdk, D)
     h, raw, q, kv, mixf, lse, mix, dy_all, w21, w22, wo, wd1, wqkv, gvec, ct, st = front(
         n,
@@ -1278,7 +1296,7 @@
         norm_gains.reshape(1, share),
         out_grad,
     )
-    res, gmid, dgf, dwo, dmh, po, t21, dw22, dwd = ffn_block(
+    res, gmid, dgf, dwo, dmh, po, t21, dw22, dwd1, dwd2 = ffn_block(
         n,
         slot_order,
         mix,
@@ -1309,11 +1327,11 @@
         res,
         dwo.reshape(groups, GROUP, r, D),
         dw22.reshape(groups, GROUP, r, -1),
-        dwd,
+        dwd1,
         t21,
         dgf,
     )
-    gtok, o1, o22, oo, og = final(
+    gtok, o1, o22, oo, og, od2 = final(
         n,
         dh1,
         tokens,
@@ -1323,8 +1341,9 @@
         two.reshape((groups,) + wo_blk),
         t2,
         gpart,
+        dwd2,
     )
-    outs = unpack(n, result, gtok, o1, o21, o22, oo.reshape(r, D), od.reshape(ffc, D), og, share)
+    outs = unpack(n, result, gtok, o1, o21, o22, oo.reshape(r, D), od.reshape(-1, D), od2.reshape(-1, D), og, share)
     return outs[:-1] + (outs[-1].reshape(share),)
 
 

time: 227 us -> 220 us (0.969)
  Pallas kernels: 226 us -> 219 us
    pallas_call x1, Pallas kernels: 78.2 us -> 73.2 us  [front(): pl.pallas_call(functools.partial(front_kernel, n), out_shape=(SDS((GROUP,...]
where the time goes in v7:
time: 220 us
  Pallas kernels  219 us (100%)
    pallas_call x1, Pallas kernels, front(): pl.pallas_call(functools.partial(front_kernel, n), out_shape=(SDS((GROUP,...  73.2 us
    pallas_call x1, Pallas kernels, ffn_block(): pl.pallas_call(functools.partial(ffn_block_kernel, n), out_shape=(SDS((BL...  66.6 us
    pallas_call x1, Pallas kernels, attn_bwd(): pl.pallas_call(functools.partial(attn_bwd_kernel, n), grid=(nb,), in_spec...  43.9 us
    pallas_call x1, Pallas kernels, final(): pl.pallas_call(functools.partial(final_kernel, n), out_shape=(SDS((BLOCK,...  31.5 us

profile of v7, /device:TPU:0, one launch (start us, length us, event | category | flops | bytes accessed | tf_op | source)
XLA Modules:
  0.0 219.9 jit_solution(3779589754693895008)
XLA Ops:
  0.6 73.2 %front.1 = (bf16[8,256,1024]{2,1,0:T(8,128)(2,1)}, f32[8,256,256]{2,1,0:T(8,128)}, bf16[8,256,128]{2,1,0:T(8,128)(2,1)}, bf16[8,256,128]{2,1,0:T(8,128)(2,1)}, f...) custom-call(s32[4,4]{1,0:T(4,128)} %len_ref.3, ...), custom_call_target="tpu_custom_call" | custom-call | tf_op jit(solution)/shard_map/front/pallas_call | solution.py:616
  73.9 66.6 %ffn_block.1 = (f32[256,1024]{1,0:T(8,128)}, f32[256,1024]{1,0:T(8,128)}, f32[1,1024]{1,0:T(1,128)}, bf16[1024,1024]{1,0:T(8,128)(2,1)}, bf16[8,256,128]{2,1,0:T...) custom-call(s32[4,16]{1,0:T(4,128)} %order.1, ...), custom_call_target="tpu_custom_call" | custom-call | tf_op jit(solution)/shard_map/ffn_block/pallas_call | solution.py:875
  140.5 43.9 %attn_bwd.1 = (bf16[8,256,1024]{2,1,0:T(8,128)(2,1)}, bf16[1024,256]{1,0:T(8,128)(2,1)}, f32[24,128]{1,0:T(8,128)}, bf16[256,1024]{1,0:T(8,128)(2,1)}, bf16[4,32...) custom-call(s32[4,4]{1,0:T(4,128)} %len_ref.3, ...), custom_call_target="tpu_custom_call" | custom-call | flops 8000000000 | bytes 16777216 | tf_op jit(solution)/shard_map/attn_bwd/pallas_call | solution.py:1062
  184.4 31.5 %final.1 = (f32[256,1024]{1,0:T(8,128)}, bf16[8,32,256]{2,1,0:T(8,128)(2,1)}, bf16[8,32,512]{2,1,0:T(8,128)(2,1)}, f32[2,16,1024]{2,1,0:T(8,128)}, f32[8,128]{1,0:T(8,128)}, /*index=5*/f32[4,16,1024]{2,1,0:T(8,128)}) custom-call(bf16[8,256,1024]{2,1,0:T(8,128)(2,1)} %get-tuple-element.85.dh, bf16[256,1024]{1,0:T(8,128)(2,1)} %x_.5, ...), custom_call_target="tpu_custom_call" | custom-call | tf_op jit(solution)/shard_map/final/pallas_call | solution.py:1193
  215.9 4.0 %unpack.1 = (bf16[256,1024]{1,0:T(8,128)(2,1)}, f32[256,1024]{1,0:T(8,128)}, f32[32,1024]{1,0:T(8,128)}, f32[32,512]{1,0:T(8,128)}, f32[32,512]{1,0:T(8,128)}, /...) custom-call(bf16[256,1024]{1,0:T(8,128)(2,1)} %get-tuple-element.84.r, ...), custom_call_target="tpu_custom_call" | custom-call | tf_op jit(solution)/shard_map/unpack/pallas_call | solution.py:1256

commit v8 on v7

--- a/solution.py
+++ b/solution.py
@@ -470,6 +470,8 @@
     local[0].wait()
     uring.start()
     xg.relay1()
+    fetch[9].wait()
+    dg.start_first()
     row = lax.broadcasted_iota(jnp.int32, (1, ROWS), 1)
     position = (row - seq_start(row, len_ref, g)).astype(F32)
     index = lax.broadcasted_iota(jnp.int32, (HEAD // 2, 1), 0).astype(F32)
@@ -480,8 +482,6 @@
     k_s[: WINDOW * BLOCK] = jnp.zeros((WINDOW * BLOCK, HEAD), BF16)
     v_s[: WINDOW * BLOCK] = jnp.zeros((WINDOW * BLOCK, 128), BF16)
     xg.relay2()
-    fetch[9].wait()
-    dg.start_first()
     for c in (wring, gring):
         c.relay()
     xg.relay3()
@@ -501,6 +501,7 @@
         @pl.when(i == 0)
         def _():
             oring.relay()
+            dg.relay1()
 
         @pl.when(i == 1)
         def _():
@@ -509,24 +510,20 @@
 
         @pl.when(i == 2)
         def _():
-            dg.relay1()
             og.start_second()
 
         @pl.when(i == 3)
         def _():
             uring.relay()
-
-        @pl.when(i == 4)
-        def _():
             dg.relay2()
 
         @pl.when(i == 5)
         def _():
             og.relay1()
+            dg.relay3()
 
         @pl.when(i == 6)
         def _():
-            dg.relay3()
             dring.relay()
 
         @pl.when(i == 7)
@@ -696,7 +693,7 @@
     return (sg * up).astype(BF16), jnp.concatenate([dg, (da * sg).astype(BF16)], axis=1)
 
 
-def ffn_block_kernel(n, order, mix_, x_, wo_, g_ref, w21_, w22_, wd1_, wd2_, dy_, res, gmid, dgf, dwo, dmh, po, t21, dw22, dwd1, dwd2, x, wo, w21, dy, fs, mbuf, h2, h2t, w2v, w22, wdv, wds, dys, acts1, acts2, dgu1, dgu2, dw21, part, mown, stage, hs, hr, os_, qs, qr, zs, zr, *red_refs):
+def ffn_block_kernel(n, order, mix_, x_, wo_, g_ref, w21_, w22_, wd1_, wd2_, dy_, res_o, gmid_o, dgf, dwo_o, dmh, po, t21, dw22_o, dwd1_o, dwd2_o, res, gmid, dwo, dw22, dwd1, dwd2, sent, x, wo, w21, dy, fs, mbuf, h2, h2t, w2v, w22, wdv, wds, dys, acts1, acts2, dgu1, dgu2, dw21, part, mown, stage, hs, hr, os_, qs, qr, zs, zr, *red_refs):
     me, p, g, groups, zq, zg = places(n)
     f1 = wd1_.shape[0]
     f2 = wds.shape[0] - f1
@@ -716,6 +713,12 @@
     barrier([me ^ m for m in range(1, GROUP)] + zq)
     gf = g_ref.at[:, D : 2 * D]
     r = w2v.shape[2]
+    away = [
+        pltpu.make_async_copy(a, b, sent.at[k])
+        for k, (a, b) in enumerate(
+            ((res, res_o), (gmid, gmid_o), (dwo, dwo_o), (dw22, dw22_o), (dwd1, dwd1_o), (dwd2, dwd2_o))
+        )
+    ]
 
     def holder(q):
         s = 0
@@ -736,6 +739,7 @@
     mown[...] = m
     z = x[...].astype(F32) + nn(m, wo[...])
     res[...] = z
+    away[0].start()
     h2[p] = (z * lax.rsqrt(jnp.mean(z * z, axis=-1, keepdims=True) + EPSILON) * gf[...]).astype(BF16)
     hb = halves(BLOCK)
     hg = PlaneGather(me, p, lambda h: h2.at[p, hb(h)], lambda b, h: h2.at[b, hb(h)], hs, hr)
@@ -828,12 +832,15 @@
         part_rows = rows // groups
         for k in range(groups):
             out[k] = dw[k * part_rows : (k + 1) * part_rows].reshape(out.shape[1:])
+    start_all(away[4:])
     red.phase2()
     ring21.relay()
     dw22[...] = nn(h2t[...], dgu2[...].reshape(ROWS, 2 * f2)).astype(BF16)
+    away[3].start()
     dx, dgain = norm_back(red.phase3(), res[...], gf[...])
     gm = dys[p].astype(F32) + dx
     gmid[...] = gm
+    away[1].start()
     dgf[...] = dgain
     gl = gm.astype(BF16)
     dm = nt(gl, wo[...]).astype(BF16)
@@ -844,6 +851,7 @@
     )
     dmh[p] = mbuf[p]
     dwo[...] = tn(mown[...], gl).astype(BF16)
+    away[2].start()
 
     def out(b, carry):
         slot = lax.rem(b, 2)
@@ -862,6 +870,7 @@
     wait_all(qc)
     hg.sent()
     t21[...] = ring21.finish().astype(BF16)
+    wait_all(away)
 
 
 def ffn_block(n, order, mix, x, wo, gvec, w21, w22, wd1, wd, dy):
@@ -887,8 +896,15 @@
             SDS((groups,) + wd2, BF16),
         ),
         in_specs=[SM, HB, HB, HB, VM, HB, HB, HB, HB, HB],
-        out_specs=(VM, VM, VM, VM, VM, HB, VM, VM, VM, VM),
+        out_specs=(HB, HB, VM, HB, VM, HB, VM, HB, HB, HB),
         scratch_shapes=[
+            pltpu.VMEM((BLOCK, D), F32),
+            pltpu.VMEM((BLOCK, D), F32),
+            vm(D, D),
+            vm(D, 2 * f2),
+            vm(groups, *wd1_blk),
+            vm(groups, *wd2),
+            DMA((6,)),
             vm(BLOCK, D),
             vm(D, D),
             vm(D, 2 * f1),
@@ -925,7 +941,7 @@
     )(order, mix, x, wo, gvec, w21, w22, wd1, wd, dy.reshape(ROWS // SLOT, SLOT, D))
 
 
-def attn_bwd_kernel(n, len_ref, dm_ref, q_ref, kvall_ref, lse_ref, mixf_ref, h_ref, raw_ref, w_ref, g_ref, ct_ref, st_ref, po_, res_, dwo_, dw2_, dwd_, t21_, dgf, dh_ref, dw_ref, gpart, result, two, t2, od, o21, k_s, v_s, dkv, dqt, dws, dg_ref, es, er, po, res, dwo, dw2, dwd, t21, fs, *rest):
+def attn_bwd_kernel(n, len_ref, dm_ref, q_ref, kvall_ref, lse_ref, mixf_ref, h_ref, raw_ref, w_ref, g_ref, ct_ref, st_ref, po_, res_, dwo_, dw2_, dwd_, t21_, dgf, dh_ref, dw_ref, gpart, result, two, t2, od, o21, k_s, v_s, dk_s, dv_s, dqt, dws, dg_ref, es, er, po, res, dwo, dw2, dwd, t21, fs, *rest):
     step_id = pl.program_id(0)
     nb = ROWS // BLOCK
     i = nb - 1 - step_id
@@ -966,7 +982,8 @@
 
     @pl.when(step_id == 0)
     def _():
-        dkv[...] = jnp.zeros_like(dkv)
+        dk_s[...] = jnp.zeros_like(dk_s)
+        dv_s[...] = jnp.zeros_like(dv_s)
         dws[...] = jnp.zeros_like(dws)
         dg_ref[...] = jnp.zeros_like(dg_ref)
         for b in range(ROWS // BLOCK):
@@ -993,15 +1010,16 @@
         ok = (kc >= qstart) & (kc <= qrow)
         pr = jnp.where(ok, jnp.exp2(nt(kb, q2) * (SCALE * LOG2E) - lse), 0.0)
         dsc = (pr * (nt(vb, do2) - delta)).astype(BF16)
-        dkv[at, :HEAD] += nn(dsc, q2)
-        dkv[at, HEAD:] += nn(pr.astype(BF16), do2)
+        dk_s[at, :] += nn(dsc, q2)
+        dv_s[at, :] += nn(pr.astype(BF16), do2)
         dqt[...] = tn(dsc, kb)
 
     windows(i, window)
     ct, st = ct_ref[...], st_ref[...]
     raw = raw_ref[0]
     dq = jnp.concatenate([dqt[:BLOCK], dqt[BLOCK:]], axis=1) * SCALE
-    dkvb = dkv[pl.ds(pl.multiple_of(i * BLOCK, BLOCK), BLOCK), :]
+    here = pl.ds(pl.multiple_of(i * BLOCK, BLOCK), BLOCK)
+    dkvb = jnp.concatenate([dk_s[here, :], dv_s[here, :]], axis=1)
     lane = lax.broadcasted_iota(jnp.int32, (BLOCK, 128), 1)
 
     def pull(d, v, gain):
@@ -1106,7 +1124,8 @@
         scratch_shapes=[
             pltpu.VMEM((ROWS, HEAD), BF16),
             pltpu.VMEM((ROWS, HEAD), BF16),
-            pltpu.VMEM((ROWS, 128), F32),
+            pltpu.VMEM((ROWS, HEAD), F32),
+            pltpu.VMEM((ROWS, HEAD), F32),
             pltpu.VMEM((2 * BLOCK, HEAD), F32),
             pltpu.VMEM((D, QKV), F32),
             pltpu.VMEM((8, 128), F32),

time: 220 us -> 217 us (0.986)
  Pallas kernels: 219 us -> 216 us
where the time goes in v8:
time: 217 us
  Pallas kernels  216 us (100%)
    pallas_call x1, Pallas kernels, front(): pl.pallas_call(functools.partial(front_kernel, n), out_shape=(SDS((GROUP,...  71.8 us
    pallas_call x1, Pallas kernels, ffn_block(): pl.pallas_call(functools.partial(ffn_block_kernel, n), out_shape=(SDS((BL...  65.5 us
    pallas_call x1, Pallas kernels, attn_bwd(): pl.pallas_call(functools.partial(attn_bwd_kernel, n), grid=(nb,), in_spec...  43.2 us
    pallas_call x1, Pallas kernels, final(): pl.pallas_call(functools.partial(final_kernel, n), out_shape=(SDS((BLOCK,...  31.4 us

profile of v8, /device:TPU:0, one launch (start us, length us, event | category | flops | bytes accessed | tf_op | source)
XLA Modules:
  0.0 216.6 jit_solution(9141066644015187302)
XLA Ops:
  0.6 71.8 %front.1 = (bf16[8,256,1024]{2,1,0:T(8,128)(2,1)}, f32[8,256,256]{2,1,0:T(8,128)}, bf16[8,256,128]{2,1,0:T(8,128)(2,1)}, bf16[8,256,128]{2,1,0:T(8,128)(2,1)}, f...) custom-call(s32[4,4]{1,0:T(4,128)} %len_ref.3, ...), custom_call_target="tpu_custom_call" | custom-call | tf_op jit(solution)/shard_map/front/pallas_call | solution.py:613
  72.5 65.5 %ffn_block.1 = (f32[256,1024]{1,0:T(8,128)}, f32[256,1024]{1,0:T(8,128)}, f32[1,1024]{1,0:T(1,128)}, bf16[1024,1024]{1,0:T(8,128)(2,1)}, bf16[8,256,128]{2,1,0:T...) custom-call(s32[4,16]{1,0:T(4,128)} %order.1, ...), custom_call_target="tpu_custom_call" | custom-call | tf_op jit(solution)/shard_map/ffn_block/pallas_call | solution.py:884
  138.0 43.2 %attn_bwd.1 = (bf16[8,256,1024]{2,1,0:T(8,128)(2,1)}, bf16[1024,256]{1,0:T(8,128)(2,1)}, f32[24,128]{1,0:T(8,128)}, bf16[256,1024]{1,0:T(8,128)(2,1)}, bf16[4,32...) custom-call(s32[4,4]{1,0:T(4,128)} %len_ref.3, ...), custom_call_target="tpu_custom_call" | custom-call | flops 8000000000 | bytes 16777216 | tf_op jit(solution)/shard_map/attn_bwd/pallas_call | solution.py:1080
  181.2 31.4 %final.1 = (f32[256,1024]{1,0:T(8,128)}, bf16[8,32,256]{2,1,0:T(8,128)(2,1)}, bf16[8,32,512]{2,1,0:T(8,128)(2,1)}, f32[2,16,1024]{2,1,0:T(8,128)}, f32[8,128]{1,0:T(8,128)}, /*index=5*/f32[4,16,1024]{2,1,0:T(8,128)}) custom-call(bf16[8,256,1024]{2,1,0:T(8,128)(2,1)} %get-tuple-element.85.dh, bf16[256,1024]{1,0:T(8,128)(2,1)} %x_.5, ...), custom_call_target="tpu_custom_call" | custom-call | tf_op jit(solution)/shard_map/final/pallas_call | solution.py:1212
  212.6 4.0 %unpack.1 = (bf16[256,1024]{1,0:T(8,128)(2,1)}, f32[256,1024]{1,0:T(8,128)}, f32[32,1024]{1,0:T(8,128)}, f32[32,512]{1,0:T(8,128)}, f32[32,512]{1,0:T(8,128)}, /...) custom-call(bf16[256,1024]{1,0:T(8,128)(2,1)} %get-tuple-element.84.r, ...), custom_call_target="tpu_custom_call" | custom-call | tf_op jit(solution)/shard_map/unpack/pallas_call | solution.py:1275

commit v9 on v8

--- a/solution.py
+++ b/solution.py
@@ -763,7 +763,7 @@
         def _():
             hg.arrive(hg.fx)
 
-        @pl.when(t == 4)
+        @pl.when(t == 3)
         def _():
             for c in wrings:
                 c.relay()

time: 217 us -> 217 us (level)
  no operation moved by 1% of the time
where the time goes in v9:
time: 217 us; the launch traced here: 216 us
  Pallas kernels  216 us (100%)
    pallas_call x1, Pallas kernels, front(): pl.pallas_call(functools.partial(front_kernel, n), out_shape=(SDS((GROUP,...  71.8 us
    pallas_call x1, Pallas kernels, ffn_block(): pl.pallas_call(functools.partial(ffn_block_kernel, n), out_shape=(SDS((BL...  64.6 us
    pallas_call x1, Pallas kernels, attn_bwd(): pl.pallas_call(functools.partial(attn_bwd_kernel, n), grid=(nb,), in_spec...  43.7 us
    pallas_call x1, Pallas kernels, final(): pl.pallas_call(functools.partial(final_kernel, n), out_shape=(SDS((BLOCK,...  31.5 us

profile of v9, /device:TPU:0, one launch (start us, length us, event | category | flops | bytes accessed | tf_op | source)
XLA Modules:
  0.0 216.3 jit_solution(5433186247505185875)
XLA Ops:
  0.6 71.8 %front.1 = (bf16[8,256,1024]{2,1,0:T(8,128)(2,1)}, f32[8,256,256]{2,1,0:T(8,128)}, bf16[8,256,128]{2,1,0:T(8,128)(2,1)}, bf16[8,256,128]{2,1,0:T(8,128)(2,1)}, f...) custom-call(s32[4,4]{1,0:T(4,128)} %len_ref.3, ...), custom_call_target="tpu_custom_call" | custom-call | tf_op jit(solution)/shard_map/front/pallas_call | solution.py:613
  72.5 64.6 %ffn_block.1 = (f32[256,1024]{1,0:T(8,128)}, f32[256,1024]{1,0:T(8,128)}, f32[1,1024]{1,0:T(1,128)}, bf16[1024,1024]{1,0:T(8,128)(2,1)}, bf16[8,256,128]{2,1,0:T...) custom-call(s32[4,16]{1,0:T(4,128)} %order.1, ...), custom_call_target="tpu_custom_call" | custom-call | tf_op jit(solution)/shard_map/ffn_block/pallas_call | solution.py:884
  137.1 43.7 %attn_bwd.1 = (bf16[8,256,1024]{2,1,0:T(8,128)(2,1)}, bf16[1024,256]{1,0:T(8,128)(2,1)}, f32[24,128]{1,0:T(8,128)}, bf16[256,1024]{1,0:T(8,128)(2,1)}, bf16[4,32...) custom-call(s32[4,4]{1,0:T(4,128)} %len_ref.3, ...), custom_call_target="tpu_custom_call" | custom-call | flops 8000000000 | bytes 16777216 | tf_op jit(solution)/shard_map/attn_bwd/pallas_call | solution.py:1080
  180.9 31.5 %final.1 = (f32[256,1024]{1,0:T(8,128)}, bf16[8,32,256]{2,1,0:T(8,128)(2,1)}, bf16[8,32,512]{2,1,0:T(8,128)(2,1)}, f32[2,16,1024]{2,1,0:T(8,128)}, f32[8,128]{1,0:T(8,128)}, /*index=5*/f32[4,16,1024]{2,1,0:T(8,128)}) custom-call(bf16[8,256,1024]{2,1,0:T(8,128)(2,1)} %get-tuple-element.85.dh, bf16[256,1024]{1,0:T(8,128)(2,1)} %x_.5, ...), custom_call_target="tpu_custom_call" | custom-call | tf_op jit(solution)/shard_map/final/pallas_call | solution.py:1212
  212.3 4.0 %unpack.1 = (bf16[256,1024]{1,0:T(8,128)(2,1)}, f32[256,1024]{1,0:T(8,128)}, f32[32,1024]{1,0:T(8,128)}, f32[32,512]{1,0:T(8,128)}, f32[32,512]{1,0:T(8,128)}, /...) custom-call(bf16[256,1024]{1,0:T(8,128)(2,1)} %get-tuple-element.84.r, ...), custom_call_target="tpu_custom_call" | custom-call | tf_op jit(solution)/shard_map/unpack/pallas_call | solution.py:1275

commit v10 on v9

--- a/solution.py
+++ b/solution.py
@@ -745,13 +745,12 @@
     hg = PlaneGather(me, p, lambda h: h2.at[p, hb(h)], lambda b, h: h2.at[b, hb(h)], hs, hr)
     red = PlaneReduce(me, lambda b: part.at[b], *red_refs[:7])
     ring21 = RingReduce(n, p, g, dw21, *red_refs[7:])
-    hg.start_first()
+    hg.start()
     wait_all(fetch[5:])
 
     def first(t, carry):
         @pl.when(t == 1)
         def _():
-            hg.start_second()
             hg.arrive(hg.o)
 
         @pl.when(t == 2)
@@ -1170,9 +1169,9 @@
             pc.append(c)
         out[p] = src[p]
 
+    exchange(1, t2, o2)
     wait_all(fetch)
     red.phase1()
-    exchange(1, t2, o2)
     tot = gpart[...]
     for m in range(1, GROUP):
         gc[m - 1].wait_recv()

time: 217 us -> 217 us (level)
  no operation moved by 1% of the time
where the time goes in v10:
time: 217 us; the launch traced here: 216 us
  Pallas kernels  216 us (100%)
    pallas_call x1, Pallas kernels, front(): pl.pallas_call(functools.partial(front_kernel, n), out_shape=(SDS((GROUP,...  71.8 us
    pallas_call x1, Pallas kernels, ffn_block(): pl.pallas_call(functools.partial(ffn_block_kernel, n), out_shape=(SDS((BL...  64.6 us
    pallas_call x1, Pallas kernels, attn_bwd(): pl.pallas_call(functools.partial(attn_bwd_kernel, n), grid=(nb,), in_spec...  43.7 us
    pallas_call x1, Pallas kernels, final(): pl.pallas_call(functools.partial(final_kernel, n), out_shape=(SDS((BLOCK,...  31.5 us

profile of v10, /device:TPU:0, one launch (start us, length us, event | category | flops | bytes accessed | tf_op | source)
XLA Modules:
  0.0 216.3 jit_solution(9500508196477765162)
XLA Ops:
  0.6 71.8 %front.1 = (bf16[8,256,1024]{2,1,0:T(8,128)(2,1)}, f32[8,256,256]{2,1,0:T(8,128)}, bf16[8,256,128]{2,1,0:T(8,128)(2,1)}, bf16[8,256,128]{2,1,0:T(8,128)(2,1)}, f...) custom-call(s32[4,4]{1,0:T(4,128)} %len_ref.3, ...), custom_call_target="tpu_custom_call" | custom-call | tf_op jit(solution)/shard_map/front/pallas_call | solution.py:613
  72.5 64.6 %ffn_block.1 = (f32[256,1024]{1,0:T(8,128)}, f32[256,1024]{1,0:T(8,128)}, f32[1,1024]{1,0:T(1,128)}, bf16[1024,1024]{1,0:T(8,128)(2,1)}, bf16[8,256,128]{2,1,0:T...) custom-call(s32[4,16]{1,0:T(4,128)} %order.1, ...), custom_call_target="tpu_custom_call" | custom-call | tf_op jit(solution)/shard_map/ffn_block/pallas_call | solution.py:883
  137.1 43.7 %attn_bwd.1 = (bf16[8,256,1024]{2,1,0:T(8,128)(2,1)}, bf16[1024,256]{1,0:T(8,128)(2,1)}, f32[24,128]{1,0:T(8,128)}, bf16[256,1024]{1,0:T(8,128)(2,1)}, bf16[4,32...) custom-call(s32[4,4]{1,0:T(4,128)} %len_ref.3, ...), custom_call_target="tpu_custom_call" | custom-call | flops 8000000000 | bytes 16777216 | tf_op jit(solution)/shard_map/attn_bwd/pallas_call | solution.py:1079
  180.8 31.5 %final.1 = (f32[256,1024]{1,0:T(8,128)}, bf16[8,32,256]{2,1,0:T(8,128)(2,1)}, bf16[8,32,512]{2,1,0:T(8,128)(2,1)}, f32[2,16,1024]{2,1,0:T(8,128)}, f32[8,128]{1,0:T(8,128)}, /*index=5*/f32[4,16,1024]{2,1,0:T(8,128)}) custom-call(bf16[8,256,1024]{2,1,0:T(8,128)(2,1)} %get-tuple-element.85.dh, bf16[256,1024]{1,0:T(8,128)(2,1)} %x_.5, ...), custom_call_target="tpu_custom_call" | custom-call | tf_op jit(solution)/shard_map/final/pallas_call | solution.py:1211
  212.3 4.0 %unpack.1 = (bf16[256,1024]{1,0:T(8,128)(2,1)}, f32[256,1024]{1,0:T(8,128)}, f32[32,1024]{1,0:T(8,128)}, f32[32,512]{1,0:T(8,128)}, f32[32,512]{1,0:T(8,128)}, /...) custom-call(bf16[256,1024]{1,0:T(8,128)(2,1)} %get-tuple-element.84.r, ...), custom_call_target="tpu_custom_call" | custom-call | tf_op jit(solution)/shard_map/unpack/pallas_call | solution.py:1274
